TPU v7x, 256 devices: a whole 4x4x8 slice. The times are simulated.
256 devices in a mesh: ctx: 64 (over x_hi, y, z), tp: 4 (over x_lo, core).
Axes of the slice: x: 4 (x_hi: 2, x_lo: 2; x = x_hi * 2 + x_lo), y: 4, z: 8, core: 2. Of those that a mesh axis runs over, the one named last changes fastest.
Arguments:
- hidden: bfloat16 [32768, 5120], P('ctx', 'tp'), may hold values from -6 to 6
- queries: bfloat16 [32768, 5120], P('ctx', 'tp'), may hold values from -600 to 600
- lengths: int32 [256], replicated, may hold values from 1 to 2048, 32768 in all
- norm_gain: float32 [5120], P('tp'), may hold values from 0.5 to 1.5
- kv_weight: bfloat16 [5120, 2, 1024], P(None, None, 'tp'), may hold values from -0.078125 to 0.078125
- kv_bias: float32 [2, 1024], P(None, 'tp'), may hold values from -3 to 3
Outputs:
- attended: bfloat16 [32768, 5120], P('ctx', 'tp')
Inputs may be any that keep to these rules, and one draw needn't show every extreme that they name: The 256 files fill the 32768 positions in order; their lengths sum to 32768 and the longest is exactly 2048.
All inputs are finite; a program needn't handle non-finite values.
Results may differ from a plain program's by a relative error of at most 0.006.
Values may be sent and summed in bfloat16 or wider, within the bound.
A program may use at most 128 MiB of HBM per device.

v0:
```python
import functools

import jax
import jax.numpy as jnp
from jax import lax
from jax.experimental import pallas as pl
from jax.experimental.pallas import tpu as pltpu
from jax.sharding import PartitionSpec as P

D = 5120
HD = 128
CYCLE = 4


def shifted(value, axis, steps):
    count = lax.axis_size(axis)
    leading, last = (max(0, -steps), min(count, count - steps))
    return lax.ppermute(value, axis, [(source, source + steps) for source in range(leading, last)])


def flipped(value, axis, bit):
    count = lax.axis_size(axis)
    return lax.ppermute(value, axis, [(source, source ^ bit) for source in range(count)])


def attention_kernel(group, tok, scale, nblocks_ref, q_ref, k_ref, v_ref, qdoc_ref, kdoc_ref,
                     o_ref, m_ref, l_ref, acc_ref):
    b = pl.program_id(1)
    last = pl.num_programs(1) - 1

    @pl.when(b < nblocks_ref[0])
    def _():
        same = qdoc_ref[...] == kdoc_ref[...]
        rows = lax.broadcasted_iota(jnp.int32, (tok, tok), 0)
        cols = lax.broadcasted_iota(jnp.int32, (tok, tok), 1)
        visible = same & ((b > 0) | (cols <= rows))
        keys = k_ref[...]
        values = v_ref[...]
        for j in range(group):
            q = q_ref[:, j * HD:(j + 1) * HD]
            s = lax.dot_general(q, keys, (((1,), (1,)), ((), ())),
                                preferred_element_type=jnp.float32) * scale
            s = jnp.where(visible, s, -1e30)
            top = jnp.max(s, axis=1, keepdims=True)

            @pl.when(b == 0)
            def _():
                p = jnp.exp(s - top)
                m_ref[j] = jnp.broadcast_to(top, (tok, HD))
                l_ref[j] = jnp.broadcast_to(jnp.sum(p, axis=1, keepdims=True), (tok, HD))
                acc_ref[j] = jnp.dot(p.astype(jnp.bfloat16), values,
                                     preferred_element_type=jnp.float32)

            @pl.when(b > 0)
            def _():
                prev = m_ref[j]
                best = jnp.maximum(prev, top)
                shrink = jnp.exp(prev - best)
                p = jnp.exp(s - best[:, :1])
                m_ref[j] = best
                l_ref[j] = l_ref[j] * shrink + jnp.sum(p, axis=1, keepdims=True)
                acc_ref[j] = acc_ref[j] * shrink + jnp.dot(
                    p.astype(jnp.bfloat16), values, preferred_element_type=jnp.float32)

    @pl.when(b == last)
    def _():
        for j in range(group):
            o_ref[:, j * HD:(j + 1) * HD] = (acc_ref[j] / l_ref[j]).astype(o_ref.dtype)


def attend_all(queries, kv_stack, qdoc, kdoc, nblocks, kv_heads):
    tok, width = queries.shape
    group = width // HD // kv_heads
    nb = kv_stack.shape[0] // tok

    def kv_index(kind):
        return lambda g, b, n: (jnp.minimum(b, n[0] - 1), kind * kv_heads + g)

    grid_spec = pltpu.PrefetchScalarGridSpec(
        num_scalar_prefetch=1,
        grid=(kv_heads, nb),
        in_specs=[
            pl.BlockSpec((tok, group * HD), lambda g, b, n: (0, g)),
            pl.BlockSpec((tok, HD), kv_index(0)),
            pl.BlockSpec((tok, HD), kv_index(1)),
            pl.BlockSpec((tok, 1), lambda g, b, n: (0, 0)),
            pl.BlockSpec((1, tok), lambda g, b, n: (0, jnp.minimum(b, n[0] - 1))),
        ],
        out_specs=pl.BlockSpec((tok, group * HD), lambda g, b, n: (0, g)),
        scratch_shapes=[
            pltpu.VMEM((group, tok, HD), jnp.float32),
            pltpu.VMEM((group, tok, HD), jnp.float32),
            pltpu.VMEM((group, tok, HD), jnp.float32),
        ],
    )
    return pl.pallas_call(
        functools.partial(attention_kernel, group, tok, HD ** (-0.5)),
        grid_spec=grid_spec,
        out_shape=jax.ShapeDtypeStruct((tok, width), queries.dtype),
        compiler_params=pltpu.CompilerParams(dimension_semantics=("arbitrary", "arbitrary")),
    )(nblocks, queries, kv_stack, kv_stack, qdoc, kdoc)


def body(hidden, queries, lengths, norm_gain, kv_weight, kv_bias):
    tok, width = hidden.shape
    tpi = lax.axis_index("tp")
    across = flipped(hidden, "tp", 2)
    pair = flipped(jnp.stack([hidden, across]), "tp", 1)
    gain_across = flipped(norm_gain, "tp", 2)
    gain_pair = flipped(jnp.stack([norm_gain, gain_across]), "tp", 1)
    blocks = [
        (hidden, norm_gain, tpi),
        (across, gain_across, tpi ^ 2),
        (pair[0], gain_pair[0], tpi ^ 1),
        (pair[1], gain_pair[1], tpi ^ 3),
    ]
    squares = None
    for part, _, _ in blocks:
        xf = part.astype(jnp.float32)
        term = jnp.sum(xf * xf, axis=1)
        squares = term if squares is None else squares + term
    scale_rows = lax.rsqrt(squares / D + 1e-06)
    flat_weight = kv_weight.reshape(kv_weight.shape[0], -1)
    summed = None
    for part, gain, owner in blocks:
        normed = (part.astype(jnp.float32) * scale_rows[:, None] * gain[None, :]).astype(jnp.bfloat16)
        rows = lax.dynamic_slice_in_dim(flat_weight, owner * width, width, 0)
        term = jnp.dot(normed, rows, preferred_element_type=jnp.float32)
        summed = term if summed is None else summed + term
    kv_local = (summed + kv_bias.reshape(-1)[None, :]).astype(jnp.bfloat16)
    kv_heads = kv_weight.shape[2] // HD

    device = lax.axis_index("ctx")
    ends = jnp.cumsum(lengths)
    backs = jnp.arange(CYCLE + 1, dtype=jnp.int32)
    starts = (device - backs) * tok
    positions = starts[:, None] + jnp.arange(tok, dtype=jnp.int32)[None, :]
    found = jnp.sum((positions[:, :, None] >= ends[None, None, :]).astype(jnp.int32), axis=2)
    kdoc = jnp.where((device - backs >= 0)[:, None], found, -1)
    qdoc = found[0]
    reach = jnp.sum((kdoc[:, tok - 1] >= qdoc[0]).astype(jnp.int32))
    nblocks = jnp.reshape(reach, (1,))

    moving = kv_local
    stack = [kv_local]
    for back in range(1, CYCLE + 1):
        moving = shifted(moving, "ctx", 1)
        stack.append(moving)
    kv_stack = jnp.concatenate(stack, axis=0)
    return attend_all(queries, kv_stack, qdoc[:, None], kdoc.reshape(1, -1), nblocks, kv_heads)


def solution(mesh):
    in_specs = (P("ctx", "tp"), P("ctx", "tp"), P(), P("tp"), P(None, None, "tp"), P(None, "tp"))
    out_specs = P("ctx", "tp")
    return jax.shard_map(body, mesh=mesh, in_specs=in_specs, out_specs=out_specs, check_vma=False)
```

profile of v0, /device:TPU:58, one launch (start us, length us, event | category | flops | bytes accessed | tf_op | source)
XLA Modules:
  0.0 170.7 jit_solution(4520587496050805521)
XLA Ops:
  0.0 0.5 collective-permute-start
  0.5 30.2 %collective-permute-done = bf16[512,1280]{1,0:T(8,128)(2,1)S(1)} collective-permute-done((bf16[512,1280]{1,0:T(8,128)(2,1)}, bf16[512,1280]{1,0:T(8,128)(2,1)S(1)}, u32[]{:S(2)}, u32[]{:S(2)}) %collective-permute-start) | collective-permute-done | bytes 1310752 | tf_op jit(solution)/shard_map/ppermute | solution.py:23
  30.7 3.2 %pad_maximum_fusion = bf16[2,512,1280]{2,1,0:T(8,128)(2,1)} fusion(bf16[1,512,1280]{2,1,0:T(8,128)(2,1)S(1)} %bitcast.36, bf16[1,512,1280]{2,1,0:T(8,128)(2,1)} %bitcast.35), kind=kLoop, calls=%fused_computation.20 | loop fusion | flops 1310720 | bytes 5242880 | tf_op jit(solution)/shard_map/stack | solution.py:108
  34.0 0.0 collective-permute-start.1
  34.0 0.0 copy-done.3
  34.0 0.5 collective-permute-start.2
  34.5 3.1 %collective-permute-done.2 = f32[1280]{0:T(1024)S(1)} collective-permute-done((f32[1280]{0:T(1024)S(1)}, f32[1280]{0:T(1024)S(1)}, u32[]{:S(2)}, u32[]{:S(2)}) %collective-permute-start.2) | collective-permute-done | bytes 5152 | tf_op jit(solution)/shard_map/ppermute | solution.py:23
  37.6 0.1 collective-permute-start.3
  37.7 0.3 fusion
  38.1 0.0 copy-start.4
  38.1 5.7 %copy.9 = bf16[640,8,2,256]{3,1,2,0:T(8,128)(2,1)} copy(bf16[640,8,2,256]{3,2,1,0:T(2,128)(2,1)} %bitcast.37) | data formatting | bytes 10485760
  43.8 0.0 copy-done.4
  43.8 0.0 collective-permute-done.3
  43.8 0.3 fusion.3
  44.2 0.0 collective-permute-done.1
  44.2 2.3 %fusion.6 = (f32[512]{0:T(512)S(1)}, f32[512]{0:T(512)S(1)}) fusion(bf16[2,512,1280]{2,1,0:T(8,128)(2,1)} %collective-permute-done.1), kind=kLoop, calls=%fused_computation.14 | loop fusion | flops 3931136 | bytes 2625536 | tf_op jit(solution)/shard_map/reduce_sum | solution.py:120
  46.5 0.0 copy-start.2
  46.5 2.4 %fusion.17 = f32[512,512]{1,0:T(8,128)S(1)} fusion(bf16[512,1280]{1,0:T(8,128)(2,1)S(1)} %copy-done.1, bf16[5120,512]{1,0:T(8,128)(2,1)} %bitcast.38, s32[]{:T(128)S(6)} %select_n.27, f32[1280]{0:T(1024)S(1)} %copy-done.3, f32[512]{0:T(512)S(1)} %add_rsqrt_fusion), kind=kOutput, calls=%fused_computation.26 | convolution fusion | flops 673710080 | bytes 3677188 | tf_op jit(solution)/shard_map/dot_general | solution.py:128
  48.9 0.5 copy-done.2
  49.4 0.9 convolution_add_fusion.1
  50.3 2.2 %fusion.13 = f32[512,512]{1,0:T(8,128)S(1)} fusion(bf16[5120,512]{1,0:T(8,128)(2,1)S(1)} %bitcast.40, s32[]{:T(128)S(6)} %select_n.30, f32[1280]{0:T(1024)S(1)} %get-tuple-element.8, f32[512]{0:T(512)S(1)} %add_rsqrt_fusion, bf16[2,512,1280]{2,1,0:T(8,128)(2,1)} %collective-permute-done.1), kind=kOutput, calls=%fused_computation.25 | convolution fusion | flops 673710080 | bytes 3680260 | tf_op jit(solution)/shard_map/dot_general | solution.py:128
  52.5 0.0 copy-start.5
  52.5 3.0 %constant_dynamic-update-slice_fusion.4 = (bf16[2560,512]{1,0:T(8,128)(2,1)S(1)}, bf16[512,512]{1,0:T(8,128)(2,1)}) fusion(f32[512]{0:T(512)S(1)} %bitcast.44, f32[512,512]{1,0:T(8,128)S(1)} %fusion.13, f32[512,512]{1,0:T(8,128)S(1)} %convolution_add_fusion.1, bf16[5120,512]{1,0:T(8,128)(2,1)S(1)} %bitcast.41, s32[]{:T(128)S(6)} %select_n.29, ...), kind=kOutput, calls=%fused_computation.48 | convolution fusion | flops 674758656 | bytes 5779460 | tf_op jit(solution)/shard_map/dot_general | solution.py:128
  55.5 3.8 %collective-permute-start.4 = (bf16[512,512]{1,0:T(8,128)(2,1)}, bf16[512,512]{1,0:T(8,128)(2,1)S(1)}, u32[]{:S(2)}, u32[]{:S(2)}) collective-permute-start(bf16[512,512]{1,0:T(8,128)(2,1)} %get-tuple-element.10), channel_id=1, source_target_pairs={{0,4},{4,8},{8,12},{12,16},{16,20},{20,24},{24,28},{28,32},{32,36}... | collective-permute-start | bytes 1572872 | tf_op jit(solution)/shard_map/ppermute | solution.py:18
  59.4 0.3 reduce-window.9
  59.7 0.1 slice.30
  59.8 0.1 slice_reduce_fusion.2
  59.9 12.0 %collective-permute-done.4 = bf16[512,512]{1,0:T(8,128)(2,1)S(1)} collective-permute-done((bf16[512,512]{1,0:T(8,128)(2,1)}, bf16[512,512]{1,0:T(8,128)(2,1)S(1)}, u32[]{:S(2)}, u32[]{:S(2)}) %collective-permute-start.4) | collective-permute-done | bytes 524320 | tf_op jit(solution)/shard_map/ppermute | solution.py:18
  71.9 3.8 %collective-permute-start.5 = (bf16[512,512]{1,0:T(8,128)(2,1)S(1)}, bf16[512,512]{1,0:T(8,128)(2,1)}, u32[]{:S(2)}, u32[]{:S(2)}) collective-permute-start(bf16[512,512]{1,0:T(8,128)(2,1)S(1)} %collective-permute-done.4), channel_id=1, source_target_pairs={{0,4},{4,8},{8,12},{12,16},{16,20},{20,24},{24,28},{28,32},{32,36}... | collective-permute-start | bytes 1572872 | tf_op jit(solution)/shard_map/ppermute | solution.py:18
  75.8 0.1 add_bitcast_fusion
  75.8 0.1 iota_add_fusion
  75.9 0.9 convert_reduce_fusion
  76.8 13.6 %collective-permute-done.5 = bf16[512,512]{1,0:T(8,128)(2,1)} collective-permute-done((bf16[512,512]{1,0:T(8,128)(2,1)S(1)}, bf16[512,512]{1,0:T(8,128)(2,1)}, u32[]{:S(2)}, u32[]{:S(2)}) %collective-permute-start.5) | collective-permute-done | bytes 524320 | tf_op jit(solution)/shard_map/ppermute | solution.py:18
  90.4 1.9 %collective-permute-start.6 = (bf16[512,512]{1,0:T(8,128)(2,1)}, bf16[512,512]{1,0:T(8,128)(2,1)}, u32[]{:S(2)}, u32[]{:S(2)}) collective-permute-start(bf16[512,512]{1,0:T(8,128)(2,1)} %collective-permute-done.5), channel_id=1, source_target_pairs={{0,4},{4,8},{8,12},{12,16},{16,20},{20,24},{24,28},{28,32},{32,36}... | collective-permute-start | bytes 1572872 | tf_op jit(solution)/shard_map/ppermute | solution.py:18
  92.3 0.1 broadcast_select_fusion
  92.4 0.1 fusion.47
  92.4 15.1 %collective-permute-done.6 = bf16[512,512]{1,0:T(8,128)(2,1)} collective-permute-done((bf16[512,512]{1,0:T(8,128)(2,1)}, bf16[512,512]{1,0:T(8,128)(2,1)}, u32[]{:S(2)}, u32[]{:S(2)}) %collective-permute-start.6) | collective-permute-done | bytes 524320 | tf_op jit(solution)/shard_map/ppermute | solution.py:18
  107.6 2.1 %collective-permute-start.7 = (bf16[512,512]{1,0:T(8,128)(2,1)}, bf16[512,512]{1,0:T(8,128)(2,1)}, u32[]{:S(2)}, u32[]{:S(2)}) collective-permute-start(bf16[512,512]{1,0:T(8,128)(2,1)} %collective-permute-done.6), channel_id=1, source_target_pairs={{0,4},{4,8},{8,12},{12,16},{16,20},{20,24},{24,28},{28,32},{32,36}... | collective-permute-start | bytes 1572872 | tf_op jit(solution)/shard_map/ppermute | solution.py:18
  109.7 0.5 slice.40
  110.2 0.6 copy.11
  110.8 0.9 copy.8.qdoc_ref
  111.7 1.3 convert_reduce_fusion.1
  113.0 1.1 constant_dynamic-update-slice_fusion.2
  114.1 1.1 constant_dynamic-update-slice_fusion.1
  115.2 8.7 %collective-permute-done.7 = bf16[512,512]{1,0:T(8,128)(2,1)} collective-permute-done((bf16[512,512]{1,0:T(8,128)(2,1)}, bf16[512,512]{1,0:T(8,128)(2,1)}, u32[]{:S(2)}, u32[]{:S(2)}) %collective-permute-start.7) | collective-permute-done | bytes 524320 | tf_op jit(solution)/shard_map/ppermute | solution.py:18
  123.8 1.1 constant_dynamic-update-slice_fusion.k_ref.v_ref
  124.9 1.5 copy-done
  126.4 44.3 %shard_map.64 = bf16[512,1280]{1,0:T(8,128)(2,1)} custom-call(s32[1]{0:T(128)} %bitcast.3.nblocks_ref, bf16[512,1280]{1,0:T(8,128)(2,1)} %q_ref.1, bf16[2560,512]{1,0:T(8,128)(2,1)} %copy-done, bf16[2560,512]{1,0:T(8,128)(2,1)} %copy-done, s32[512,1]{1,0:T(8,128)} %copy.8.qdoc_ref, s32[1,2560]{1,0:T(1,128)} %bitcast.42), custom_call_target="tpu_custom_call" | custom-call | tf_op jit(solution)/shard_map/pallas_call | solution.py:96
  (16 shorter events, 0.2 us)
Async XLA Ops:
  0.0 30.7 %collective-permute-start = (bf16[512,1280]{1,0:T(8,128)(2,1)}, bf16[512,1280]{1,0:T(8,128)(2,1)S(1)}, u32[]{:S(2)}, u32[]{:S(2)}) collective-permute-start(bf16[512,1280]{1,0:T(8,128)(2,1)} %param.6), channel_id=1, source_target_pairs={{0,2},{1,3},{2,0},{3,1},{4,6},{5,7},{6,4},{7,5},{8,10},{9,11},{10,... | collective-permute-start | bytes 3932168 | tf_op jit(solution)/shard_map/ppermute | solution.py:23
  30.7 3.2 %copy-start.3 = (f32[1280]{0:T(1024)S(1)}, f32[1280]{0:T(1024)}, u32[]{:S(2)}) copy-start(f32[1280]{0:T(1024)} %param.9) | copy-start | bytes 15364
  30.7 7.0 %copy-start.1 = (bf16[512,1280]{1,0:T(8,128)(2,1)S(1)}, bf16[512,1280]{1,0:T(8,128)(2,1)}, u32[]{:S(2)}) copy-start(bf16[512,1280]{1,0:T(8,128)(2,1)} %param.6) | copy-start | bytes 3932164
  34.0 10.2 %collective-permute-start.1 = (bf16[2,512,1280]{2,1,0:T(8,128)(2,1)}, bf16[2,512,1280]{2,1,0:T(8,128)(2,1)}, u32[]{:S(2)}, u32[]{:S(2)}) collective-permute-start(bf16[2,512,1280]{2,1,0:T(8,128)(2,1)} %pad_maximum_fusion), channel_id=1, source_target_pairs={{0,1},{1,0},{2,3},{3,2},{4,5},{5,4},{6,7},{7,6},{8,9},{9,8},{10,11... | collective-permute-start | bytes 7864328 | tf_op jit(solution)/shard_map/ppermute | solution.py:23
  34.0 3.7 %collective-permute-start.2 = (f32[1280]{0:T(1024)S(1)}, f32[1280]{0:T(1024)S(1)}, u32[]{:S(2)}, u32[]{:S(2)}) collective-permute-start(f32[1280]{0:T(1024)S(1)} %copy-done.3), channel_id=1, source_target_pairs={{0,2},{1,3},{2,0},{3,1},{4,6},{5,7},{6,4},{7,5},{8,10},{9,11},{10,... | collective-permute-start | bytes 15368 | tf_op jit(solution)/shard_map/ppermute | solution.py:23
  37.6 6.2 %collective-permute-start.3 = (f32[2,1280]{1,0:T(2,128)S(1)}, f32[2,1280]{1,0:T(2,128)S(1)}, u32[]{:S(2)}, u32[]{:S(2)}) collective-permute-start(f32[2,1280]{1,0:T(2,128)S(1)} %pad_maximum_fusion.1), channel_id=1, source_target_pairs={{0,1},{1,0},{2,3},{3,2},{4,5},{5,4},{6,7},{7,6},{8,9},{9,8},{10,11... | collective-permute-start | bytes 30728 | tf_op jit(solution)/shard_map/ppermute | solution.py:23
  38.1 5.7 %copy-start.4 = (f32[2,256]{1,0:T(2,128)S(1)}, f32[2,256]{1,0:T(2,128)}, u32[]{:S(2)}) copy-start(f32[2,256]{1,0:T(2,128)} %param.11) | copy-start | bytes 6148
  46.5 2.9 %copy-start.2 = (bf16[640,8,2,256]{3,1,2,0:T(8,128)(2,1)S(1)}, bf16[640,8,2,256]{3,1,2,0:T(8,128)(2,1)}, u32[]{:S(2)}) copy-start(bf16[640,8,2,256]{3,1,2,0:T(8,128)(2,1)} %copy.9) | copy-start | bytes 15728644
  52.5 6.9 %copy-start.5 = (s32[256]{0:T(256)S(1)}, s32[256]{0:T(256)}, u32[]{:S(2)}) copy-start(s32[256]{0:T(256)} %param.8) | copy-start | bytes 3076
  55.5 16.4 %collective-permute-start.4 = (bf16[512,512]{1,0:T(8,128)(2,1)}, bf16[512,512]{1,0:T(8,128)(2,1)S(1)}, u32[]{:S(2)}, u32[]{:S(2)}) collective-permute-start(bf16[512,512]{1,0:T(8,128)(2,1)} %get-tuple-element.10), channel_id=1, source_target_pairs={{0,4},{4,8},{8,12},{12,16},{16,20},{20,24},{24,28},{28,32},{32,36}... | collective-permute-start | bytes 1572872 | tf_op jit(solution)/shard_map/ppermute | solution.py:18
  71.9 18.4 %collective-permute-start.5 = (bf16[512,512]{1,0:T(8,128)(2,1)S(1)}, bf16[512,512]{1,0:T(8,128)(2,1)}, u32[]{:S(2)}, u32[]{:S(2)}) collective-permute-start(bf16[512,512]{1,0:T(8,128)(2,1)S(1)} %collective-permute-done.4), channel_id=1, source_target_pairs={{0,4},{4,8},{8,12},{12,16},{16,20},{20,24},{24,28},{28,32},{32,36}... | collective-permute-start | bytes 1572872 | tf_op jit(solution)/shard_map/ppermute | solution.py:18
  90.4 17.2 %collective-permute-start.6 = (bf16[512,512]{1,0:T(8,128)(2,1)}, bf16[512,512]{1,0:T(8,128)(2,1)}, u32[]{:S(2)}, u32[]{:S(2)}) collective-permute-start(bf16[512,512]{1,0:T(8,128)(2,1)} %collective-permute-done.5), channel_id=1, source_target_pairs={{0,4},{4,8},{8,12},{12,16},{16,20},{20,24},{24,28},{28,32},{32,36}... | collective-permute-start | bytes 1572872 | tf_op jit(solution)/shard_map/ppermute | solution.py:18
  107.6 16.3 %collective-permute-start.7 = (bf16[512,512]{1,0:T(8,128)(2,1)}, bf16[512,512]{1,0:T(8,128)(2,1)}, u32[]{:S(2)}, u32[]{:S(2)}) collective-permute-start(bf16[512,512]{1,0:T(8,128)(2,1)} %collective-permute-done.6), channel_id=1, source_target_pairs={{0,4},{4,8},{8,12},{12,16},{16,20},{20,24},{24,28},{28,32},{32,36}... | collective-permute-start | bytes 1572872 | tf_op jit(solution)/shard_map/ppermute | solution.py:18
  124.9 1.5 copy-start
where the time goes:
time: 171 us
  waiting for transfers between devices  82.7 us (48%)
  Pallas kernels  44.3 us (26%)
  local copies, waits for them, and re-layouts  13.2 us (8%)
  starting transfers between devices  12.8 us (7%)
  other arithmetic  9.08 us (5%)
  matrix products  8.49 us (5%)
    ppermute x4, waiting for transfers between devices, shifted(): lax.ppermute(value, axis, [(source, source + steps) for source in range(l...  49.4 us
    pallas_call x1, Pallas kernels, attend_all(): pl.pallas_call(functools.partial(attention_kernel, group, tok, HD ** (-0....  44.3 us
    ppermute x4, waiting for transfers between devices, flipped(): lax.ppermute(value, axis, [(source, source ^ bit) for source in range(cou...  33.3 us
    ppermute x4, starting transfers between devices, shifted(): lax.ppermute(value, axis, [(source, source + steps) for source in range(l...  11.6 us
    unnamed x18, local copies, waits for them, and re-layouts  10.5 us
    dot_general x4, matrix products, body(): term = jnp.dot(normed, rows, preferred_element_type=jnp.float32)  8.49 us
  transfers between devices with their start and end apart: 8, of which 6 were waited for; matrix products, arithmetic and copies ran while one was open for 8% of the time, Pallas kernels for 0%

commit v1 on v0

v1 whole, which is shorter than its diff:
```python
import functools

import jax
import jax.numpy as jnp
from jax import lax
from jax.experimental import pallas as pl
from jax.experimental.pallas import tpu as pltpu
from jax.sharding import PartitionSpec as P

D = 5120
HD = 128
CYCLE = 4


def shifted(value, axis, steps):
    count = lax.axis_size(axis)
    leading, last = (max(0, -steps), min(count, count - steps))
    return lax.ppermute(value, axis, [(source, source + steps) for source in range(leading, last)])


def flipped(value, axis, bit):
    count = lax.axis_size(axis)
    return lax.ppermute(value, axis, [(source, source ^ bit) for source in range(count)])


def ring_kernel(group, tok, scale, q_ref, kv_ref, qdoc_ref, kdoc_ref, o_ref,
                recv, send_sem, recv_sem, m_ref, l_ref, acc_ref, bias_ref):
    c = lax.axis_index("ctx")
    t = lax.axis_index("tp")
    n = lax.axis_size("ctx")
    heads = q_ref.shape[1] // HD
    kv_width = kv_ref.shape[1] // 2
    half = tok // 2

    barrier = pltpu.get_barrier_semaphore()

    @pl.when(c > 0)
    def _():
        pl.semaphore_signal(barrier, inc=1, device_id=(c - 1, t), device_id_type=pl.DeviceIdType.MESH)

    @pl.when(c < n - 1)
    def _():
        pl.semaphore_signal(barrier, inc=1, device_id=(c + 1, t), device_id_type=pl.DeviceIdType.MESH)

    peers = (c > 0).astype(jnp.int32) + (c < n - 1).astype(jnp.int32)
    pl.semaphore_wait(barrier, peers)

    def copy_of(step):
        src = kv_ref if step == 0 else recv.at[step - 1]
        return pltpu.make_async_remote_copy(
            src_ref=src, dst_ref=recv.at[step], send_sem=send_sem.at[step],
            recv_sem=recv_sem.at[step], device_id=(c + 1, t),
            device_id_type=pl.DeviceIdType.MESH)

    def sends_at(step):
        return (c >= step) & (c < n - 1)

    m_ref[...] = jnp.full(m_ref.shape, -1e30, jnp.float32)
    l_ref[...] = jnp.zeros(l_ref.shape, jnp.float32)
    acc_ref[...] = jnp.zeros(acc_ref.shape, jnp.float32)

    def compute(b, kv, tiles):
        for r0, rr, c0, cc in tiles:
            same = qdoc_ref[r0:r0 + rr, :] == kdoc_ref[b:b + 1, c0:c0 + cc]
            if b == 0:
                rows = lax.broadcasted_iota(jnp.int32, (rr, cc), 0) + r0
                cols = lax.broadcasted_iota(jnp.int32, (rr, cc), 1) + c0
                same = same & (cols <= rows)
            bias_ref[r0:r0 + rr, c0:c0 + cc] = jnp.where(same, 0.0, -1e30)

        def head(h, carry):
            g = h // group
            qcol = pl.multiple_of(h * HD, HD)
            kcol = pl.multiple_of(g * HD, HD)
            vcol = pl.multiple_of(kv_width + g * HD, HD)
            for r0, rr, c0, cc in tiles:
                q = q_ref[r0:r0 + rr, pl.ds(qcol, HD)]
                keys = kv[c0:c0 + cc, pl.ds(kcol, HD)]
                values = kv[c0:c0 + cc, pl.ds(vcol, HD)]
                s = lax.dot_general(q, keys, (((1,), (1,)), ((), ())),
                                    preferred_element_type=jnp.float32) * scale
                s = s + bias_ref[r0:r0 + rr, c0:c0 + cc]
                prev = m_ref[h, r0:r0 + rr, :]
                top = jnp.max(s, axis=1, keepdims=True)
                best = jnp.maximum(prev, top)
                shrink = jnp.exp(prev - best)
                p = jnp.exp(s - best[:, :1])
                m_ref[h, r0:r0 + rr, :] = best
                l_ref[h, r0:r0 + rr, :] = l_ref[h, r0:r0 + rr, :] * shrink + jnp.sum(p, axis=1, keepdims=True)
                acc_ref[h, r0:r0 + rr, :] = acc_ref[h, r0:r0 + rr, :] * shrink + jnp.dot(
                    p.astype(jnp.bfloat16), values, preferred_element_type=jnp.float32)
            return carry

        lax.fori_loop(0, heads, head, 0)

    full = [(0, tok, 0, tok)]
    lower = [(0, half, 0, half), (half, half, 0, tok)]
    upper = [(0, half, 0, tok), (half, half, half, half)]
    nback = recv.shape[0]

    @pl.when(c < n - 1)
    def _():
        copy_of(0).start()

    compute(0, kv_ref, lower)
    for s in range(1, nback + 1):
        @pl.when(c >= s)
        def _():
            copy_of(s - 1).wait_recv()

        if s < nback:
            @pl.when(sends_at(s))
            def _():
                copy_of(s).start()

        @pl.when(c >= s)
        def _():
            compute(s, recv.at[s - 1], upper if s == nback else full)

    for s in range(nback):
        @pl.when(sends_at(s))
        def _():
            copy_of(s).wait_send()

    def finish(h, carry):
        col = pl.multiple_of(h * HD, HD)
        o_ref[:, pl.ds(col, HD)] = (acc_ref[h] / l_ref[h]).astype(o_ref.dtype)
        return carry

    lax.fori_loop(0, heads, finish, 0)


def ring_attention(queries, kv_local, qdoc, kdoc, kv_heads):
    tok, width = queries.shape
    group = width // HD // kv_heads
    heads = width // HD
    vmem = pltpu.VMEM
    return pl.pallas_call(
        functools.partial(ring_kernel, group, tok, HD ** (-0.5)),
        out_shape=jax.ShapeDtypeStruct((tok, width), queries.dtype),
        in_specs=[pl.BlockSpec(memory_space=vmem)] * 4,
        out_specs=pl.BlockSpec(memory_space=vmem),
        scratch_shapes=[
            vmem((CYCLE, tok, kv_local.shape[1]), kv_local.dtype),
            pltpu.SemaphoreType.DMA((CYCLE,)),
            pltpu.SemaphoreType.DMA((CYCLE,)),
            vmem((heads, tok, HD), jnp.float32),
            vmem((heads, tok, HD), jnp.float32),
            vmem((heads, tok, HD), jnp.float32),
            vmem((tok, tok), jnp.float32),
        ],
        compiler_params=pltpu.CompilerParams(
            collective_id=0, has_side_effects=True, vmem_limit_bytes=48 * 1024 * 1024),
    )(queries, kv_local, qdoc, kdoc)


def body(hidden, queries, lengths, norm_gain, kv_weight, kv_bias):
    tok, width = hidden.shape
    tpi = lax.axis_index("tp")
    across = flipped(hidden, "tp", 2)
    pair = flipped(jnp.stack([hidden, across]), "tp", 1)
    gain_across = flipped(norm_gain, "tp", 2)
    gain_pair = flipped(jnp.stack([norm_gain, gain_across]), "tp", 1)
    blocks = [
        (hidden, norm_gain, tpi),
        (across, gain_across, tpi ^ 2),
        (pair[0], gain_pair[0], tpi ^ 1),
        (pair[1], gain_pair[1], tpi ^ 3),
    ]
    squares = None
    for part, _, _ in blocks:
        xf = part.astype(jnp.float32)
        term = jnp.sum(xf * xf, axis=1)
        squares = term if squares is None else squares + term
    scale_rows = lax.rsqrt(squares / D + 1e-06)
    flat_weight = kv_weight.reshape(kv_weight.shape[0], -1)
    summed = None
    for part, gain, owner in blocks:
        normed = (part.astype(jnp.float32) * scale_rows[:, None] * gain[None, :]).astype(jnp.bfloat16)
        rows = lax.dynamic_slice_in_dim(flat_weight, owner * width, width, 0)
        term = jnp.dot(normed, rows, preferred_element_type=jnp.float32)
        summed = term if summed is None else summed + term
    kv_local = (summed + kv_bias.reshape(-1)[None, :]).astype(jnp.bfloat16)
    kv_heads = kv_weight.shape[2] // HD

    device = lax.axis_index("ctx")
    ends = jnp.cumsum(lengths)
    backs = jnp.arange(CYCLE + 1, dtype=jnp.int32)
    starts = (device - backs) * tok
    positions = starts[:, None] + jnp.arange(tok, dtype=jnp.int32)[None, :]
    found = jnp.sum((positions[:, :, None] >= ends[None, None, :]).astype(jnp.int32), axis=2)
    kdoc = jnp.where((device - backs >= 0)[:, None], found, -1)
    qdoc = found[0]
    kdoc = jnp.concatenate([kdoc, jnp.full((8 - CYCLE - 1, tok), -1, jnp.int32)], axis=0)
    return ring_attention(queries, kv_local, qdoc[:, None], kdoc, kv_heads)


def solution(mesh):
    in_specs = (P("ctx", "tp"), P("ctx", "tp"), P(), P("tp"), P(None, None, "tp"), P(None, "tp"))
    out_specs = P("ctx", "tp")
    return jax.shard_map(body, mesh=mesh, in_specs=in_specs, out_specs=out_specs, check_vma=False)
```

time: 171 us -> 127 us (0.74)
  the two profiles are of different devices: /device:TPU:58 before, /device:TPU:6 now
where the time goes in v1:
time: 127 us; the launch traced here: 126 us
  Pallas kernels  70.4 us (55%)
  waiting for transfers between devices  31.1 us (24%)
  matrix products  7.78 us (6%)
  other arithmetic  7.67 us (6%)
  local copies, waits for them, and re-layouts  7.66 us (6%)
  starting transfers between devices  1.75 us (1%)
    pallas_call x1, Pallas kernels, ring_attention(): pl.pallas_call(functools.partial(ring_kernel, group, tok, HD ** (-0.5)),...  70.4 us
    ppermute x4, waiting for transfers between devices, flipped(): lax.ppermute(value, axis, [(source, source ^ bit) for source in range(cou...  31.1 us
    dot_general x4, matrix products, body(): term = jnp.dot(normed, rows, preferred_element_type=jnp.float32)  7.78 us
    unnamed x15, local copies, waits for them, and re-layouts  7.28 us
    another operation x1, other arithmetic, body(): pair = flipped(jnp.stack([hidden, across]), 'tp', 1)  3.23 us
    reduce_sum x3, other arithmetic, body(): term = jnp.sum(xf * xf, axis=1)  2.96 us
  transfers between devices with their start and end apart: 4, of which 2 were waited for; matrix products, arithmetic and copies ran while one was open for 6% of the time, Pallas kernels for 0%

profile of v1, /device:TPU:6, one launch (start us, length us, event | category | flops | bytes accessed | tf_op | source)
XLA Modules:
  0.0 126.5 jit_solution(4918623644390977394)
XLA Ops:
  0.0 0.8 collective-permute-start
  0.8 29.9 %collective-permute-done = bf16[512,1280]{1,0:T(8,128)(2,1)S(1)} collective-permute-done((bf16[512,1280]{1,0:T(8,128)(2,1)}, bf16[512,1280]{1,0:T(8,128)(2,1)S(1)}, u32[]{:S(2)}, u32[]{:S(2)}) %collective-permute-start) | collective-permute-done | bytes 1310752 | tf_op jit(solution)/shard_map/ppermute | solution.py:23
  30.7 0.0 copy-start.3
  30.7 0.0 copy-start.5
  30.7 0.0 copy-start.1
  30.7 3.2 %pad_maximum_fusion = bf16[2,512,1280]{2,1,0:T(8,128)(2,1)} fusion(bf16[1,512,1280]{2,1,0:T(8,128)(2,1)S(1)} %bitcast.28, bf16[1,512,1280]{2,1,0:T(8,128)(2,1)} %bitcast.27), kind=kLoop, calls=%fused_computation.20 | loop fusion | flops 1310720 | bytes 5242880 | tf_op jit(solution)/shard_map/stack | solution.py:161
  34.0 0.0 collective-permute-start.1
  34.0 0.0 copy-done.3
  34.0 0.8 collective-permute-start.2
  34.8 0.0 copy-done.5
  34.8 0.3 reduce-window.9
  35.1 0.1 slice.26
  35.2 0.1 slice_reduce_fusion.2
  35.3 0.1 add_bitcast_fusion
  35.4 0.1 iota_add_fusion
  35.5 0.9 convert_reduce_fusion
  36.4 0.1 broadcast_select_fusion
  36.5 1.1 collective-permute-done.2
  37.6 0.1 collective-permute-start.3
  37.7 0.0 copy-done.1
  37.8 0.3 fusion
  38.1 0.0 copy-start.4
  38.1 5.7 %copy.9 = bf16[640,8,2,256]{3,1,2,0:T(8,128)(2,1)} copy(bf16[640,8,2,256]{3,2,1,0:T(2,128)(2,1)} %bitcast.29) | data formatting | bytes 10485760
  43.8 0.0 copy-done.4
  43.8 0.1 copy.8.qdoc_ref
  44.0 0.0 collective-permute-done.3
  44.0 0.3 fusion.3
  44.4 0.0 collective-permute-done.1
  44.4 2.3 %fusion.6 = (f32[512]{0:T(512)S(1)}, f32[512]{0:T(512)S(1)}) fusion(bf16[2,512,1280]{2,1,0:T(8,128)(2,1)} %collective-permute-done.1), kind=kLoop, calls=%fused_computation.14 | loop fusion | flops 3931136 | bytes 2625536 | tf_op jit(solution)/shard_map/reduce_sum | solution.py:173
  46.7 0.0 copy-start.2
  46.7 2.4 %fusion.17 = f32[512,512]{1,0:T(8,128)S(1)} fusion(bf16[512,1280]{1,0:T(8,128)(2,1)S(1)} %copy-done.1, bf16[5120,512]{1,0:T(8,128)(2,1)} %bitcast.30, s32[]{:T(128)S(6)} %select_n.16, f32[1280]{0:T(1024)S(1)} %copy-done.3, f32[512]{0:T(512)S(1)} %add_rsqrt_fusion), kind=kOutput, calls=%fused_computation.26 | convolution fusion | flops 673710080 | bytes 3677188 | tf_op jit(solution)/shard_map/dot_general | solution.py:181
  49.1 0.5 copy-done.2
  49.6 0.9 convolution_add_fusion.1
  50.5 2.2 %fusion.13 = f32[512,512]{1,0:T(8,128)S(1)} fusion(bf16[5120,512]{1,0:T(8,128)(2,1)S(1)} %bitcast.32, s32[]{:T(128)S(6)} %select_n.19, f32[1280]{0:T(1024)S(1)} %get-tuple-element.8, f32[512]{0:T(512)S(1)} %add_rsqrt_fusion, bf16[2,512,1280]{2,1,0:T(8,128)(2,1)} %collective-permute-done.1), kind=kOutput, calls=%fused_computation.25 | convolution fusion | flops 673710080 | bytes 3680260 | tf_op jit(solution)/shard_map/dot_general | solution.py:181
  52.7 0.0 copy-start
  52.7 2.3 %fusion.36.kv_ref = bf16[512,512]{1,0:T(8,128)(2,1)S(1)} fusion(f32[512,512]{1,0:T(8,128)S(1)} %fusion.13, f32[512,512]{1,0:T(8,128)S(1)} %convolution_add_fusion.1, bf16[5120,512]{1,0:T(8,128)(2,1)S(1)} %bitcast.33, s32[]{:T(128)S(6)} %select_n.18, f32[1280]{0:T(1024)S(1)} %get-tuple-element.7, f32[512]{0:T(512)S(1)} %add_rsqrt_fusion, ...), kind=kOutput, calls=%fused_computation.42 | convolution fusion | flops 674758656 | bytes 5255172 | tf_op jit(solution)/shard_map/dot_general | solution.py:181
  55.0 0.0 copy-done
  55.0 70.4 %shard_map.64 = bf16[512,1280]{1,0:T(8,128)(2,1)S(1)} custom-call(bf16[512,1280]{1,0:T(8,128)(2,1)S(1)} %copy-done, bf16[512,512]{1,0:T(8,128)(2,1)S(1)} %fusion.36.kv_ref, s32[512,1]{1,0:T(8,128)S(1)} %copy.8.qdoc_ref, s32[8,512]{1,0:T(8,128)S(1)} %concatenate.3.kdoc_ref), custom_call_target="tpu_custom_call" | custom-call | tf_op jit(solution)/shard_map/pallas_call | solution.py:138
  125.4 1.1 copy.12
  (11 shorter events, 0.1 us)
Async XLA Ops:
  0.0 30.7 %collective-permute-start = (bf16[512,1280]{1,0:T(8,128)(2,1)}, bf16[512,1280]{1,0:T(8,128)(2,1)S(1)}, u32[]{:S(2)}, u32[]{:S(2)}) collective-permute-start(bf16[512,1280]{1,0:T(8,128)(2,1)} %param.6), channel_id=1, source_target_pairs={{0,2},{1,3},{2,0},{3,1},{4,6},{5,7},{6,4},{7,5},{8,10},{9,11},{10,... | collective-permute-start | bytes 3932168 | tf_op jit(solution)/shard_map/ppermute | solution.py:23
  30.7 3.2 %copy-start.3 = (f32[1280]{0:T(1024)S(1)}, f32[1280]{0:T(1024)}, u32[]{:S(2)}) copy-start(f32[1280]{0:T(1024)} %param.9) | copy-start | bytes 15364
  30.7 4.1 %copy-start.5 = (s32[256]{0:T(256)S(1)}, s32[256]{0:T(256)}, u32[]{:S(2)}) copy-start(s32[256]{0:T(256)} %param.8) | copy-start | bytes 3076
  30.7 7.0 %copy-start.1 = (bf16[512,1280]{1,0:T(8,128)(2,1)S(1)}, bf16[512,1280]{1,0:T(8,128)(2,1)}, u32[]{:S(2)}) copy-start(bf16[512,1280]{1,0:T(8,128)(2,1)} %param.6) | copy-start | bytes 3932164
  34.0 10.4 %collective-permute-start.1 = (bf16[2,512,1280]{2,1,0:T(8,128)(2,1)}, bf16[2,512,1280]{2,1,0:T(8,128)(2,1)}, u32[]{:S(2)}, u32[]{:S(2)}) collective-permute-start(bf16[2,512,1280]{2,1,0:T(8,128)(2,1)} %pad_maximum_fusion), channel_id=1, source_target_pairs={{0,1},{1,0},{2,3},{3,2},{4,5},{5,4},{6,7},{7,6},{8,9},{9,8},{10,11... | collective-permute-start | bytes 7864328 | tf_op jit(solution)/shard_map/ppermute | solution.py:23
  34.0 3.7 %collective-permute-start.2 = (f32[1280]{0:T(1024)S(1)}, f32[1280]{0:T(1024)S(1)}, u32[]{:S(2)}, u32[]{:S(2)}) collective-permute-start(f32[1280]{0:T(1024)S(1)} %copy-done.3), channel_id=1, source_target_pairs={{0,2},{1,3},{2,0},{3,1},{4,6},{5,7},{6,4},{7,5},{8,10},{9,11},{10,... | collective-permute-start | bytes 15368 | tf_op jit(solution)/shard_map/ppermute | solution.py:23
  37.6 6.3 %collective-permute-start.3 = (f32[2,1280]{1,0:T(2,128)S(1)}, f32[2,1280]{1,0:T(2,128)S(1)}, u32[]{:S(2)}, u32[]{:S(2)}) collective-permute-start(f32[2,1280]{1,0:T(2,128)S(1)} %pad_maximum_fusion.1), channel_id=1, source_target_pairs={{0,1},{1,0},{2,3},{3,2},{4,5},{5,4},{6,7},{7,6},{8,9},{9,8},{10,11... | collective-permute-start | bytes 30728 | tf_op jit(solution)/shard_map/ppermute | solution.py:23
  38.1 5.7 %copy-start.4 = (f32[2,256]{1,0:T(2,128)S(1)}, f32[2,256]{1,0:T(2,128)}, u32[]{:S(2)}) copy-start(f32[2,256]{1,0:T(2,128)} %param.11) | copy-start | bytes 6148
  46.7 2.9 %copy-start.2 = (bf16[640,8,2,256]{3,1,2,0:T(8,128)(2,1)S(1)}, bf16[640,8,2,256]{3,1,2,0:T(8,128)(2,1)}, u32[]{:S(2)}) copy-start(bf16[640,8,2,256]{3,1,2,0:T(8,128)(2,1)} %copy.9) | copy-start | bytes 15728644
  52.7 2.3 %copy-start = (bf16[512,1280]{1,0:T(8,128)(2,1)S(1)}, bf16[512,1280]{1,0:T(8,128)(2,1)}, u32[]{:S(2)}) copy-start(bf16[512,1280]{1,0:T(8,128)(2,1)} %q_ref.1) | copy-start | bytes 3932164

commit v2 on v1

--- a/solution.py
+++ b/solution.py
@@ -68,30 +68,31 @@
                 same = same & (cols <= rows)
             bias_ref[r0:r0 + rr, c0:c0 + cc] = jnp.where(same, 0.0, -1e30)
 
-        def head(h, carry):
-            g = h // group
-            qcol = pl.multiple_of(h * HD, HD)
+        def pair_of_heads(g, carry):
             kcol = pl.multiple_of(g * HD, HD)
             vcol = pl.multiple_of(kv_width + g * HD, HD)
-            for r0, rr, c0, cc in tiles:
-                q = q_ref[r0:r0 + rr, pl.ds(qcol, HD)]
-                keys = kv[c0:c0 + cc, pl.ds(kcol, HD)]
-                values = kv[c0:c0 + cc, pl.ds(vcol, HD)]
-                s = lax.dot_general(q, keys, (((1,), (1,)), ((), ())),
-                                    preferred_element_type=jnp.float32) * scale
-                s = s + bias_ref[r0:r0 + rr, c0:c0 + cc]
-                prev = m_ref[h, r0:r0 + rr, :]
-                top = jnp.max(s, axis=1, keepdims=True)
-                best = jnp.maximum(prev, top)
-                shrink = jnp.exp(prev - best)
-                p = jnp.exp(s - best[:, :1])
-                m_ref[h, r0:r0 + rr, :] = best
-                l_ref[h, r0:r0 + rr, :] = l_ref[h, r0:r0 + rr, :] * shrink + jnp.sum(p, axis=1, keepdims=True)
-                acc_ref[h, r0:r0 + rr, :] = acc_ref[h, r0:r0 + rr, :] * shrink + jnp.dot(
-                    p.astype(jnp.bfloat16), values, preferred_element_type=jnp.float32)
+            for j in range(group):
+                h = g * group + j
+                qcol = pl.multiple_of(h * HD, HD)
+                for r0, rr, c0, cc in tiles:
+                    q = q_ref[r0:r0 + rr, pl.ds(qcol, HD)]
+                    keys = kv[c0:c0 + cc, pl.ds(kcol, HD)]
+                    values = kv[c0:c0 + cc, pl.ds(vcol, HD)]
+                    s = lax.dot_general(q, keys, (((1,), (1,)), ((), ())),
+                                        preferred_element_type=jnp.float32) * scale
+                    s = s + bias_ref[r0:r0 + rr, c0:c0 + cc]
+                    prev = m_ref[h, r0:r0 + rr, :]
+                    top = jnp.max(s, axis=1, keepdims=True)
+                    best = jnp.maximum(prev, top)
+                    shrink = jnp.exp(prev - best)
+                    p = jnp.exp(s - best[:, :1])
+                    m_ref[h, r0:r0 + rr, :] = best
+                    l_ref[h, r0:r0 + rr, :] = l_ref[h, r0:r0 + rr, :] * shrink + jnp.sum(p, axis=1, keepdims=True)
+                    acc_ref[h, r0:r0 + rr, :] = acc_ref[h, r0:r0 + rr, :] * shrink + jnp.dot(
+                        p.astype(jnp.bfloat16), values, preferred_element_type=jnp.float32)
             return carry
 
-        lax.fori_loop(0, heads, head, 0)
+        lax.fori_loop(0, heads // group, pair_of_heads, 0)
 
     full = [(0, tok, 0, tok)]
     lower = [(0, half, 0, half), (half, half, 0, tok)]
@@ -158,14 +159,16 @@
     tok, width = hidden.shape
     tpi = lax.axis_index("tp")
     across = flipped(hidden, "tp", 2)
-    pair = flipped(jnp.stack([hidden, across]), "tp", 1)
+    beside = flipped(hidden, "tp", 1)
+    diagonal = flipped(across, "tp", 1)
     gain_across = flipped(norm_gain, "tp", 2)
-    gain_pair = flipped(jnp.stack([norm_gain, gain_across]), "tp", 1)
+    gain_beside = flipped(norm_gain, "tp", 1)
+    gain_diagonal = flipped(gain_across, "tp", 1)
     blocks = [
         (hidden, norm_gain, tpi),
         (across, gain_across, tpi ^ 2),
-        (pair[0], gain_pair[0], tpi ^ 1),
-        (pair[1], gain_pair[1], tpi ^ 3),
+        (beside, gain_beside, tpi ^ 1),
+        (diagonal, gain_diagonal, tpi ^ 3),
     ]
     squares = None
     for part, _, _ in blocks:

time: 127 us -> 121 us (0.953)
  waiting for transfers between devices: 31.1 us -> 27.4 us
  Pallas kernels: 70.4 us -> 67.3 us
    ppermute x4 -> x6, waiting for transfers between devices: 31.1 us -> 27.4 us  [flipped(): lax.ppermute(value, axis, [(source, source ^ bit) for source in range(cou...]
    pallas_call x1, Pallas kernels: 70.4 us -> 67.3 us  [ring_attention(): pl.pallas_call(functools.partial(ring_kernel, group, tok, HD ** (-0.5)),...]
    another operation x5 -> x3, other arithmetic: 3.66 us -> 1.09 us  [the longest x1 3.23 us: body(): pair = flipped(jnp.stack([hidden, across]), 'tp', 1)]
    reduce_sum x3 -> x4, other arithmetic: 2.96 us -> 5.27 us  [body(): term = jnp.sum(xf * xf, axis=1)]
    ppermute x4 -> x6, starting transfers between devices: 1.75 us -> 2.85 us  [flipped(): lax.ppermute(value, axis, [(source, source ^ bit) for source in range(cou...]
    unnamed x15 -> x13, local copies, waits for them, and re-layouts: 7.28 us -> 7.27 us
  transfers between devices with their start and end apart: 4 -> 6, of which waited for: 2 -> 1; matrix products, arithmetic and copies ran while one was open for 6% -> 16% of each run, Pallas kernels for 0% -> 0%
where the time goes in v2:
time: 121 us
  Pallas kernels  67.3 us (56%)
  waiting for transfers between devices  27.4 us (23%)
  matrix products  7.77 us (6%)
  local copies, waits for them, and re-layouts  7.61 us (6%)
  other arithmetic  7.4 us (6%)
  starting transfers between devices  2.85 us (2%)
    pallas_call x1, Pallas kernels, ring_attention(): pl.pallas_call(functools.partial(ring_kernel, group, tok, HD ** (-0.5)),...  67.3 us
    ppermute x6, waiting for transfers between devices, flipped(): lax.ppermute(value, axis, [(source, source ^ bit) for source in range(cou...  27.4 us
    dot_general x4, matrix products, body(): term = jnp.dot(normed, rows, preferred_element_type=jnp.float32)  7.77 us
    unnamed x13, local copies, waits for them, and re-layouts  7.27 us
    reduce_sum x4, other arithmetic, body(): term = jnp.sum(xf * xf, axis=1)  5.27 us
    ppermute x6, starting transfers between devices, flipped(): lax.ppermute(value, axis, [(source, source ^ bit) for source in range(cou...  2.85 us
  transfers between devices with their start and end apart: 6, of which 1 were waited for; matrix products, arithmetic and copies ran while one was open for 16% of the time, Pallas kernels for 0%

profile of v2, /device:TPU:6, one launch (start us, length us, event | category | flops | bytes accessed | tf_op | source)
XLA Modules:
  0.0 120.5 jit_solution(7078908557918757257)
XLA Ops:
  0.0 0.8 collective-permute-start
  0.8 0.0 collective-permute-start.1
  0.8 1.2 collective-permute-start.3
  2.0 0.2 collective-permute-start.4
  2.3 1.0 reduce-window.9
  3.2 0.1 slice.10
  3.4 0.1 slice_reduce_fusion
  3.5 0.1 iota_add_fusion
  3.5 27.4 %collective-permute-done = bf16[512,1280]{1,0:T(8,128)(2,1)} collective-permute-done((bf16[512,1280]{1,0:T(8,128)(2,1)}, bf16[512,1280]{1,0:T(8,128)(2,1)}, u32[]{:S(2)}, u32[]{:S(2)}) %collective-permute-start) | collective-permute-done | bytes 1310752 | tf_op jit(solution)/shard_map/ppermute | solution.py:23
  30.9 0.0 collective-permute-start.2
  30.9 0.1 add_bitcast_fusion
  31.0 0.9 convert_reduce_fusion
  31.9 0.1 broadcast_select_fusion
  32.0 1.6 %fusion = f32[512]{0:T(512)S(1)} fusion(bf16[512,1280]{1,0:T(8,128)(2,1)} %param.6), kind=kLoop, calls=%fused_computation.8 | loop fusion | flops 1965568 | bytes 1312768 | tf_op jit(solution)/shard_map/reduce_sum | solution.py:176
  33.6 0.0 copy-start.3
  33.7 5.7 %copy.9 = bf16[640,8,2,256]{3,1,2,0:T(8,128)(2,1)} copy(bf16[640,8,2,256]{3,2,1,0:T(2,128)(2,1)} %bitcast.9) | data formatting | bytes 10485760
  39.3 0.0 copy-start.2
  39.3 0.0 copy-start.4
  39.3 0.0 copy-done.3
  39.3 0.1 copy.8.qdoc_ref
  39.5 0.0 collective-permute-done.3
  39.5 0.6 collective-permute-start.5
  40.1 1.6 %fusion.3 = f32[512]{0:T(512)S(1)} fusion(bf16[512,1280]{1,0:T(8,128)(2,1)} %collective-permute-done), kind=kLoop, calls=%fused_computation.11 | loop fusion | flops 1965568 | bytes 1312768 | tf_op jit(solution)/shard_map/reduce_sum | solution.py:176
  41.8 0.0 collective-permute-done.1
  41.8 0.3 fusion.6
  42.1 0.0 collective-permute-done.2
  42.1 1.6 %fusion.9 = f32[512]{0:T(512)S(1)} fusion(bf16[512,1280]{1,0:T(8,128)(2,1)} %collective-permute-done.2), kind=kLoop, calls=%fused_computation.17 | loop fusion | flops 1965568 | bytes 1312768 | tf_op jit(solution)/shard_map/reduce_sum | solution.py:176
  43.8 0.0 copy-done.2
  43.8 0.0 copy-done.4
  43.8 0.0 copy-start.1
  43.8 2.4 %fusion.16 = f32[512,512]{1,0:T(8,128)S(1)} fusion(bf16[512,1280]{1,0:T(8,128)(2,1)S(1)} %copy-done.2, bf16[5120,512]{1,0:T(8,128)(2,1)} %bitcast.10, s32[]{:T(128)S(6)} %select_n.16, f32[1280]{0:T(1024)S(1)} %copy-done.4, f32[512]{0:T(512)S(1)} %add_rsqrt_fusion), kind=kOutput, calls=%fused_computation.25 | convolution fusion | flops 673710080 | bytes 3677188 | tf_op jit(solution)/shard_map/dot_general | solution.py:184
  46.2 0.5 copy-done.1
  46.7 2.2 %convolution_add_fusion.2 = f32[512,512]{1,0:T(8,128)S(1)} fusion(f32[512,512]{1,0:T(8,128)S(1)} %fusion.16, bf16[512,1280]{1,0:T(8,128)(2,1)} %collective-permute-done, bf16[5120,512]{1,0:T(8,128)(2,1)S(1)} %bitcast.11, s32[]{:T(128)S(6)} %select_n.17, f32[1280]{0:T(1024)S(1)} %collective-permute-done.3, f32[512]{0:T(512)S(1)} %add_rsqrt_fusion), kind=kOutput, calls=%fused_computation.24 | convolution fusion | flops 673972224 | bytes 4728836 | tf_op jit(solution)/shard_map/dot_general | solution.py:184
  48.9 0.0 collective-permute-done.4
  48.9 0.9 convolution_add_fusion.1
  49.8 0.0 collective-permute-done.5
  49.8 0.0 copy-start
  49.8 2.3 %fusion.30.kv_ref = bf16[512,512]{1,0:T(8,128)(2,1)S(1)} fusion(f32[512,512]{1,0:T(8,128)S(1)} %convolution_add_fusion.1, bf16[5120,512]{1,0:T(8,128)(2,1)S(1)} %bitcast.13, s32[]{:T(128)S(6)} %select_n.19, bf16[512,1280]{1,0:T(8,128)(2,1)} %collective-permute-done.2, f32[1280]{0:T(1024)S(1)} %collective-permute-done.5, f32[512]{0:T(512)S(1)} %add_rsqrt_fusion, ...), kind=kOutput, calls=%fused_computation.38 | convolution fusion | flops 674496512 | bytes 4206596 | tf_op jit(solution)/shard_map/dot_general | solution.py:184
  52.2 0.0 copy-done
  52.2 67.3 %shard_map.64 = bf16[512,1280]{1,0:T(8,128)(2,1)S(1)} custom-call(bf16[512,1280]{1,0:T(8,128)(2,1)S(1)} %copy-done, bf16[512,512]{1,0:T(8,128)(2,1)S(1)} %fusion.30.kv_ref, s32[512,1]{1,0:T(8,128)S(1)} %copy.8.qdoc_ref, s32[8,512]{1,0:T(8,128)S(1)} %concatenate.3.kdoc_ref), custom_call_target="tpu_custom_call" | custom-call | tf_op jit(solution)/shard_map/pallas_call | solution.py:139
  119.4 1.1 copy.12
  (7 shorter events, 0.1 us)
Async XLA Ops:
  0.0 30.9 %collective-permute-start = (bf16[512,1280]{1,0:T(8,128)(2,1)}, bf16[512,1280]{1,0:T(8,128)(2,1)}, u32[]{:S(2)}, u32[]{:S(2)}) collective-permute-start(bf16[512,1280]{1,0:T(8,128)(2,1)} %param.6), channel_id=1, source_target_pairs={{0,2},{1,3},{2,0},{3,1},{4,6},{5,7},{6,4},{7,5},{8,10},{9,11},{10,... | collective-permute-start | bytes 3932168 | tf_op jit(solution)/shard_map/ppermute | solution.py:23
  0.8 41.0 %collective-permute-start.1 = (bf16[512,1280]{1,0:T(8,128)(2,1)}, bf16[512,1280]{1,0:T(8,128)(2,1)S(1)}, u32[]{:S(2)}, u32[]{:S(2)}) collective-permute-start(bf16[512,1280]{1,0:T(8,128)(2,1)} %param.6), channel_id=1, source_target_pairs={{0,1},{1,0},{2,3},{3,2},{4,5},{5,4},{6,7},{7,6},{8,9},{9,8},{10,11... | collective-permute-start | bytes 3932168 | tf_op jit(solution)/shard_map/ppermute | solution.py:23
  0.8 38.7 %collective-permute-start.3 = (f32[1280]{0:T(1024)}, f32[1280]{0:T(1024)S(1)}, u32[]{:S(2)}, u32[]{:S(2)}) collective-permute-start(f32[1280]{0:T(1024)} %param.9), channel_id=1, source_target_pairs={{0,2},{1,3},{2,0},{3,1},{4,6},{5,7},{6,4},{7,5},{8,10},{9,11},{10,... | collective-permute-start | bytes 15368 | tf_op jit(solution)/shard_map/ppermute | solution.py:23
  2.0 46.9 %collective-permute-start.4 = (f32[1280]{0:T(1024)}, f32[1280]{0:T(1024)S(1)}, u32[]{:S(2)}, u32[]{:S(2)}) collective-permute-start(f32[1280]{0:T(1024)} %param.9), channel_id=1, source_target_pairs={{0,1},{1,0},{2,3},{3,2},{4,5},{5,4},{6,7},{7,6},{8,9},{9,8},{10,11... | collective-permute-start | bytes 15368 | tf_op jit(solution)/shard_map/ppermute | solution.py:23
  30.9 11.2 %collective-permute-start.2 = (bf16[512,1280]{1,0:T(8,128)(2,1)}, bf16[512,1280]{1,0:T(8,128)(2,1)}, u32[]{:S(2)}, u32[]{:S(2)}) collective-permute-start(bf16[512,1280]{1,0:T(8,128)(2,1)} %collective-permute-done), channel_id=1, source_target_pairs={{0,1},{1,0},{2,3},{3,2},{4,5},{5,4},{6,7},{7,6},{8,9},{9,8},{10,11... | collective-permute-start | bytes 3932168 | tf_op jit(solution)/shard_map/ppermute | solution.py:23
  33.6 5.7 %copy-start.3 = (f32[2,256]{1,0:T(2,128)S(1)}, f32[2,256]{1,0:T(2,128)}, u32[]{:S(2)}) copy-start(f32[2,256]{1,0:T(2,128)} %param.11) | copy-start | bytes 6148
  39.3 4.5 %copy-start.2 = (bf16[512,1280]{1,0:T(8,128)(2,1)S(1)}, bf16[512,1280]{1,0:T(8,128)(2,1)}, u32[]{:S(2)}) copy-start(bf16[512,1280]{1,0:T(8,128)(2,1)} %param.6) | copy-start | bytes 3932164
  39.3 4.5 %copy-start.4 = (f32[1280]{0:T(1024)S(1)}, f32[1280]{0:T(1024)}, u32[]{:S(2)}) copy-start(f32[1280]{0:T(1024)} %param.9) | copy-start | bytes 15364
  39.5 10.3 %collective-permute-start.5 = (f32[1280]{0:T(1024)S(1)}, f32[1280]{0:T(1024)S(1)}, u32[]{:S(2)}, u32[]{:S(2)}) collective-permute-start(f32[1280]{0:T(1024)S(1)} %collective-permute-done.3), channel_id=1, source_target_pairs={{0,1},{1,0},{2,3},{3,2},{4,5},{5,4},{6,7},{7,6},{8,9},{9,8},{10,11... | collective-permute-start | bytes 15368 | tf_op jit(solution)/shard_map/ppermute | solution.py:23
  43.8 2.9 %copy-start.1 = (bf16[640,8,2,256]{3,1,2,0:T(8,128)(2,1)S(1)}, bf16[640,8,2,256]{3,1,2,0:T(8,128)(2,1)}, u32[]{:S(2)}) copy-start(bf16[640,8,2,256]{3,1,2,0:T(8,128)(2,1)} %copy.9) | copy-start | bytes 15728644
  49.8 2.3 %copy-start = (bf16[512,1280]{1,0:T(8,128)(2,1)S(1)}, bf16[512,1280]{1,0:T(8,128)(2,1)}, u32[]{:S(2)}) copy-start(bf16[512,1280]{1,0:T(8,128)(2,1)} %q_ref.1) | copy-start | bytes 3932164

commit v3 on v2

--- a/solution.py
+++ b/solution.py
@@ -158,31 +158,30 @@
 def body(hidden, queries, lengths, norm_gain, kv_weight, kv_bias):
     tok, width = hidden.shape
     tpi = lax.axis_index("tp")
-    across = flipped(hidden, "tp", 2)
+    own_squares = jnp.sum(jnp.square(hidden.astype(jnp.float32)), axis=1)
+    squares_across = flipped(own_squares, "tp", 2)
+    squares_beside = flipped(own_squares, "tp", 1)
+    squares_diagonal = flipped(squares_across, "tp", 1)
+    squares = own_squares + squares_beside + squares_across + squares_diagonal
+    scale_rows = lax.rsqrt(squares / D + 1e-06)
+    sending, _ = lax.optimization_barrier((hidden, squares_across))
+    across = flipped(sending, "tp", 2)
     beside = flipped(hidden, "tp", 1)
-    diagonal = flipped(across, "tp", 1)
     gain_across = flipped(norm_gain, "tp", 2)
     gain_beside = flipped(norm_gain, "tp", 1)
     gain_diagonal = flipped(gain_across, "tp", 1)
-    blocks = [
-        (hidden, norm_gain, tpi),
-        (across, gain_across, tpi ^ 2),
-        (beside, gain_beside, tpi ^ 1),
-        (diagonal, gain_diagonal, tpi ^ 3),
-    ]
-    squares = None
-    for part, _, _ in blocks:
-        xf = part.astype(jnp.float32)
-        term = jnp.sum(xf * xf, axis=1)
-        squares = term if squares is None else squares + term
-    scale_rows = lax.rsqrt(squares / D + 1e-06)
     flat_weight = kv_weight.reshape(kv_weight.shape[0], -1)
-    summed = None
-    for part, gain, owner in blocks:
+
+    def project(part, gain, owner):
         normed = (part.astype(jnp.float32) * scale_rows[:, None] * gain[None, :]).astype(jnp.bfloat16)
         rows = lax.dynamic_slice_in_dim(flat_weight, owner * width, width, 0)
-        term = jnp.dot(normed, rows, preferred_element_type=jnp.float32)
-        summed = term if summed is None else summed + term
+        return jnp.dot(normed, rows, preferred_element_type=jnp.float32)
+
+    summed = project(hidden, norm_gain, tpi) + project(beside, gain_beside, tpi ^ 1)
+    across, summed = lax.optimization_barrier((across, summed))
+    diagonal = flipped(across, "tp", 1)
+    summed = summed + project(across, gain_across, tpi ^ 2)
+    summed = summed + project(diagonal, gain_diagonal, tpi ^ 3)
     kv_local = (summed + kv_bias.reshape(-1)[None, :]).astype(jnp.bfloat16)
     kv_heads = kv_weight.shape[2] // HD
 

time: 121 us -> 111 us (0.917)
  waiting for transfers between devices: 27.4 us -> 17.6 us
  other arithmetic: 7.4 us -> 3.78 us
  matrix products: 7.77 us -> 10.7 us
  starting transfers between devices: 2.85 us -> 4.13 us
    ppermute x6 -> x9, waiting for transfers between devices: 27.4 us -> 17.6 us  [flipped(): lax.ppermute(value, axis, [(source, source ^ bit) for source in range(cou...]
    reduce_sum x4 -> x1, other arithmetic: 5.27 us -> 1.65 us  [body(): own_squares = jnp.sum(jnp.square(hidden.astype(jnp.float32)), axis=1)]
    dot_general x4, matrix products: 7.77 us -> 10.7 us  [project(): return jnp.dot(normed, rows, preferred_element_type=jnp.float32)]
    ppermute x6 -> x9, starting transfers between devices: 2.85 us -> 4.13 us  [flipped(): lax.ppermute(value, axis, [(source, source ^ bit) for source in range(cou...]
  transfers between devices with their start and end apart: 6 -> 9, of which waited for: 1 -> 2; matrix products, arithmetic and copies ran while one was open for 16% -> 16% of each run, Pallas kernels for 0% -> 0%
where the time goes in v3:
time: 111 us
  Pallas kernels  67.2 us (61%)
  waiting for transfers between devices  17.6 us (16%)
  matrix products  10.7 us (10%)
  local copies, waits for them, and re-layouts  7.21 us (6%)
  starting transfers between devices  4.13 us (4%)
  other arithmetic  3.78 us (3%)
    pallas_call x1, Pallas kernels, ring_attention(): pl.pallas_call(functools.partial(ring_kernel, group, tok, HD ** (-0.5)),...  67.2 us
    ppermute x9, waiting for transfers between devices, flipped(): lax.ppermute(value, axis, [(source, source ^ bit) for source in range(cou...  17.6 us
    dot_general x4, matrix products, project(): return jnp.dot(normed, rows, preferred_element_type=jnp.float32)  10.7 us
    unnamed x13, local copies, waits for them, and re-layouts  6.87 us
    ppermute x9, starting transfers between devices, flipped(): lax.ppermute(value, axis, [(source, source ^ bit) for source in range(cou...  4.13 us
  transfers between devices with their start and end apart: 9, of which 2 were waited for; matrix products, arithmetic and copies ran while one was open for 16% of the time, Pallas kernels for 0%

profile of v3, /device:TPU:6, one launch (start us, length us, event | category | flops | bytes accessed | tf_op | source)
XLA Modules:
  0.0 110.8 jit_solution(11945827216371113340)
XLA Ops:
  0.0 0.0 collective-permute-start.4
  0.0 1.6 %fusion = f32[512]{0:T(512)S(1)} fusion(bf16[512,1280]{1,0:T(8,128)(2,1)} %param.6), kind=kLoop, calls=%fused_computation.2 | loop fusion | flops 1965568 | bytes 1312768 | tf_op jit(solution)/shard_map/reduce_sum | solution.py:161
  1.6 0.9 collective-permute-start
  2.6 2.8 %collective-permute-done = f32[512]{0:T(512)S(1)} collective-permute-done((f32[512]{0:T(512)S(1)}, f32[512]{0:T(512)S(1)}, u32[]{:S(2)}, u32[]{:S(2)}) %collective-permute-start) | collective-permute-done | bytes 2080 | tf_op jit(solution)/shard_map/ppermute | solution.py:23
  5.3 0.8 collective-permute-start.1
  6.2 0.0 collective-permute-start.2
  6.2 0.5 collective-permute-start.5
  6.7 1.0 reduce-window.9
  7.6 0.1 slice.10
  7.8 0.1 slice_reduce_fusion
  7.9 0.1 collective-permute-start.3
  8.0 0.0 copy-start.3
  8.0 0.0 copy-start.1
  8.0 5.8 %copy.9 = bf16[640,8,2,256]{3,1,2,0:T(8,128)(2,1)} copy(bf16[640,8,2,256]{3,2,1,0:T(2,128)(2,1)} %bitcast.9) | data formatting | bytes 10485760
  13.8 0.0 collective-permute-done.2
  13.8 0.0 copy-done.3
  13.8 1.2 %collective-permute-start.6 = (f32[1280]{0:T(1024)S(1)}, f32[1280]{0:T(1024)S(1)}, u32[]{:S(2)}, u32[]{:S(2)}) collective-permute-start(f32[1280]{0:T(1024)S(1)} %copy-done.3), channel_id=1, source_target_pairs={{0,2},{1,3},{2,0},{3,1},{4,6},{5,7},{6,4},{7,5},{8,10},{9,11},{10,... | collective-permute-start | bytes 15368 | tf_op jit(solution)/shard_map/ppermute | solution.py:23
  15.0 0.0 collective-permute-done.3
  15.0 0.0 copy-done.1
  15.0 2.2 %fusion.5 = f32[512,512]{1,0:T(8,128)S(1)} fusion(bf16[512,1280]{1,0:T(8,128)(2,1)S(1)} %copy-done.1, bf16[5120,512]{1,0:T(8,128)(2,1)} %bitcast.10, s32[]{:T(128)S(6)} %select_n.16, f32[1280]{0:T(1024)S(1)} %copy-done.3, f32[512]{0:T(512)S(1)} %add_rsqrt_fusion), kind=kOutput, calls=%fused_computation.12 | convolution fusion | flops 673710080 | bytes 3677188 | tf_op jit(solution)/shard_map/dot_general | solution.py:178
  17.2 0.0 copy-start.2
  17.2 0.0 collective-permute-done.5
  17.3 0.0 collective-permute-done.4
  17.3 3.6 %convolution_add_fusion = f32[512,512]{1,0:T(8,128)} fusion(f32[512,512]{1,0:T(8,128)S(1)} %fusion.5, bf16[512,1280]{1,0:T(8,128)(2,1)} %collective-permute-done.4, bf16[5120,512]{1,0:T(8,128)(2,1)} %bitcast.11, s32[]{:T(128)S(6)} %select_n.17, f32[1280]{0:T(1024)S(1)} %collective-permute-done.5, f32[512]{0:T(512)S(1)} %add_rsqrt_fusion), kind=kOutput, calls=%fused_computation.9 | convolution fusion | flops 673972224 | bytes 4725764 | tf_op jit(solution)/shard_map/dot_general | solution.py:178
  20.8 14.8 %collective-permute-done.1 = bf16[512,1280]{1,0:T(8,128)(2,1)S(1)} collective-permute-done((bf16[512,1280]{1,0:T(8,128)(2,1)}, bf16[512,1280]{1,0:T(8,128)(2,1)S(1)}, u32[]{:S(2)}, u32[]{:S(2)}) %collective-permute-start.1) | collective-permute-done | bytes 1310752 | tf_op jit(solution)/shard_map/ppermute | solution.py:23
  35.7 0.0 collective-permute-start.7
  35.7 0.1 add_bitcast_fusion
  35.7 0.1 iota_add_fusion
  35.8 0.9 convert_reduce_fusion
  36.7 0.1 broadcast_select_fusion
  36.8 0.0 copy-done.2
  36.8 0.1 copy.8.qdoc_ref
  37.0 0.0 copy-start.4
  37.0 0.0 collective-permute-done.6
  37.0 0.6 collective-permute-start.8
  37.6 2.2 %fusion.3 = f32[512,512]{1,0:T(8,128)S(1)} fusion(bf16[512,1280]{1,0:T(8,128)(2,1)S(1)} %collective-permute-done.1, bf16[5120,512]{1,0:T(8,128)(2,1)} %bitcast.12, s32[]{:T(128)S(6)} %select_n.18, f32[1280]{0:T(1024)S(1)} %collective-permute-done.6, f32[512]{0:T(512)S(1)} %add_rsqrt_fusion), kind=kOutput, calls=%fused_computation.10 | convolution fusion | flops 673710080 | bytes 3677188 | tf_op jit(solution)/shard_map/dot_general | solution.py:178
  39.8 0.0 collective-permute-done.8
  39.8 0.0 collective-permute-done.7
  39.8 0.0 copy-done.4
  39.8 0.0 copy-start
  39.8 2.7 %fusion.25.kv_ref = bf16[512,512]{1,0:T(8,128)(2,1)S(1)} fusion(bf16[5120,512]{1,0:T(8,128)(2,1)} %bitcast.13, s32[]{:T(128)S(6)} %select_n.19, bf16[512,1280]{1,0:T(8,128)(2,1)} %collective-permute-done.7, f32[1280]{0:T(1024)S(1)} %collective-permute-done.8, f32[512]{0:T(512)S(1)} %add_rsqrt_fusion, f32[512,512]{1,0:T(8,128)S(1)} %copy-done.4, ...), kind=kOutput, calls=%fused_computation.27 | convolution fusion | flops 674758656 | bytes 5252100 | tf_op jit(solution)/shard_map/dot_general | solution.py:178
  42.6 0.0 copy-done
  42.6 67.2 %shard_map.64 = bf16[512,1280]{1,0:T(8,128)(2,1)S(1)} custom-call(bf16[512,1280]{1,0:T(8,128)(2,1)S(1)} %copy-done, bf16[512,512]{1,0:T(8,128)(2,1)S(1)} %fusion.25.kv_ref, s32[512,1]{1,0:T(8,128)S(1)} %copy.8.qdoc_ref, s32[8,512]{1,0:T(8,128)S(1)} %concatenate.3.kdoc_ref), custom_call_target="tpu_custom_call" | custom-call | tf_op jit(solution)/shard_map/pallas_call | solution.py:139
  109.7 1.1 copy.12
  (7 shorter events, 0.1 us)
Async XLA Ops:
  0.0 17.3 %collective-permute-start.4 = (bf16[512,1280]{1,0:T(8,128)(2,1)}, bf16[512,1280]{1,0:T(8,128)(2,1)}, u32[]{:S(2)}, u32[]{:S(2)}) collective-permute-start(bf16[512,1280]{1,0:T(8,128)(2,1)} %param.6), channel_id=1, source_target_pairs={{0,1},{1,0},{2,3},{3,2},{4,5},{5,4},{6,7},{7,6},{8,9},{9,8},{10,11... | collective-permute-start | bytes 3932168 | tf_op jit(solution)/shard_map/ppermute | solution.py:23
  1.6 3.7 %collective-permute-start = (f32[512]{0:T(512)S(1)}, f32[512]{0:T(512)S(1)}, u32[]{:S(2)}, u32[]{:S(2)}) collective-permute-start(f32[512]{0:T(512)S(1)} %fusion), channel_id=1, source_target_pairs={{0,2},{1,3},{2,0},{3,1},{4,6},{5,7},{6,4},{7,5},{8,10},{9,11},{10,... | collective-permute-start | bytes 6152 | tf_op jit(solution)/shard_map/ppermute | solution.py:23
  5.3 30.3 %collective-permute-start.1 = (bf16[512,1280]{1,0:T(8,128)(2,1)}, bf16[512,1280]{1,0:T(8,128)(2,1)S(1)}, u32[]{:S(2)}, u32[]{:S(2)}) collective-permute-start(bf16[512,1280]{1,0:T(8,128)(2,1)} %param.6), channel_id=1, source_target_pairs={{0,2},{1,3},{2,0},{3,1},{4,6},{5,7},{6,4},{7,5},{8,10},{9,11},{10,... | collective-permute-start | bytes 3932168 | tf_op jit(solution)/shard_map/ppermute | solution.py:23
  6.2 7.6 %collective-permute-start.2 = (f32[512]{0:T(512)S(1)}, f32[512]{0:T(512)S(1)}, u32[]{:S(2)}, u32[]{:S(2)}) collective-permute-start(f32[512]{0:T(512)S(1)} %fusion), channel_id=1, source_target_pairs={{0,1},{1,0},{2,3},{3,2},{4,5},{5,4},{6,7},{7,6},{8,9},{9,8},{10,11... | collective-permute-start | bytes 6152 | tf_op jit(solution)/shard_map/ppermute | solution.py:23
  6.2 11.1 %collective-permute-start.5 = (f32[1280]{0:T(1024)}, f32[1280]{0:T(1024)S(1)}, u32[]{:S(2)}, u32[]{:S(2)}) collective-permute-start(f32[1280]{0:T(1024)} %param.9), channel_id=1, source_target_pairs={{0,1},{1,0},{2,3},{3,2},{4,5},{5,4},{6,7},{7,6},{8,9},{9,8},{10,11... | collective-permute-start | bytes 15368 | tf_op jit(solution)/shard_map/ppermute | solution.py:23
  7.9 7.1 %collective-permute-start.3 = (f32[512]{0:T(512)S(1)}, f32[512]{0:T(512)S(1)}, u32[]{:S(2)}, u32[]{:S(2)}) collective-permute-start(f32[512]{0:T(512)S(1)} %collective-permute-done), channel_id=1, source_target_pairs={{0,1},{1,0},{2,3},{3,2},{4,5},{5,4},{6,7},{7,6},{8,9},{9,8},{10,11... | collective-permute-start | bytes 6152 | tf_op jit(solution)/shard_map/ppermute | solution.py:23
  8.0 5.8 %copy-start.3 = (f32[1280]{0:T(1024)S(1)}, f32[1280]{0:T(1024)}, u32[]{:S(2)}) copy-start(f32[1280]{0:T(1024)} %param.9) | copy-start | bytes 15364
  8.0 7.0 %copy-start.1 = (bf16[512,1280]{1,0:T(8,128)(2,1)S(1)}, bf16[512,1280]{1,0:T(8,128)(2,1)}, u32[]{:S(2)}) copy-start(bf16[512,1280]{1,0:T(8,128)(2,1)} %param.6) | copy-start | bytes 3932164
  13.8 23.2 %collective-permute-start.6 = (f32[1280]{0:T(1024)S(1)}, f32[1280]{0:T(1024)S(1)}, u32[]{:S(2)}, u32[]{:S(2)}) collective-permute-start(f32[1280]{0:T(1024)S(1)} %copy-done.3), channel_id=1, source_target_pairs={{0,2},{1,3},{2,0},{3,1},{4,6},{5,7},{6,4},{7,5},{8,10},{9,11},{10,... | collective-permute-start | bytes 15368 | tf_op jit(solution)/shard_map/ppermute | solution.py:23
  17.2 19.5 %copy-start.2 = (f32[2,256]{1,0:T(2,128)S(1)}, f32[2,256]{1,0:T(2,128)}, u32[]{:S(2)}) copy-start(f32[2,256]{1,0:T(2,128)} %param.11) | copy-start | bytes 6148
  35.7 4.1 %collective-permute-start.7 = (bf16[512,1280]{1,0:T(8,128)(2,1)S(1)}, bf16[512,1280]{1,0:T(8,128)(2,1)}, u32[]{:S(2)}, u32[]{:S(2)}) collective-permute-start(bf16[512,1280]{1,0:T(8,128)(2,1)S(1)} %collective-permute-done.1), channel_id=1, source_target_pairs={{0,1},{1,0},{2,3},{3,2},{4,5},{5,4},{6,7},{7,6},{8,9},{9,8},{10,11... | collective-permute-start | bytes 3932168 | tf_op jit(solution)/shard_map/ppermute | solution.py:23
  37.0 2.9 %copy-start.4 = (f32[512,512]{1,0:T(8,128)S(1)}, f32[512,512]{1,0:T(8,128)}, u32[]{:S(2)}) copy-start(f32[512,512]{1,0:T(8,128)} %convolution_add_fusion) | copy-start | bytes 3145732
  37.0 2.8 %collective-permute-start.8 = (f32[1280]{0:T(1024)S(1)}, f32[1280]{0:T(1024)S(1)}, u32[]{:S(2)}, u32[]{:S(2)}) collective-permute-start(f32[1280]{0:T(1024)S(1)} %collective-permute-done.6), channel_id=1, source_target_pairs={{0,1},{1,0},{2,3},{3,2},{4,5},{5,4},{6,7},{7,6},{8,9},{9,8},{10,11... | collective-permute-start | bytes 15368 | tf_op jit(solution)/shard_map/ppermute | solution.py:23
  39.8 2.7 %copy-start = (bf16[512,1280]{1,0:T(8,128)(2,1)S(1)}, bf16[512,1280]{1,0:T(8,128)(2,1)}, u32[]{:S(2)}) copy-start(bf16[512,1280]{1,0:T(8,128)(2,1)} %q_ref.1) | copy-start | bytes 3932164

commit v4 on v1

--- a/solution.py
+++ b/solution.py
@@ -23,14 +23,19 @@
     return lax.ppermute(value, axis, [(source, source ^ bit) for source in range(count)])
 
 
-def ring_kernel(group, tok, scale, q_ref, kv_ref, qdoc_ref, kdoc_ref, o_ref,
-                recv, send_sem, recv_sem, m_ref, l_ref, acc_ref, bias_ref):
+def ring_kernel(group, scale, key_half, first, final, q_ref, kv_ref, qdoc_ref, kdoc_ref, *rest):
+    if first:
+        (out_m, out_l, out_acc, recv, send_sem, recv_sem, m_ref, l_ref, acc_ref, bias_ref) = rest
+    else:
+        (in_m, in_l, in_acc, o_ref, recv, send_sem, recv_sem, m_ref, l_ref, acc_ref, bias_ref) = rest
     c = lax.axis_index("ctx")
     t = lax.axis_index("tp")
     n = lax.axis_size("ctx")
+    tok = q_ref.shape[0]
+    keys_n = kv_ref.shape[0]
     heads = q_ref.shape[1] // HD
     kv_width = kv_ref.shape[1] // 2
-    half = tok // 2
+    key_base = key_half * keys_n
 
     barrier = pltpu.get_barrier_semaphore()
 
@@ -55,16 +60,25 @@
     def sends_at(step):
         return (c >= step) & (c < n - 1)
 
-    m_ref[...] = jnp.full(m_ref.shape, -1e30, jnp.float32)
-    l_ref[...] = jnp.zeros(l_ref.shape, jnp.float32)
-    acc_ref[...] = jnp.zeros(acc_ref.shape, jnp.float32)
+    @pl.when(c < n - 1)
+    def _():
+        copy_of(0).start()
+
+    if first:
+        m_ref[...] = jnp.full(m_ref.shape, -1e30, jnp.float32)
+        l_ref[...] = jnp.zeros(l_ref.shape, jnp.float32)
+        acc_ref[...] = jnp.zeros(acc_ref.shape, jnp.float32)
+    else:
+        m_ref[...] = in_m[...]
+        l_ref[...] = in_l[...]
+        acc_ref[...] = in_acc[...]
 
     def compute(b, kv, tiles):
         for r0, rr, c0, cc in tiles:
             same = qdoc_ref[r0:r0 + rr, :] == kdoc_ref[b:b + 1, c0:c0 + cc]
             if b == 0:
                 rows = lax.broadcasted_iota(jnp.int32, (rr, cc), 0) + r0
-                cols = lax.broadcasted_iota(jnp.int32, (rr, cc), 1) + c0
+                cols = lax.broadcasted_iota(jnp.int32, (rr, cc), 1) + (c0 + key_base)
                 same = same & (cols <= rows)
             bias_ref[r0:r0 + rr, c0:c0 + cc] = jnp.where(same, 0.0, -1e30)
 
@@ -93,16 +107,16 @@
 
         lax.fori_loop(0, heads, head, 0)
 
-    full = [(0, tok, 0, tok)]
-    lower = [(0, half, 0, half), (half, half, 0, tok)]
-    upper = [(0, half, 0, tok), (half, half, half, half)]
+    lead = tok - keys_n
+    if key_half == 0:
+        own = [(0, keys_n, 0, keys_n), (keys_n, lead, 0, keys_n)]
+        oldest = [(0, keys_n, 0, keys_n)]
+    else:
+        own = [(key_base, keys_n, 0, keys_n)]
+        oldest = [(0, tok, 0, keys_n)]
     nback = recv.shape[0]
 
-    @pl.when(c < n - 1)
-    def _():
-        copy_of(0).start()
-
-    compute(0, kv_ref, lower)
+    compute(0, kv_ref, own)
     for s in range(1, nback + 1):
         @pl.when(c >= s)
         def _():
@@ -115,72 +129,91 @@
 
         @pl.when(c >= s)
         def _():
-            compute(s, recv.at[s - 1], upper if s == nback else full)
+            compute(s, recv.at[s - 1], oldest if s == nback else [(0, tok, 0, keys_n)])
 
     for s in range(nback):
         @pl.when(sends_at(s))
         def _():
             copy_of(s).wait_send()
 
-    def finish(h, carry):
-        col = pl.multiple_of(h * HD, HD)
-        o_ref[:, pl.ds(col, HD)] = (acc_ref[h] / l_ref[h]).astype(o_ref.dtype)
-        return carry
-
-    lax.fori_loop(0, heads, finish, 0)
-
-
-def ring_attention(queries, kv_local, qdoc, kdoc, kv_heads):
+    if first:
+        out_m[...] = m_ref[...]
+        out_l[...] = l_ref[...]
+        out_acc[...] = acc_ref[...]
+    else:
+        def finish(h, carry):
+            col = pl.multiple_of(h * HD, HD)
+            o_ref[:, pl.ds(col, HD)] = (acc_ref[h] / l_ref[h]).astype(o_ref.dtype)
+            return carry
+
+        lax.fori_loop(0, heads, finish, 0)
+
+
+def ring_attention(queries, kv_half, qdoc, kdoc, kv_heads, key_half, state=None):
     tok, width = queries.shape
     group = width // HD // kv_heads
     heads = width // HD
+    first = state is None
     vmem = pltpu.VMEM
+    stat = jax.ShapeDtypeStruct((heads, tok, HD), jnp.float32)
+    if first:
+        out_shape = (stat, stat, stat)
+        out_specs = (pl.BlockSpec(memory_space=vmem),) * 3
+        operands = (queries, kv_half, qdoc, kdoc)
+    else:
+        out_shape = jax.ShapeDtypeStruct((tok, width), queries.dtype)
+        out_specs = pl.BlockSpec(memory_space=vmem)
+        operands = (queries, kv_half, qdoc, kdoc) + tuple(state)
     return pl.pallas_call(
-        functools.partial(ring_kernel, group, tok, HD ** (-0.5)),
-        out_shape=jax.ShapeDtypeStruct((tok, width), queries.dtype),
-        in_specs=[pl.BlockSpec(memory_space=vmem)] * 4,
-        out_specs=pl.BlockSpec(memory_space=vmem),
+        functools.partial(ring_kernel, group, HD ** (-0.5), key_half, first, not first),
+        out_shape=out_shape,
+        in_specs=[pl.BlockSpec(memory_space=vmem)] * len(operands),
+        out_specs=out_specs,
         scratch_shapes=[
-            vmem((CYCLE, tok, kv_local.shape[1]), kv_local.dtype),
+            vmem((CYCLE,) + kv_half.shape, kv_half.dtype),
             pltpu.SemaphoreType.DMA((CYCLE,)),
             pltpu.SemaphoreType.DMA((CYCLE,)),
             vmem((heads, tok, HD), jnp.float32),
             vmem((heads, tok, HD), jnp.float32),
             vmem((heads, tok, HD), jnp.float32),
-            vmem((tok, tok), jnp.float32),
+            vmem((tok, kv_half.shape[0]), jnp.float32),
         ],
         compiler_params=pltpu.CompilerParams(
-            collective_id=0, has_side_effects=True, vmem_limit_bytes=48 * 1024 * 1024),
-    )(queries, kv_local, qdoc, kdoc)
+            collective_id=key_half, has_side_effects=True, vmem_limit_bytes=56 * 1024 * 1024),
+    )(*operands)
 
 
 def body(hidden, queries, lengths, norm_gain, kv_weight, kv_bias):
     tok, width = hidden.shape
     tpi = lax.axis_index("tp")
-    across = flipped(hidden, "tp", 2)
-    pair = flipped(jnp.stack([hidden, across]), "tp", 1)
+    own_squares = jnp.sum(jnp.square(hidden.astype(jnp.float32)), axis=1)
+    squares_across = flipped(own_squares, "tp", 2)
+    squares_beside = flipped(own_squares, "tp", 1)
+    squares_diagonal = flipped(squares_across, "tp", 1)
+    squares = own_squares + squares_beside + squares_across + squares_diagonal
+    scale_rows = lax.rsqrt(squares / D + 1e-06)
+    half = tok // 2
+    sending, _ = lax.optimization_barrier((hidden[:half], squares_across))
+    across_a = flipped(sending, "tp", 2)
+    beside = flipped(hidden, "tp", 1)
     gain_across = flipped(norm_gain, "tp", 2)
-    gain_pair = flipped(jnp.stack([norm_gain, gain_across]), "tp", 1)
-    blocks = [
-        (hidden, norm_gain, tpi),
-        (across, gain_across, tpi ^ 2),
-        (pair[0], gain_pair[0], tpi ^ 1),
-        (pair[1], gain_pair[1], tpi ^ 3),
-    ]
-    squares = None
-    for part, _, _ in blocks:
-        xf = part.astype(jnp.float32)
-        term = jnp.sum(xf * xf, axis=1)
-        squares = term if squares is None else squares + term
-    scale_rows = lax.rsqrt(squares / D + 1e-06)
+    gain_beside = flipped(norm_gain, "tp", 1)
+    gain_diagonal = flipped(gain_across, "tp", 1)
     flat_weight = kv_weight.reshape(kv_weight.shape[0], -1)
-    summed = None
-    for part, gain, owner in blocks:
-        normed = (part.astype(jnp.float32) * scale_rows[:, None] * gain[None, :]).astype(jnp.bfloat16)
+    bias = kv_bias.reshape(-1)[None, :]
+
+    def project(part, gain, owner, scale):
+        normed = (part.astype(jnp.float32) * scale[:, None] * gain[None, :]).astype(jnp.bfloat16)
         rows = lax.dynamic_slice_in_dim(flat_weight, owner * width, width, 0)
-        term = jnp.dot(normed, rows, preferred_element_type=jnp.float32)
-        summed = term if summed is None else summed + term
-    kv_local = (summed + kv_bias.reshape(-1)[None, :]).astype(jnp.bfloat16)
+        return jnp.dot(normed, rows, preferred_element_type=jnp.float32)
+
+    summed = project(hidden, norm_gain, tpi, scale_rows) + project(beside, gain_beside, tpi ^ 1, scale_rows)
+    across_a, summed = lax.optimization_barrier((across_a, summed))
+    sending, _ = lax.optimization_barrier((hidden[half:], across_a))
+    across_b = flipped(sending, "tp", 2)
+    diagonal_a = flipped(across_a, "tp", 1)
+    kv_a = (summed[:half] + project(across_a, gain_across, tpi ^ 2, scale_rows[:half])
+            + project(diagonal_a, gain_diagonal, tpi ^ 3, scale_rows[:half]) + bias).astype(jnp.bfloat16)
     kv_heads = kv_weight.shape[2] // HD
 
     device = lax.axis_index("ctx")
@@ -190,9 +223,15 @@
     positions = starts[:, None] + jnp.arange(tok, dtype=jnp.int32)[None, :]
     found = jnp.sum((positions[:, :, None] >= ends[None, None, :]).astype(jnp.int32), axis=2)
     kdoc = jnp.where((device - backs >= 0)[:, None], found, -1)
-    qdoc = found[0]
+    qdoc = found[0][:, None]
     kdoc = jnp.concatenate([kdoc, jnp.full((8 - CYCLE - 1, tok), -1, jnp.int32)], axis=0)
-    return ring_attention(queries, kv_local, qdoc[:, None], kdoc, kv_heads)
+
+    state = ring_attention(queries, kv_a, qdoc, kdoc[:, :half], kv_heads, 0)
+    across_b, state = lax.optimization_barrier((across_b, state))
+    diagonal_b = flipped(across_b, "tp", 1)
+    kv_b = (summed[half:] + project(across_b, gain_across, tpi ^ 2, scale_rows[half:])
+            + project(diagonal_b, gain_diagonal, tpi ^ 3, scale_rows[half:]) + bias).astype(jnp.bfloat16)
+    return ring_attention(queries, kv_b, qdoc, kdoc[:, half:], kv_heads, 1, state)
 
 
 def solution(mesh):

time: 127 us -> 152 us (1.20)
  Pallas kernels: 70.4 us -> 110 us
  waiting for transfers between devices: 31.1 us -> 10.9 us
  matrix products: 7.78 us -> 13.4 us
  other arithmetic: 7.67 us -> 3.22 us
  starting transfers between devices: 1.75 us -> 4.8 us
  local copies, waits for them, and re-layouts: 7.66 us -> 9.91 us
    pallas_call x1 -> x2, Pallas kernels: 70.4 us -> 110 us  [ring_attention(): pl.pallas_call(functools.partial(ring_kernel, group, HD ** (-0.5), key_ha...]
    ppermute x4 -> x11, waiting for transfers between devices: 31.1 us -> 10.9 us  [flipped(): lax.ppermute(value, axis, [(source, source ^ bit) for source in range(cou...]
    dot_general x4 -> x6, matrix products: 7.78 us -> 13.4 us  [project(): return jnp.dot(normed, rows, preferred_element_type=jnp.float32)]
    another operation x5 -> x3, other arithmetic: 3.66 us -> 0.42 us  [the longest x1 3.23 us: body(): pair = flipped(jnp.stack([hidden, across]), 'tp', 1)]
    ppermute x4 -> x11, starting transfers between devices: 1.75 us -> 4.8 us  [flipped(): lax.ppermute(value, axis, [(source, source ^ bit) for source in range(cou...]
    unnamed x15 -> x19, local copies, waits for them, and re-layouts: 7.28 us -> 8.17 us
  transfers between devices with their start and end apart: 4 -> 11, of which waited for: 2 -> 2; matrix products, arithmetic and copies ran while one was open for 6% -> 14% of each run, Pallas kernels for 0% -> 37%
where the time goes in v4:
time: 152 us
  Pallas kernels  110 us (72%)
  matrix products  13.4 us (9%)
  waiting for transfers between devices  10.9 us (7%)
  local copies, waits for them, and re-layouts  9.91 us (7%)
  starting transfers between devices  4.8 us (3%)
  other arithmetic  3.22 us (2%)
    pallas_call x2, Pallas kernels, ring_attention(): pl.pallas_call(functools.partial(ring_kernel, group, HD ** (-0.5), key_ha...  110 us
    dot_general x6, matrix products, project(): return jnp.dot(normed, rows, preferred_element_type=jnp.float32)  13.4 us
    ppermute x11, waiting for transfers between devices, flipped(): lax.ppermute(value, axis, [(source, source ^ bit) for source in range(cou...  10.9 us
    unnamed x19, local copies, waits for them, and re-layouts  8.17 us
    ppermute x11, starting transfers between devices, flipped(): lax.ppermute(value, axis, [(source, source ^ bit) for source in range(cou...  4.8 us
  transfers between devices with their start and end apart: 11, of which 2 were waited for; matrix products, arithmetic and copies ran while one was open for 14% of the time, Pallas kernels for 37%

profile of v4, /device:TPU:6, one launch (start us, length us, event | category | flops | bytes accessed | tf_op | source)
XLA Modules:
  0.0 152.0 jit_solution(746196646436007077)
XLA Ops:
  0.0 1.7 %fusion = f32[512]{0:T(512)S(1)} fusion(bf16[512,1280]{1,0:T(8,128)(2,1)} %param.6), kind=kLoop, calls=%fused_computation.2 | loop fusion | flops 1965568 | bytes 1312768 | tf_op jit(solution)/shard_map/reduce_sum | solution.py:189
  1.8 0.1 collective-permute-start.2
  1.9 0.9 collective-permute-start
  2.8 1.2 collective-permute-start.7
  4.0 0.0 collective-permute-start.5
  4.0 0.0 copy-done
  4.0 0.5 collective-permute-start.4
  4.5 0.3 reduce-window.9
  4.8 0.1 slice.41
  4.9 0.1 slice_reduce_fusion
  5.0 0.1 add_bitcast_fusion
  5.1 0.1 iota_add_fusion
  5.2 0.9 convert_reduce_fusion
  6.1 0.1 fusion.53
  6.2 0.0 collective-permute-done
  6.2 0.1 collective-permute-start.3
  6.3 0.1 broadcast_select_fusion
  6.4 5.7 %copy.11 = bf16[640,8,2,256]{3,1,2,0:T(8,128)(2,1)} copy(bf16[640,8,2,256]{3,2,1,0:T(2,128)(2,1)} %bitcast.9) | data formatting | bytes 10485760
  12.0 0.0 collective-permute-done.2
  12.0 0.8 collective-permute-start.1
  12.9 0.0 collective-permute-done.3
  12.9 0.0 copy-done.3
  12.9 2.2 %fusion.3 = f32[512,512]{1,0:T(8,128)S(1)} fusion(bf16[512,1280]{1,0:T(8,128)(2,1)S(1)} %copy-done, bf16[5120,512]{1,0:T(8,128)(2,1)} %bitcast.10, s32[]{:T(128)S(6)} %select_n.18, f32[1280]{0:T(1024)S(1)} %copy-done.3, f32[512]{0:T(512)S(1)} %add_rsqrt_fusion), kind=kOutput, calls=%fused_computation.8 | convolution fusion | flops 673710080 | bytes 3677188 | tf_op jit(solution)/shard_map/dot_general | solution.py:208
  15.1 0.0 copy-start.1
  15.1 0.0 collective-permute-done.5
  15.1 0.0 collective-permute-done.4
  15.1 0.0 slice-start
  15.1 3.7 %convolution_add_fusion = f32[512,512]{1,0:T(8,128)} fusion(f32[512,512]{1,0:T(8,128)S(1)} %fusion.3, bf16[512,1280]{1,0:T(8,128)(2,1)} %collective-permute-done.4, bf16[5120,512]{1,0:T(8,128)(2,1)} %bitcast.11, s32[]{:T(128)S(6)} %select_n.19, f32[1280]{0:T(1024)S(1)} %collective-permute-done.5, f32[512]{0:T(512)S(1)} %add_rsqrt_fusion), kind=kOutput, calls=%fused_computation.7 | convolution fusion | flops 673972224 | bytes 4725764 | tf_op jit(solution)/shard_map/dot_general | solution.py:208
  18.8 10.4 %collective-permute-done.1 = bf16[256,1280]{1,0:T(8,128)(2,1)S(1)} collective-permute-done((bf16[256,1280]{1,0:T(8,128)(2,1)S(1)}, bf16[256,1280]{1,0:T(8,128)(2,1)S(1)}, u32[]{:S(2)}, u32[]{:S(2)}) %collective-permute-start.1) | collective-permute-done | bytes 655392 | tf_op jit(solution)/shard_map/ppermute | solution.py:23
  29.2 0.0 collective-permute-start.8
  29.2 0.9 copy.9.qdoc_ref
  30.0 0.6 pad_slice_fusion
  30.7 0.8 collective-permute-start.6
  31.5 0.0 collective-permute-done.7
  31.5 0.2 collective-permute-start.9
  31.7 2.0 %fusion.17 = f32[256,512]{1,0:T(8,128)S(1)} fusion(bf16[5120,512]{1,0:T(8,128)(2,1)} %bitcast.12, s32[]{:T(128)S(6)} %select_n.20, bf16[256,1280]{1,0:T(8,128)(2,1)S(1)} %collective-permute-done.1, f32[1280]{0:T(1024)S(1)} %collective-permute-done.7, f32[256]{0:T(256)S(1)} %get-tuple-element.32), kind=kOutput, calls=%fused_computation.25 | convolution fusion | flops 336855040 | bytes 2496516 | tf_op jit(solution)/shard_map/dot_general | solution.py:208
  33.7 0.0 collective-permute-done.9
  33.7 0.0 collective-permute-done.8
  33.8 2.6 %fusion.38.kv_ref = bf16[256,512]{1,0:T(8,128)(2,1)} fusion(bf16[5120,512]{1,0:T(8,128)(2,1)} %bitcast.13, s32[]{:T(128)S(6)} %select_n.21, bf16[256,1280]{1,0:T(8,128)(2,1)S(1)} %collective-permute-done.8, f32[1280]{0:T(1024)S(1)} %collective-permute-done.9, f32[256]{0:T(256)S(1)} %get-tuple-element.32, f32[256,512]{1,0:T(8,128)S(1)} %fusion.17, ...), kind=kOutput, calls=%fused_computation.36 | convolution fusion | flops 337379328 | bytes 3284996 | tf_op jit(solution)/shard_map/dot_general | solution.py:208
  36.3 55.6 %shard_map.64 = (f32[10,512,128]{2,1,0:T(8,128)}, f32[10,512,128]{2,1,0:T(8,128)}, f32[10,512,128]{2,1,0:T(8,128)}) custom-call(bf16[512,1280]{1,0:T(8,128)(2,1)} %q_ref.3, bf16[256,512]{1,0:T(8,128)(2,1)} %fusion.38.kv_ref, s32[512,1]{1,0:T(8,128)} %copy.9.qdoc_ref, s32[8,256]{1,0:T(8,128)} %get-tuple-element.30.kdoc_ref), custom_call_target="tpu_custom_call" | custom-call | tf_op jit(solution)/shard_map/pallas_call | solution.py:167
  91.9 0.0 collective-permute-done.6
  91.9 0.1 collective-permute-start.10
  92.0 0.0 copy-start.5
  92.0 1.7 %fusion.15 = f32[256,512]{1,0:T(8,128)S(1)} fusion(bf16[5120,512]{1,0:T(8,128)(2,1)S(1)} %bitcast.16, s32[]{:T(128)S(6)} %select_n.20, bf16[256,1280]{1,0:T(8,128)(2,1)} %collective-permute-done.6, f32[256]{0:T(256)S(1)} %get-tuple-element.31, f32[1280]{0:T(1024)S(1)} %collective-permute-done.7), kind=kOutput, calls=%fused_computation.23 | convolution fusion | flops 336855040 | bytes 2499588 | tf_op jit(solution)/shard_map/dot_general | solution.py:208
  93.8 0.5 collective-permute-done.10
  94.3 1.3 fusion.35.kv_ref
  95.6 54.0 %shard_map.65 = bf16[512,1280]{1,0:T(8,128)(2,1)} custom-call(bf16[512,1280]{1,0:T(8,128)(2,1)} %q_ref.3, bf16[256,512]{1,0:T(8,128)(2,1)} %fusion.35.kv_ref, s32[512,1]{1,0:T(8,128)} %copy.9.qdoc_ref, s32[8,256]{1,0:T(8,128)} %get-tuple-element.29.kdoc_ref, f32[10,512,128]{2,1,0:T(8,128)} %get-tuple-element.24.rest_0_, ...), custom_call_target="tpu_custom_call" | custom-call | tf_op jit(solution)/shard_map/pallas_call | solution.py:167
  149.6 2.5 %copy.14 = bf16[512,1280]{1,0:T(8,128)(2,1)} copy(bf16[512,1280]{1,0:T(8,128)(2,1)} %shard_map.65) | data formatting | bytes 2621440
  (19 shorter events, 0.1 us)
Async XLA Ops:
  0.0 4.0 %copy-start = (bf16[512,1280]{1,0:T(8,128)(2,1)S(1)}, bf16[512,1280]{1,0:T(8,128)(2,1)}, u32[]{:S(2)}) copy-start(bf16[512,1280]{1,0:T(8,128)(2,1)} %param.6) | copy-start | bytes 3932164
  0.0 4.5 %copy-start.2 = (s32[256]{0:T(256)S(1)}, s32[256]{0:T(256)}, u32[]{:S(2)}) copy-start(s32[256]{0:T(256)} %param.8) | copy-start | bytes 3076
  1.8 10.3 %collective-permute-start.2 = (f32[512]{0:T(512)S(1)}, f32[512]{0:T(512)S(1)}, u32[]{:S(2)}, u32[]{:S(2)}) collective-permute-start(f32[512]{0:T(512)S(1)} %fusion), channel_id=1, source_target_pairs={{0,1},{1,0},{2,3},{3,2},{4,5},{5,4},{6,7},{7,6},{8,9},{9,8},{10,11... | collective-permute-start | bytes 6152 | tf_op jit(solution)/shard_map/ppermute | solution.py:23
  1.9 4.3 %collective-permute-start = (f32[512]{0:T(512)S(1)}, f32[512]{0:T(512)S(1)}, u32[]{:S(2)}, u32[]{:S(2)}) collective-permute-start(f32[512]{0:T(512)S(1)} %fusion), channel_id=1, source_target_pairs={{0,2},{1,3},{2,0},{3,1},{4,6},{5,7},{6,4},{7,5},{8,10},{9,11},{10,... | collective-permute-start | bytes 6152 | tf_op jit(solution)/shard_map/ppermute | solution.py:23
  2.8 28.7 %collective-permute-start.7 = (f32[1280]{0:T(1024)}, f32[1280]{0:T(1024)S(1)}, u32[]{:S(2)}, u32[]{:S(2)}) collective-permute-start(f32[1280]{0:T(1024)} %param.9), channel_id=1, source_target_pairs={{0,2},{1,3},{2,0},{3,1},{4,6},{5,7},{6,4},{7,5},{8,10},{9,11},{10,... | collective-permute-start | bytes 15368 | tf_op jit(solution)/shard_map/ppermute | solution.py:23
  4.0 11.2 %collective-permute-start.5 = (f32[1280]{0:T(1024)}, f32[1280]{0:T(1024)S(1)}, u32[]{:S(2)}, u32[]{:S(2)}) collective-permute-start(f32[1280]{0:T(1024)} %param.9), channel_id=1, source_target_pairs={{0,1},{1,0},{2,3},{3,2},{4,5},{5,4},{6,7},{7,6},{8,9},{9,8},{10,11... | collective-permute-start | bytes 15368 | tf_op jit(solution)/shard_map/ppermute | solution.py:23
  4.0 11.2 %collective-permute-start.4 = (bf16[512,1280]{1,0:T(8,128)(2,1)S(1)}, bf16[512,1280]{1,0:T(8,128)(2,1)}, u32[]{:S(2)}, u32[]{:S(2)}) collective-permute-start(bf16[512,1280]{1,0:T(8,128)(2,1)S(1)} %copy-done), channel_id=1, source_target_pairs={{0,1},{1,0},{2,3},{3,2},{4,5},{5,4},{6,7},{7,6},{8,9},{9,8},{10,11... | collective-permute-start | bytes 3932168 | tf_op jit(solution)/shard_map/ppermute | solution.py:23
  6.2 6.7 %collective-permute-start.3 = (f32[512]{0:T(512)S(1)}, f32[512]{0:T(512)S(1)}, u32[]{:S(2)}, u32[]{:S(2)}) collective-permute-start(f32[512]{0:T(512)S(1)} %collective-permute-done), channel_id=1, source_target_pairs={{0,1},{1,0},{2,3},{3,2},{4,5},{5,4},{6,7},{7,6},{8,9},{9,8},{10,11... | collective-permute-start | bytes 6152 | tf_op jit(solution)/shard_map/ppermute | solution.py:23
  6.4 6.5 %copy-start.3 = (f32[1280]{0:T(1024)S(1)}, f32[1280]{0:T(1024)}, u32[]{:S(2)}) copy-start(f32[1280]{0:T(1024)} %param.9) | copy-start | bytes 15364
  12.0 17.1 %collective-permute-start.1 = (bf16[256,1280]{1,0:T(8,128)(2,1)S(1)}, bf16[256,1280]{1,0:T(8,128)(2,1)S(1)}, u32[]{:S(2)}, u32[]{:S(2)}) collective-permute-start(bf16[256,1280]{1,0:T(8,128)(2,1)S(1)} %get-tuple-element.16), channel_id=1, source_target_pairs={{0,2},{1,3},{2,0},{3,1},{4,6},{5,7},{6,4},{7,5},{8,10},{9,11},{10,... | collective-permute-start | bytes 1966088 | tf_op jit(solution)/shard_map/ppermute | solution.py:23
  15.1 14.1 %copy-start.1 = (f32[2,256]{1,0:T(2,128)S(1)}, f32[2,256]{1,0:T(2,128)}, u32[]{:S(2)}) copy-start(f32[2,256]{1,0:T(2,128)} %param.11) | copy-start | bytes 6148
  15.1 76.9 %slice-start = ((s8[5242880]{0:T(1024)(128)(4,1)}), s8[1048576]{0:T(1024)(128)(4,1)S(1)}, s32[]{:S(2)}) async-start(s8[5242880]{0:T(1024)(128)(4,1)} %bitcast.14), calls=%async_computation | async-start | bytes 2097152
  29.2 4.6 %collective-permute-start.8 = (bf16[256,1280]{1,0:T(8,128)(2,1)S(1)}, bf16[256,1280]{1,0:T(8,128)(2,1)S(1)}, u32[]{:S(2)}, u32[]{:S(2)}) collective-permute-start(bf16[256,1280]{1,0:T(8,128)(2,1)S(1)} %collective-permute-done.1), channel_id=1, source_target_pairs={{0,1},{1,0},{2,3},{3,2},{4,5},{5,4},{6,7},{7,6},{8,9},{9,8},{10,11... | collective-permute-start | bytes 1966088 | tf_op jit(solution)/shard_map/ppermute | solution.py:23
  30.0 3.7 %copy-start.4 = (f32[512,512]{1,0:T(8,128)S(1)}, f32[512,512]{1,0:T(8,128)}, u32[]{:S(2)}) copy-start(f32[512,512]{1,0:T(8,128)} %convolution_add_fusion) | copy-start | bytes 3145732
  30.7 61.2 %collective-permute-start.6 = (bf16[256,1280]{1,0:T(8,128)(2,1)S(1)}, bf16[256,1280]{1,0:T(8,128)(2,1)}, u32[]{:S(2)}, u32[]{:S(2)}) collective-permute-start(bf16[256,1280]{1,0:T(8,128)(2,1)S(1)} %get-tuple-element.19), channel_id=1, source_target_pairs={{0,2},{1,3},{2,0},{3,1},{4,6},{5,7},{6,4},{7,5},{8,10},{9,11},{10,... | collective-permute-start | bytes 1966088 | tf_op jit(solution)/shard_map/ppermute | solution.py:23
  31.5 2.2 %collective-permute-start.9 = (f32[1280]{0:T(1024)S(1)}, f32[1280]{0:T(1024)S(1)}, u32[]{:S(2)}, u32[]{:S(2)}) collective-permute-start(f32[1280]{0:T(1024)S(1)} %collective-permute-done.7), channel_id=1, source_target_pairs={{0,1},{1,0},{2,3},{3,2},{4,5},{5,4},{6,7},{7,6},{8,9},{9,8},{10,11... | collective-permute-start | bytes 15368 | tf_op jit(solution)/shard_map/ppermute | solution.py:23
  31.7 60.3 %slice-start.1 = ((s8[5242880]{0:T(1024)(128)(4,1)}), s8[4194304]{0:T(1024)(128)(4,1)S(1)}, s32[]{:S(2)}) async-start(s8[5242880]{0:T(1024)(128)(4,1)} %bitcast.14), calls=%async_computation.1 | async-start | bytes 8388608
  91.9 2.4 %collective-permute-start.10 = (bf16[256,1280]{1,0:T(8,128)(2,1)}, bf16[256,1280]{1,0:T(8,128)(2,1)S(1)}, u32[]{:S(2)}, u32[]{:S(2)}) collective-permute-start(bf16[256,1280]{1,0:T(8,128)(2,1)} %collective-permute-done.6), channel_id=1, source_target_pairs={{0,1},{1,0},{2,3},{3,2},{4,5},{5,4},{6,7},{7,6},{8,9},{9,8},{10,11... | collective-permute-start | bytes 1966088 | tf_op jit(solution)/shard_map/ppermute | solution.py:23
  92.0 2.3 %copy-start.5 = (f32[512,512]{1,0:T(8,128)S(1)}, f32[512,512]{1,0:T(8,128)}, u32[]{:S(2)}) copy-start(f32[512,512]{1,0:T(8,128)} %convolution_add_fusion) | copy-start | bytes 3145732

commit v5 on v3

--- a/solution.py
+++ b/solution.py
@@ -158,14 +158,13 @@
 def body(hidden, queries, lengths, norm_gain, kv_weight, kv_bias):
     tok, width = hidden.shape
     tpi = lax.axis_index("tp")
+    across = flipped(hidden, "tp", 2)
     own_squares = jnp.sum(jnp.square(hidden.astype(jnp.float32)), axis=1)
-    squares_across = flipped(own_squares, "tp", 2)
+    squares_diagonal = flipped(own_squares, "tp", 3)
     squares_beside = flipped(own_squares, "tp", 1)
-    squares_diagonal = flipped(squares_across, "tp", 1)
+    squares_across = flipped(squares_diagonal, "tp", 1)
     squares = own_squares + squares_beside + squares_across + squares_diagonal
     scale_rows = lax.rsqrt(squares / D + 1e-06)
-    sending, _ = lax.optimization_barrier((hidden, squares_across))
-    across = flipped(sending, "tp", 2)
     beside = flipped(hidden, "tp", 1)
     gain_across = flipped(norm_gain, "tp", 2)
     gain_beside = flipped(norm_gain, "tp", 1)
@@ -176,14 +175,6 @@
         normed = (part.astype(jnp.float32) * scale_rows[:, None] * gain[None, :]).astype(jnp.bfloat16)
         rows = lax.dynamic_slice_in_dim(flat_weight, owner * width, width, 0)
         return jnp.dot(normed, rows, preferred_element_type=jnp.float32)
-
-    summed = project(hidden, norm_gain, tpi) + project(beside, gain_beside, tpi ^ 1)
-    across, summed = lax.optimization_barrier((across, summed))
-    diagonal = flipped(across, "tp", 1)
-    summed = summed + project(across, gain_across, tpi ^ 2)
-    summed = summed + project(diagonal, gain_diagonal, tpi ^ 3)
-    kv_local = (summed + kv_bias.reshape(-1)[None, :]).astype(jnp.bfloat16)
-    kv_heads = kv_weight.shape[2] // HD
 
     device = lax.axis_index("ctx")
     ends = jnp.cumsum(lengths)
@@ -194,6 +185,15 @@
     kdoc = jnp.where((device - backs >= 0)[:, None], found, -1)
     qdoc = found[0]
     kdoc = jnp.concatenate([kdoc, jnp.full((8 - CYCLE - 1, tok), -1, jnp.int32)], axis=0)
+
+    summed = project(hidden, norm_gain, tpi) + project(beside, gain_beside, tpi ^ 1)
+    across, summed, qdoc, kdoc = lax.optimization_barrier((across, summed, qdoc, kdoc))
+    diagonal = flipped(across, "tp", 1)
+    summed = summed + project(across, gain_across, tpi ^ 2)
+    summed = summed + project(diagonal, gain_diagonal, tpi ^ 3)
+    kv_local = (summed + kv_bias.reshape(-1)[None, :]).astype(jnp.bfloat16)
+    kv_heads = kv_weight.shape[2] // HD
+
     return ring_attention(queries, kv_local, qdoc[:, None], kdoc, kv_heads)
 
 

time: 111 us -> 114 us (1.027)
  matrix products: 10.7 us -> 12.3 us
  Pallas kernels: 67.2 us -> 68.7 us
    dot_general x4, matrix products: 10.7 us -> 12.3 us  [project(): return jnp.dot(normed, rows, preferred_element_type=jnp.float32)]
    pallas_call x1, Pallas kernels: 67.2 us -> 68.7 us  [ring_attention(): pl.pallas_call(functools.partial(ring_kernel, group, tok, HD ** (-0.5)),...]
  transfers between devices with their start and end apart: 9 -> 9, of which waited for: 2 -> 2; matrix products, arithmetic and copies ran while one was open for 16% -> 15% of each run, Pallas kernels for 0% -> 0%
where the time goes in v5:
time: 114 us
  Pallas kernels  68.7 us (60%)
  waiting for transfers between devices  18 us (16%)
  matrix products  12.3 us (11%)
  local copies, waits for them, and re-layouts  7.2 us (6%)
  starting transfers between devices  4.03 us (4%)
  other arithmetic  3.79 us (3%)
    pallas_call x1, Pallas kernels, ring_attention(): pl.pallas_call(functools.partial(ring_kernel, group, tok, HD ** (-0.5)),...  68.7 us
    ppermute x9, waiting for transfers between devices, flipped(): lax.ppermute(value, axis, [(source, source ^ bit) for source in range(cou...  18 us
    dot_general x4, matrix products, project(): return jnp.dot(normed, rows, preferred_element_type=jnp.float32)  12.3 us
    unnamed x13, local copies, waits for them, and re-layouts  6.85 us
    ppermute x9, starting transfers between devices, flipped(): lax.ppermute(value, axis, [(source, source ^ bit) for source in range(cou...  4.03 us
  transfers between devices with their start and end apart: 9, of which 2 were waited for; matrix products, arithmetic and copies ran while one was open for 15% of the time, Pallas kernels for 0%

profile of v5, /device:TPU:6, one launch (start us, length us, event | category | flops | bytes accessed | tf_op | source)
XLA Modules:
  0.0 114.2 jit_solution(872544002659632215)
XLA Ops:
  0.0 1.6 %fusion = f32[512]{0:T(512)S(1)} fusion(bf16[512,1280]{1,0:T(8,128)(2,1)} %param.6), kind=kLoop, calls=%fused_computation.2 | loop fusion | flops 1965568 | bytes 1312768 | tf_op jit(solution)/shard_map/reduce_sum | solution.py:162
  1.6 0.4 collective-permute-start.2
  2.0 0.7 collective-permute-start.1
  2.7 0.0 collective-permute-start.4
  2.7 1.2 %collective-permute-start = (bf16[512,1280]{1,0:T(8,128)(2,1)}, bf16[512,1280]{1,0:T(8,128)(2,1)S(1)}, u32[]{:S(2)}, u32[]{:S(2)}) collective-permute-start(bf16[512,1280]{1,0:T(8,128)(2,1)} %param.6), channel_id=1, source_target_pairs={{0,2},{1,3},{2,0},{3,1},{4,6},{5,7},{6,4},{7,5},{8,10},{9,11},{10,... | collective-permute-start | bytes 3932168 | tf_op jit(solution)/shard_map/ppermute | solution.py:23
  3.9 0.2 collective-permute-start.5
  4.1 0.1 iota_add_fusion
  4.2 1.0 reduce-window.9
  5.2 0.1 slice.10
  5.3 0.1 slice_reduce_fusion
  5.4 0.1 add_bitcast_fusion
  5.5 0.9 convert_reduce_fusion
  6.4 0.0 copy-start.2
  6.4 0.0 collective-permute-done.2
  6.4 0.4 collective-permute-start.3
  6.8 0.1 broadcast_select_fusion
  6.8 0.0 copy-start.1
  6.8 0.0 copy-start.4
  6.8 5.8 %copy.9 = bf16[640,8,2,256]{3,1,2,0:T(8,128)(2,1)} copy(bf16[640,8,2,256]{3,2,1,0:T(2,128)(2,1)} %bitcast.9) | data formatting | bytes 10485760
  12.6 0.0 copy-done.2
  12.6 0.0 collective-permute-done.1
  12.6 0.0 collective-permute-done.3
  12.6 0.0 copy-done.1
  12.7 0.0 copy-done.4
  12.7 2.2 %fusion.5 = f32[512,512]{1,0:T(8,128)S(1)} fusion(bf16[512,1280]{1,0:T(8,128)(2,1)S(1)} %copy-done.1, bf16[5120,512]{1,0:T(8,128)(2,1)} %bitcast.10, s32[]{:T(128)S(6)} %select_n.16, f32[1280]{0:T(1024)S(1)} %copy-done.4, f32[512]{0:T(512)S(1)} %add_rsqrt_fusion), kind=kOutput, calls=%fused_computation.12 | convolution fusion | flops 673710080 | bytes 3677188 | tf_op jit(solution)/shard_map/dot_general | solution.py:177
  14.9 0.0 copy-start.3
  14.9 0.0 collective-permute-done.5
  14.9 0.0 collective-permute-done.4
  14.9 3.6 %convolution_add_fusion = f32[512,512]{1,0:T(8,128)} fusion(f32[512,512]{1,0:T(8,128)S(1)} %fusion.5, bf16[512,1280]{1,0:T(8,128)(2,1)} %collective-permute-done.4, bf16[5120,512]{1,0:T(8,128)(2,1)} %bitcast.11, s32[]{:T(128)S(6)} %select_n.17, f32[1280]{0:T(1024)S(1)} %collective-permute-done.5, f32[512]{0:T(512)S(1)} %add_rsqrt_fusion), kind=kOutput, calls=%fused_computation.9 | convolution fusion | flops 673972224 | bytes 4725764 | tf_op jit(solution)/shard_map/dot_general | solution.py:177
  18.5 15.6 %collective-permute-done = bf16[512,1280]{1,0:T(8,128)(2,1)S(1)} collective-permute-done((bf16[512,1280]{1,0:T(8,128)(2,1)}, bf16[512,1280]{1,0:T(8,128)(2,1)S(1)}, u32[]{:S(2)}, u32[]{:S(2)}) %collective-permute-start) | collective-permute-done | bytes 1310752 | tf_op jit(solution)/shard_map/ppermute | solution.py:23
  34.1 0.0 collective-permute-start.7
  34.1 1.2 %collective-permute-start.6 = (f32[1280]{0:T(1024)S(1)}, f32[1280]{0:T(1024)S(1)}, u32[]{:S(2)}, u32[]{:S(2)}) collective-permute-start(f32[1280]{0:T(1024)S(1)} %copy-done.4), channel_id=1, source_target_pairs={{0,2},{1,3},{2,0},{3,1},{4,6},{5,7},{6,4},{7,5},{8,10},{9,11},{10,... | collective-permute-start | bytes 15368 | tf_op jit(solution)/shard_map/ppermute | solution.py:23
  35.3 0.0 copy-done.3
  35.3 0.0 slice-start
  35.3 2.4 %collective-permute-done.6 = f32[1280]{0:T(1024)S(1)} collective-permute-done((f32[1280]{0:T(1024)S(1)}, f32[1280]{0:T(1024)S(1)}, u32[]{:S(2)}, u32[]{:S(2)}) %collective-permute-start.6) | collective-permute-done | bytes 5152 | tf_op jit(solution)/shard_map/ppermute | solution.py:23
  37.7 0.0 collective-permute-start.8
  37.7 3.2 %fusion.3 = f32[512,512]{1,0:T(8,128)} fusion(bf16[512,1280]{1,0:T(8,128)(2,1)S(1)} %collective-permute-done, bf16[5120,512]{1,0:T(8,128)(2,1)} %bitcast.12, s32[]{:T(128)S(6)} %select_n.19, f32[1280]{0:T(1024)S(1)} %collective-permute-done.6, f32[512]{0:T(512)S(1)} %add_rsqrt_fusion), kind=kOutput, calls=%fused_computation.10 | convolution fusion | flops 673710080 | bytes 3677188 | tf_op jit(solution)/shard_map/dot_general | solution.py:177
  40.9 0.0 slice-done
  40.9 0.1 copy.8.qdoc_ref
  41.1 0.0 collective-permute-done.8
  41.1 0.0 collective-permute-done.7
  41.1 0.0 copy-start
  41.1 3.3 %fusion.25.kv_ref = bf16[512,512]{1,0:T(8,128)(2,1)S(1)} fusion(bf16[5120,512]{1,0:T(8,128)(2,1)} %bitcast.13, s32[]{:T(128)S(6)} %select_n.20, bf16[512,1280]{1,0:T(8,128)(2,1)} %collective-permute-done.7, f32[1280]{0:T(1024)S(1)} %collective-permute-done.8, f32[512]{0:T(512)S(1)} %add_rsqrt_fusion, f32[512,512]{1,0:T(8,128)} %convolution_add_fusion, ...), kind=kOutput, calls=%fused_computation.27 | convolution fusion | flops 674758656 | bytes 5252100 | tf_op jit(solution)/shard_map/dot_general | solution.py:177
  44.5 0.0 copy-done
  44.5 68.7 %shard_map.64 = bf16[512,1280]{1,0:T(8,128)(2,1)S(1)} custom-call(bf16[512,1280]{1,0:T(8,128)(2,1)S(1)} %copy-done, bf16[512,512]{1,0:T(8,128)(2,1)S(1)} %fusion.25.kv_ref, s32[512,1]{1,0:T(8,128)S(1)} %copy.8.qdoc_ref, s32[8,512]{1,0:T(8,128)S(1)} %concatenate.3.kdoc_ref), custom_call_target="tpu_custom_call" | custom-call | tf_op jit(solution)/shard_map/pallas_call | solution.py:139
  113.2 1.1 copy.12
  (6 shorter events, 0.1 us)
Async XLA Ops:
  1.6 4.7 %collective-permute-start.2 = (f32[512]{0:T(512)S(1)}, f32[512]{0:T(512)S(1)}, u32[]{:S(2)}, u32[]{:S(2)}) collective-permute-start(f32[512]{0:T(512)S(1)} %fusion), channel_id=1, source_target_pairs={{0,3},{1,2},{2,1},{3,0},{4,7},{5,6},{6,5},{7,4},{8,11},{9,10},{10,... | collective-permute-start | bytes 6152 | tf_op jit(solution)/shard_map/ppermute | solution.py:23
  2.0 10.6 %collective-permute-start.1 = (f32[512]{0:T(512)S(1)}, f32[512]{0:T(512)S(1)}, u32[]{:S(2)}, u32[]{:S(2)}) collective-permute-start(f32[512]{0:T(512)S(1)} %fusion), channel_id=1, source_target_pairs={{0,1},{1,0},{2,3},{3,2},{4,5},{5,4},{6,7},{7,6},{8,9},{9,8},{10,11... | collective-permute-start | bytes 6152 | tf_op jit(solution)/shard_map/ppermute | solution.py:23
  2.7 12.2 %collective-permute-start.4 = (bf16[512,1280]{1,0:T(8,128)(2,1)}, bf16[512,1280]{1,0:T(8,128)(2,1)}, u32[]{:S(2)}, u32[]{:S(2)}) collective-permute-start(bf16[512,1280]{1,0:T(8,128)(2,1)} %param.6), channel_id=1, source_target_pairs={{0,1},{1,0},{2,3},{3,2},{4,5},{5,4},{6,7},{7,6},{8,9},{9,8},{10,11... | collective-permute-start | bytes 3932168 | tf_op jit(solution)/shard_map/ppermute | solution.py:23
  2.7 31.4 %collective-permute-start = (bf16[512,1280]{1,0:T(8,128)(2,1)}, bf16[512,1280]{1,0:T(8,128)(2,1)S(1)}, u32[]{:S(2)}, u32[]{:S(2)}) collective-permute-start(bf16[512,1280]{1,0:T(8,128)(2,1)} %param.6), channel_id=1, source_target_pairs={{0,2},{1,3},{2,0},{3,1},{4,6},{5,7},{6,4},{7,5},{8,10},{9,11},{10,... | collective-permute-start | bytes 3932168 | tf_op jit(solution)/shard_map/ppermute | solution.py:23
  3.9 11.0 %collective-permute-start.5 = (f32[1280]{0:T(1024)}, f32[1280]{0:T(1024)S(1)}, u32[]{:S(2)}, u32[]{:S(2)}) collective-permute-start(f32[1280]{0:T(1024)} %param.9), channel_id=1, source_target_pairs={{0,1},{1,0},{2,3},{3,2},{4,5},{5,4},{6,7},{7,6},{8,9},{9,8},{10,11... | collective-permute-start | bytes 15368 | tf_op jit(solution)/shard_map/ppermute | solution.py:23
  6.4 6.3 %copy-start.2 = (s32[5,512]{1,0:T(8,128)}, s32[5,512]{1,0:T(8,128)S(1)}, u32[]{:S(2)}) copy-start(s32[5,512]{1,0:T(8,128)S(1)} %convert_reduce_fusion) | copy-start | bytes 30724
  6.4 6.2 %collective-permute-start.3 = (f32[512]{0:T(512)S(1)}, f32[512]{0:T(512)S(1)}, u32[]{:S(2)}, u32[]{:S(2)}) collective-permute-start(f32[512]{0:T(512)S(1)} %collective-permute-done.2), channel_id=1, source_target_pairs={{0,1},{1,0},{2,3},{3,2},{4,5},{5,4},{6,7},{7,6},{8,9},{9,8},{10,11... | collective-permute-start | bytes 6152 | tf_op jit(solution)/shard_map/ppermute | solution.py:23
  6.8 5.8 %copy-start.1 = (bf16[512,1280]{1,0:T(8,128)(2,1)S(1)}, bf16[512,1280]{1,0:T(8,128)(2,1)}, u32[]{:S(2)}) copy-start(bf16[512,1280]{1,0:T(8,128)(2,1)} %param.6) | copy-start | bytes 3932164
  6.8 5.8 %copy-start.4 = (f32[1280]{0:T(1024)S(1)}, f32[1280]{0:T(1024)}, u32[]{:S(2)}) copy-start(f32[1280]{0:T(1024)} %param.9) | copy-start | bytes 15364
  14.9 20.4 %copy-start.3 = (f32[2,256]{1,0:T(2,128)S(1)}, f32[2,256]{1,0:T(2,128)}, u32[]{:S(2)}) copy-start(f32[2,256]{1,0:T(2,128)} %param.11) | copy-start | bytes 6148
  34.1 7.0 %collective-permute-start.7 = (bf16[512,1280]{1,0:T(8,128)(2,1)S(1)}, bf16[512,1280]{1,0:T(8,128)(2,1)}, u32[]{:S(2)}, u32[]{:S(2)}) collective-permute-start(bf16[512,1280]{1,0:T(8,128)(2,1)S(1)} %collective-permute-done), channel_id=1, source_target_pairs={{0,1},{1,0},{2,3},{3,2},{4,5},{5,4},{6,7},{7,6},{8,9},{9,8},{10,11... | collective-permute-start | bytes 3932168 | tf_op jit(solution)/shard_map/ppermute | solution.py:23
  34.1 3.7 %collective-permute-start.6 = (f32[1280]{0:T(1024)S(1)}, f32[1280]{0:T(1024)S(1)}, u32[]{:S(2)}, u32[]{:S(2)}) collective-permute-start(f32[1280]{0:T(1024)S(1)} %copy-done.4), channel_id=1, source_target_pairs={{0,2},{1,3},{2,0},{3,1},{4,6},{5,7},{6,4},{7,5},{8,10},{9,11},{10,... | collective-permute-start | bytes 15368 | tf_op jit(solution)/shard_map/ppermute | solution.py:23
  35.3 5.7 %slice-start = ((s32[5,512]{1,0:T(8,128)}), s32[1,512]{1,0:T(1,128)S(1)}, s32[]{:S(2)}) async-start(s32[5,512]{1,0:T(8,128)} %copy-done.2), calls=%async_computation | async-start | bytes 4096 | tf_op jit(solution)/shard_map/slice | solution.py:186
  37.7 3.4 %collective-permute-start.8 = (f32[1280]{0:T(1024)S(1)}, f32[1280]{0:T(1024)S(1)}, u32[]{:S(2)}, u32[]{:S(2)}) collective-permute-start(f32[1280]{0:T(1024)S(1)} %collective-permute-done.6), channel_id=1, source_target_pairs={{0,1},{1,0},{2,3},{3,2},{4,5},{5,4},{6,7},{7,6},{8,9},{9,8},{10,11... | collective-permute-start | bytes 15368 | tf_op jit(solution)/shard_map/ppermute | solution.py:23
  41.1 3.4 %copy-start = (bf16[512,1280]{1,0:T(8,128)(2,1)S(1)}, bf16[512,1280]{1,0:T(8,128)(2,1)}, u32[]{:S(2)}) copy-start(bf16[512,1280]{1,0:T(8,128)(2,1)} %q_ref.1) | copy-start | bytes 3932164

commit v6 on v3

--- a/solution.py
+++ b/solution.py
@@ -55,11 +55,7 @@
     def sends_at(step):
         return (c >= step) & (c < n - 1)
 
-    m_ref[...] = jnp.full(m_ref.shape, -1e30, jnp.float32)
-    l_ref[...] = jnp.zeros(l_ref.shape, jnp.float32)
-    acc_ref[...] = jnp.zeros(acc_ref.shape, jnp.float32)
-
-    def compute(b, kv, tiles):
+    def compute(b, kv, tiles, finish=False):
         for r0, rr, c0, cc in tiles:
             same = qdoc_ref[r0:r0 + rr, :] == kdoc_ref[b:b + 1, c0:c0 + cc]
             if b == 0:
@@ -81,15 +77,24 @@
                     s = lax.dot_general(q, keys, (((1,), (1,)), ((), ())),
                                         preferred_element_type=jnp.float32) * scale
                     s = s + bias_ref[r0:r0 + rr, c0:c0 + cc]
-                    prev = m_ref[h, r0:r0 + rr, :]
                     top = jnp.max(s, axis=1, keepdims=True)
-                    best = jnp.maximum(prev, top)
-                    shrink = jnp.exp(prev - best)
-                    p = jnp.exp(s - best[:, :1])
-                    m_ref[h, r0:r0 + rr, :] = best
-                    l_ref[h, r0:r0 + rr, :] = l_ref[h, r0:r0 + rr, :] * shrink + jnp.sum(p, axis=1, keepdims=True)
-                    acc_ref[h, r0:r0 + rr, :] = acc_ref[h, r0:r0 + rr, :] * shrink + jnp.dot(
-                        p.astype(jnp.bfloat16), values, preferred_element_type=jnp.float32)
+                    if b == 0:
+                        p = jnp.exp(s - top)
+                        m_ref[h, r0:r0 + rr, :] = jnp.broadcast_to(top, (rr, HD))
+                        l_ref[h, r0:r0 + rr, :] = jnp.broadcast_to(jnp.sum(p, axis=1, keepdims=True), (rr, HD))
+                        acc_ref[h, r0:r0 + rr, :] = jnp.dot(
+                            p.astype(jnp.bfloat16), values, preferred_element_type=jnp.float32)
+                    else:
+                        prev = m_ref[h, r0:r0 + rr, :]
+                        best = jnp.maximum(prev, top)
+                        shrink = jnp.exp(prev - best)
+                        p = jnp.exp(s - best[:, :1])
+                        m_ref[h, r0:r0 + rr, :] = best
+                        l_ref[h, r0:r0 + rr, :] = l_ref[h, r0:r0 + rr, :] * shrink + jnp.sum(p, axis=1, keepdims=True)
+                        acc_ref[h, r0:r0 + rr, :] = acc_ref[h, r0:r0 + rr, :] * shrink + jnp.dot(
+                            p.astype(jnp.bfloat16), values, preferred_element_type=jnp.float32)
+                if finish:
+                    o_ref[:, pl.ds(qcol, HD)] = (acc_ref[h] / l_ref[h]).astype(o_ref.dtype)
             return carry
 
         lax.fori_loop(0, heads // group, pair_of_heads, 0)
@@ -116,7 +121,7 @@
 
         @pl.when(c >= s)
         def _():
-            compute(s, recv.at[s - 1], upper if s == nback else full)
+            compute(s, recv.at[s - 1], upper if s == nback else full, finish=s == nback)
 
     for s in range(nback):
         @pl.when(sends_at(s))
@@ -128,7 +133,9 @@
         o_ref[:, pl.ds(col, HD)] = (acc_ref[h] / l_ref[h]).astype(o_ref.dtype)
         return carry
 
-    lax.fori_loop(0, heads, finish, 0)
+    @pl.when(c < nback)
+    def _():
+        lax.fori_loop(0, heads, finish, 0)
 
 
 def ring_attention(queries, kv_local, qdoc, kdoc, kv_heads):

time: 111 us -> 110 us (level)
  no operation moved by 1% of the time
where the time goes in v6:
time: 110 us
  Pallas kernels  66.3 us (60%)
  waiting for transfers between devices  17.6 us (16%)
  matrix products  10.7 us (10%)
  local copies, waits for them, and re-layouts  7.21 us (7%)
  starting transfers between devices  4.13 us (4%)
  other arithmetic  3.78 us (3%)
    pallas_call x1, Pallas kernels, ring_attention(): pl.pallas_call(functools.partial(ring_kernel, group, tok, HD ** (-0.5)),...  66.3 us
    ppermute x9, waiting for transfers between devices, flipped(): lax.ppermute(value, axis, [(source, source ^ bit) for source in range(cou...  17.6 us
    dot_general x4, matrix products, project(): return jnp.dot(normed, rows, preferred_element_type=jnp.float32)  10.7 us
    unnamed x13, local copies, waits for them, and re-layouts  6.87 us
    ppermute x9, starting transfers between devices, flipped(): lax.ppermute(value, axis, [(source, source ^ bit) for source in range(cou...  4.13 us
  transfers between devices with their start and end apart: 9, of which 2 were waited for; matrix products, arithmetic and copies ran while one was open for 16% of the time, Pallas kernels for 0%

profile of v6, /device:TPU:6, one launch (start us, length us, event | category | flops | bytes accessed | tf_op | source)
XLA Modules:
  0.0 109.9 jit_solution(1281748430750600291)
XLA Ops:
  0.0 0.0 collective-permute-start.4
  0.0 1.6 %fusion = f32[512]{0:T(512)S(1)} fusion(bf16[512,1280]{1,0:T(8,128)(2,1)} %param.6), kind=kLoop, calls=%fused_computation.2 | loop fusion | flops 1965568 | bytes 1312768 | tf_op jit(solution)/shard_map/reduce_sum | solution.py:168
  1.6 0.9 collective-permute-start
  2.6 2.8 %collective-permute-done = f32[512]{0:T(512)S(1)} collective-permute-done((f32[512]{0:T(512)S(1)}, f32[512]{0:T(512)S(1)}, u32[]{:S(2)}, u32[]{:S(2)}) %collective-permute-start) | collective-permute-done | bytes 2080 | tf_op jit(solution)/shard_map/ppermute | solution.py:23
  5.3 0.8 collective-permute-start.1
  6.2 0.0 collective-permute-start.2
  6.2 0.5 collective-permute-start.5
  6.7 1.0 reduce-window.9
  7.6 0.1 slice.10
  7.8 0.1 slice_reduce_fusion
  7.9 0.1 collective-permute-start.3
  8.0 0.0 copy-start.3
  8.0 0.0 copy-start.1
  8.0 5.8 %copy.9 = bf16[640,8,2,256]{3,1,2,0:T(8,128)(2,1)} copy(bf16[640,8,2,256]{3,2,1,0:T(2,128)(2,1)} %bitcast.9) | data formatting | bytes 10485760
  13.8 0.0 collective-permute-done.2
  13.8 0.0 copy-done.3
  13.8 1.2 %collective-permute-start.6 = (f32[1280]{0:T(1024)S(1)}, f32[1280]{0:T(1024)S(1)}, u32[]{:S(2)}, u32[]{:S(2)}) collective-permute-start(f32[1280]{0:T(1024)S(1)} %copy-done.3), channel_id=1, source_target_pairs={{0,2},{1,3},{2,0},{3,1},{4,6},{5,7},{6,4},{7,5},{8,10},{9,11},{10,... | collective-permute-start | bytes 15368 | tf_op jit(solution)/shard_map/ppermute | solution.py:23
  15.0 0.0 collective-permute-done.3
  15.0 0.0 copy-done.1
  15.0 2.2 %fusion.5 = f32[512,512]{1,0:T(8,128)S(1)} fusion(bf16[512,1280]{1,0:T(8,128)(2,1)S(1)} %copy-done.1, bf16[5120,512]{1,0:T(8,128)(2,1)} %bitcast.10, s32[]{:T(128)S(6)} %select_n.16, f32[1280]{0:T(1024)S(1)} %copy-done.3, f32[512]{0:T(512)S(1)} %add_rsqrt_fusion), kind=kOutput, calls=%fused_computation.12 | convolution fusion | flops 673710080 | bytes 3677188 | tf_op jit(solution)/shard_map/dot_general | solution.py:185
  17.2 0.0 copy-start.2
  17.2 0.0 collective-permute-done.5
  17.3 0.0 collective-permute-done.4
  17.3 3.6 %convolution_add_fusion = f32[512,512]{1,0:T(8,128)} fusion(f32[512,512]{1,0:T(8,128)S(1)} %fusion.5, bf16[512,1280]{1,0:T(8,128)(2,1)} %collective-permute-done.4, bf16[5120,512]{1,0:T(8,128)(2,1)} %bitcast.11, s32[]{:T(128)S(6)} %select_n.17, f32[1280]{0:T(1024)S(1)} %collective-permute-done.5, f32[512]{0:T(512)S(1)} %add_rsqrt_fusion), kind=kOutput, calls=%fused_computation.9 | convolution fusion | flops 673972224 | bytes 4725764 | tf_op jit(solution)/shard_map/dot_general | solution.py:185
  20.8 14.8 %collective-permute-done.1 = bf16[512,1280]{1,0:T(8,128)(2,1)S(1)} collective-permute-done((bf16[512,1280]{1,0:T(8,128)(2,1)}, bf16[512,1280]{1,0:T(8,128)(2,1)S(1)}, u32[]{:S(2)}, u32[]{:S(2)}) %collective-permute-start.1) | collective-permute-done | bytes 1310752 | tf_op jit(solution)/shard_map/ppermute | solution.py:23
  35.7 0.0 collective-permute-start.7
  35.7 0.1 add_bitcast_fusion
  35.7 0.1 iota_add_fusion
  35.8 0.9 convert_reduce_fusion
  36.7 0.1 broadcast_select_fusion
  36.8 0.0 copy-done.2
  36.8 0.1 copy.8.qdoc_ref
  37.0 0.0 copy-start.4
  37.0 0.0 collective-permute-done.6
  37.0 0.6 collective-permute-start.8
  37.6 2.2 %fusion.3 = f32[512,512]{1,0:T(8,128)S(1)} fusion(bf16[512,1280]{1,0:T(8,128)(2,1)S(1)} %collective-permute-done.1, bf16[5120,512]{1,0:T(8,128)(2,1)} %bitcast.12, s32[]{:T(128)S(6)} %select_n.18, f32[1280]{0:T(1024)S(1)} %collective-permute-done.6, f32[512]{0:T(512)S(1)} %add_rsqrt_fusion), kind=kOutput, calls=%fused_computation.10 | convolution fusion | flops 673710080 | bytes 3677188 | tf_op jit(solution)/shard_map/dot_general | solution.py:185
  39.8 0.0 collective-permute-done.8
  39.8 0.0 collective-permute-done.7
  39.8 0.0 copy-done.4
  39.8 0.0 copy-start
  39.8 2.7 %fusion.25.kv_ref = bf16[512,512]{1,0:T(8,128)(2,1)S(1)} fusion(bf16[5120,512]{1,0:T(8,128)(2,1)} %bitcast.13, s32[]{:T(128)S(6)} %select_n.19, bf16[512,1280]{1,0:T(8,128)(2,1)} %collective-permute-done.7, f32[1280]{0:T(1024)S(1)} %collective-permute-done.8, f32[512]{0:T(512)S(1)} %add_rsqrt_fusion, f32[512,512]{1,0:T(8,128)S(1)} %copy-done.4, ...), kind=kOutput, calls=%fused_computation.27 | convolution fusion | flops 674758656 | bytes 5252100 | tf_op jit(solution)/shard_map/dot_general | solution.py:185
  42.6 0.0 copy-done
  42.6 66.3 %shard_map.64 = bf16[512,1280]{1,0:T(8,128)(2,1)S(1)} custom-call(bf16[512,1280]{1,0:T(8,128)(2,1)S(1)} %copy-done, bf16[512,512]{1,0:T(8,128)(2,1)S(1)} %fusion.25.kv_ref, s32[512,1]{1,0:T(8,128)S(1)} %copy.8.qdoc_ref, s32[8,512]{1,0:T(8,128)S(1)} %concatenate.3.kdoc_ref), custom_call_target="tpu_custom_call" | custom-call | tf_op jit(solution)/shard_map/pallas_call | solution.py:146
  108.8 1.1 copy.12
  (7 shorter events, 0.1 us)
Async XLA Ops:
  0.0 17.3 %collective-permute-start.4 = (bf16[512,1280]{1,0:T(8,128)(2,1)}, bf16[512,1280]{1,0:T(8,128)(2,1)}, u32[]{:S(2)}, u32[]{:S(2)}) collective-permute-start(bf16[512,1280]{1,0:T(8,128)(2,1)} %param.6), channel_id=1, source_target_pairs={{0,1},{1,0},{2,3},{3,2},{4,5},{5,4},{6,7},{7,6},{8,9},{9,8},{10,11... | collective-permute-start | bytes 3932168 | tf_op jit(solution)/shard_map/ppermute | solution.py:23
  1.6 3.7 %collective-permute-start = (f32[512]{0:T(512)S(1)}, f32[512]{0:T(512)S(1)}, u32[]{:S(2)}, u32[]{:S(2)}) collective-permute-start(f32[512]{0:T(512)S(1)} %fusion), channel_id=1, source_target_pairs={{0,2},{1,3},{2,0},{3,1},{4,6},{5,7},{6,4},{7,5},{8,10},{9,11},{10,... | collective-permute-start | bytes 6152 | tf_op jit(solution)/shard_map/ppermute | solution.py:23
  5.3 30.3 %collective-permute-start.1 = (bf16[512,1280]{1,0:T(8,128)(2,1)}, bf16[512,1280]{1,0:T(8,128)(2,1)S(1)}, u32[]{:S(2)}, u32[]{:S(2)}) collective-permute-start(bf16[512,1280]{1,0:T(8,128)(2,1)} %param.6), channel_id=1, source_target_pairs={{0,2},{1,3},{2,0},{3,1},{4,6},{5,7},{6,4},{7,5},{8,10},{9,11},{10,... | collective-permute-start | bytes 3932168 | tf_op jit(solution)/shard_map/ppermute | solution.py:23
  6.2 7.6 %collective-permute-start.2 = (f32[512]{0:T(512)S(1)}, f32[512]{0:T(512)S(1)}, u32[]{:S(2)}, u32[]{:S(2)}) collective-permute-start(f32[512]{0:T(512)S(1)} %fusion), channel_id=1, source_target_pairs={{0,1},{1,0},{2,3},{3,2},{4,5},{5,4},{6,7},{7,6},{8,9},{9,8},{10,11... | collective-permute-start | bytes 6152 | tf_op jit(solution)/shard_map/ppermute | solution.py:23
  6.2 11.1 %collective-permute-start.5 = (f32[1280]{0:T(1024)}, f32[1280]{0:T(1024)S(1)}, u32[]{:S(2)}, u32[]{:S(2)}) collective-permute-start(f32[1280]{0:T(1024)} %param.9), channel_id=1, source_target_pairs={{0,1},{1,0},{2,3},{3,2},{4,5},{5,4},{6,7},{7,6},{8,9},{9,8},{10,11... | collective-permute-start | bytes 15368 | tf_op jit(solution)/shard_map/ppermute | solution.py:23
  7.9 7.1 %collective-permute-start.3 = (f32[512]{0:T(512)S(1)}, f32[512]{0:T(512)S(1)}, u32[]{:S(2)}, u32[]{:S(2)}) collective-permute-start(f32[512]{0:T(512)S(1)} %collective-permute-done), channel_id=1, source_target_pairs={{0,1},{1,0},{2,3},{3,2},{4,5},{5,4},{6,7},{7,6},{8,9},{9,8},{10,11... | collective-permute-start | bytes 6152 | tf_op jit(solution)/shard_map/ppermute | solution.py:23
  8.0 5.8 %copy-start.3 = (f32[1280]{0:T(1024)S(1)}, f32[1280]{0:T(1024)}, u32[]{:S(2)}) copy-start(f32[1280]{0:T(1024)} %param.9) | copy-start | bytes 15364
  8.0 7.0 %copy-start.1 = (bf16[512,1280]{1,0:T(8,128)(2,1)S(1)}, bf16[512,1280]{1,0:T(8,128)(2,1)}, u32[]{:S(2)}) copy-start(bf16[512,1280]{1,0:T(8,128)(2,1)} %param.6) | copy-start | bytes 3932164
  13.8 23.2 %collective-permute-start.6 = (f32[1280]{0:T(1024)S(1)}, f32[1280]{0:T(1024)S(1)}, u32[]{:S(2)}, u32[]{:S(2)}) collective-permute-start(f32[1280]{0:T(1024)S(1)} %copy-done.3), channel_id=1, source_target_pairs={{0,2},{1,3},{2,0},{3,1},{4,6},{5,7},{6,4},{7,5},{8,10},{9,11},{10,... | collective-permute-start | bytes 15368 | tf_op jit(solution)/shard_map/ppermute | solution.py:23
  17.2 19.5 %copy-start.2 = (f32[2,256]{1,0:T(2,128)S(1)}, f32[2,256]{1,0:T(2,128)}, u32[]{:S(2)}) copy-start(f32[2,256]{1,0:T(2,128)} %param.11) | copy-start | bytes 6148
  35.7 4.1 %collective-permute-start.7 = (bf16[512,1280]{1,0:T(8,128)(2,1)S(1)}, bf16[512,1280]{1,0:T(8,128)(2,1)}, u32[]{:S(2)}, u32[]{:S(2)}) collective-permute-start(bf16[512,1280]{1,0:T(8,128)(2,1)S(1)} %collective-permute-done.1), channel_id=1, source_target_pairs={{0,1},{1,0},{2,3},{3,2},{4,5},{5,4},{6,7},{7,6},{8,9},{9,8},{10,11... | collective-permute-start | bytes 3932168 | tf_op jit(solution)/shard_map/ppermute | solution.py:23
  37.0 2.9 %copy-start.4 = (f32[512,512]{1,0:T(8,128)S(1)}, f32[512,512]{1,0:T(8,128)}, u32[]{:S(2)}) copy-start(f32[512,512]{1,0:T(8,128)} %convolution_add_fusion) | copy-start | bytes 3145732
  37.0 2.8 %collective-permute-start.8 = (f32[1280]{0:T(1024)S(1)}, f32[1280]{0:T(1024)S(1)}, u32[]{:S(2)}, u32[]{:S(2)}) collective-permute-start(f32[1280]{0:T(1024)S(1)} %collective-permute-done.6), channel_id=1, source_target_pairs={{0,1},{1,0},{2,3},{3,2},{4,5},{5,4},{6,7},{7,6},{8,9},{9,8},{10,11... | collective-permute-start | bytes 15368 | tf_op jit(solution)/shard_map/ppermute | solution.py:23
  39.8 2.7 %copy-start = (bf16[512,1280]{1,0:T(8,128)(2,1)S(1)}, bf16[512,1280]{1,0:T(8,128)(2,1)}, u32[]{:S(2)}) copy-start(bf16[512,1280]{1,0:T(8,128)(2,1)} %q_ref.1) | copy-start | bytes 3932164

commit v7 on v6

--- a/solution.py
+++ b/solution.py
@@ -171,24 +171,32 @@
     squares_diagonal = flipped(squares_across, "tp", 1)
     squares = own_squares + squares_beside + squares_across + squares_diagonal
     scale_rows = lax.rsqrt(squares / D + 1e-06)
-    sending, _ = lax.optimization_barrier((hidden, squares_across))
-    across = flipped(sending, "tp", 2)
+    half = tok // 2
+    sending, _ = lax.optimization_barrier((hidden[:half], squares_across))
+    across_a = flipped(sending, "tp", 2)
     beside = flipped(hidden, "tp", 1)
     gain_across = flipped(norm_gain, "tp", 2)
     gain_beside = flipped(norm_gain, "tp", 1)
     gain_diagonal = flipped(gain_across, "tp", 1)
     flat_weight = kv_weight.reshape(kv_weight.shape[0], -1)
 
-    def project(part, gain, owner):
-        normed = (part.astype(jnp.float32) * scale_rows[:, None] * gain[None, :]).astype(jnp.bfloat16)
+    def project(part, gain, owner, scale):
+        normed = (part.astype(jnp.float32) * scale[:, None] * gain[None, :]).astype(jnp.bfloat16)
         rows = lax.dynamic_slice_in_dim(flat_weight, owner * width, width, 0)
         return jnp.dot(normed, rows, preferred_element_type=jnp.float32)
 
-    summed = project(hidden, norm_gain, tpi) + project(beside, gain_beside, tpi ^ 1)
-    across, summed = lax.optimization_barrier((across, summed))
-    diagonal = flipped(across, "tp", 1)
-    summed = summed + project(across, gain_across, tpi ^ 2)
-    summed = summed + project(diagonal, gain_diagonal, tpi ^ 3)
+    summed = project(hidden, norm_gain, tpi, scale_rows) + project(beside, gain_beside, tpi ^ 1, scale_rows)
+    across_a, summed = lax.optimization_barrier((across_a, summed))
+    sending, _ = lax.optimization_barrier((hidden[half:], across_a))
+    across_b = flipped(sending, "tp", 2)
+    diagonal_a = flipped(across_a, "tp", 1)
+    kv_a = (summed[:half] + project(across_a, gain_across, tpi ^ 2, scale_rows[:half])
+            + project(diagonal_a, gain_diagonal, tpi ^ 3, scale_rows[:half]))
+    across_b, kv_a = lax.optimization_barrier((across_b, kv_a))
+    diagonal_b = flipped(across_b, "tp", 1)
+    kv_b = (summed[half:] + project(across_b, gain_across, tpi ^ 2, scale_rows[half:])
+            + project(diagonal_b, gain_diagonal, tpi ^ 3, scale_rows[half:]))
+    summed = jnp.concatenate([kv_a, kv_b], axis=0)
     kv_local = (summed + kv_bias.reshape(-1)[None, :]).astype(jnp.bfloat16)
     kv_heads = kv_weight.shape[2] // HD
 

time: 110 us -> 122 us (1.11)
  waiting for transfers between devices: 17.6 us -> 23.5 us
  matrix products: 10.7 us -> 12.7 us
  local copies, waits for them, and re-layouts: 7.21 us -> 8.87 us
  Pallas kernels: 66.3 us -> 67.9 us
    ppermute x9 -> x11, waiting for transfers between devices: 17.6 us -> 23.5 us  [flipped(): lax.ppermute(value, axis, [(source, source ^ bit) for source in range(cou...]
    dot_general x4 -> x6, matrix products: 10.7 us -> 12.7 us  [project(): return jnp.dot(normed, rows, preferred_element_type=jnp.float32)]
    pallas_call x1, Pallas kernels: 66.3 us -> 67.9 us  [ring_attention(): pl.pallas_call(functools.partial(ring_kernel, group, tok, HD ** (-0.5)),...]
    unnamed x13, local copies, waits for them, and re-layouts: 6.87 us -> 8.44 us
    ppermute x9 -> x11, starting transfers between devices: 4.13 us -> 4.9 us  [flipped(): lax.ppermute(value, axis, [(source, source ^ bit) for source in range(cou...]
  transfers between devices with their start and end apart: 9 -> 11, of which waited for: 2 -> 2; matrix products, arithmetic and copies ran while one was open for 16% -> 15% of each run, Pallas kernels for 0% -> 0%
where the time goes in v7:
time: 122 us; the launch traced here: 121 us
  Pallas kernels  67.9 us (56%)
  waiting for transfers between devices  23.5 us (19%)
  matrix products  12.7 us (10%)
  local copies, waits for them, and re-layouts  8.87 us (7%)
  starting transfers between devices  4.9 us (4%)
  other arithmetic  3.33 us (3%)
    pallas_call x1, Pallas kernels, ring_attention(): pl.pallas_call(functools.partial(ring_kernel, group, tok, HD ** (-0.5)),...  67.9 us
    ppermute x11, waiting for transfers between devices, flipped(): lax.ppermute(value, axis, [(source, source ^ bit) for source in range(cou...  23.5 us
    dot_general x6, matrix products, project(): return jnp.dot(normed, rows, preferred_element_type=jnp.float32)  12.7 us
    unnamed x13, local copies, waits for them, and re-layouts  8.44 us
    ppermute x11, starting transfers between devices, flipped(): lax.ppermute(value, axis, [(source, source ^ bit) for source in range(cou...  4.9 us
  transfers between devices with their start and end apart: 11, of which 2 were waited for; matrix products, arithmetic and copies ran while one was open for 15% of the time, Pallas kernels for 0%

profile of v7, /device:TPU:6, one launch (start us, length us, event | category | flops | bytes accessed | tf_op | source)
XLA Modules:
  0.0 121.4 jit_solution(1634153766750432037)
XLA Ops:
  0.0 1.7 %fusion = f32[512]{0:T(512)S(1)} fusion(bf16[512,1280]{1,0:T(8,128)(2,1)} %param.6), kind=kLoop, calls=%fused_computation.2 | loop fusion | flops 1965568 | bytes 1312768 | tf_op jit(solution)/shard_map/reduce_sum | solution.py:168
  1.8 0.9 collective-permute-start
  2.7 0.0 collective-permute-start.2
  2.7 0.0 copy-done.1
  2.7 0.5 collective-permute-start.4
  3.2 0.0 collective-permute-start.5
  3.2 1.2 collective-permute-start.7
  4.4 0.1 fusion.42
  4.5 0.1 iota_add_fusion
  4.5 0.5 copy-done.3
  5.1 0.3 reduce-window.9
  5.4 0.1 slice.36
  5.5 0.0 collective-permute-done
  5.5 0.3 collective-permute-start.3
  5.8 0.1 slice_reduce_fusion
  5.9 0.0 copy-start.4
  5.9 5.7 %copy.9 = bf16[640,8,2,256]{3,1,2,0:T(8,128)(2,1)} copy(bf16[640,8,2,256]{3,2,1,0:T(2,128)(2,1)} %bitcast.15) | data formatting | bytes 10485760
  11.6 0.0 collective-permute-done.2
  11.6 0.8 collective-permute-start.1
  12.4 0.0 collective-permute-done.3
  12.4 2.2 %fusion.3 = f32[512,512]{1,0:T(8,128)S(1)} fusion(bf16[512,1280]{1,0:T(8,128)(2,1)S(1)} %copy-done.1, bf16[5120,512]{1,0:T(8,128)(2,1)} %bitcast.9, s32[]{:T(128)S(6)} %select_n.18, f32[1280]{0:T(1024)S(1)} %copy-done.4, f32[512]{0:T(512)S(1)} %add_rsqrt_fusion), kind=kOutput, calls=%fused_computation.8 | convolution fusion | flops 673710080 | bytes 3677188 | tf_op jit(solution)/shard_map/dot_general | solution.py:186
  14.6 0.0 collective-permute-done.5
  14.7 0.0 collective-permute-done.4
  14.7 2.6 %convolution_add_fusion = f32[512,512]{1,0:T(8,128)S(1)} fusion(f32[512,512]{1,0:T(8,128)S(1)} %fusion.3, bf16[512,1280]{1,0:T(8,128)(2,1)} %collective-permute-done.4, bf16[5120,512]{1,0:T(8,128)(2,1)} %bitcast.10, s32[]{:T(128)S(6)} %select_n.19, f32[1280]{0:T(1024)S(1)} %collective-permute-done.5, f32[512]{0:T(512)S(1)} %add_rsqrt_fusion), kind=kOutput, calls=%fused_computation.7 | convolution fusion | flops 673972224 | bytes 4725764 | tf_op jit(solution)/shard_map/dot_general | solution.py:186
  17.3 11.3 %collective-permute-done.1 = bf16[256,1280]{1,0:T(8,128)(2,1)} collective-permute-done((bf16[256,1280]{1,0:T(8,128)(2,1)S(1)}, bf16[256,1280]{1,0:T(8,128)(2,1)}, u32[]{:S(2)}, u32[]{:S(2)}) %collective-permute-start.1) | collective-permute-done | bytes 655392 | tf_op jit(solution)/shard_map/ppermute | solution.py:23
  28.6 0.0 collective-permute-start.8
  28.6 0.1 add_bitcast_fusion
  28.7 0.9 convert_reduce_fusion
  29.6 0.9 collective-permute-start.6
  30.5 0.0 collective-permute-done.7
  30.5 0.2 collective-permute-start.9
  30.7 2.1 %fusion.17 = f32[256,512]{1,0:T(8,128)S(1)} fusion(bf16[5120,512]{1,0:T(8,128)(2,1)} %bitcast.11, s32[]{:T(128)S(6)} %select_n.20, bf16[256,1280]{1,0:T(8,128)(2,1)} %collective-permute-done.1, f32[1280]{0:T(1024)S(1)} %collective-permute-done.7, f32[256]{0:T(256)S(1)} %get-tuple-element.20), kind=kOutput, calls=%fused_computation.25 | convolution fusion | flops 336855040 | bytes 2496516 | tf_op jit(solution)/shard_map/dot_general | solution.py:186
  32.8 0.0 copy-start.2
  32.8 0.0 collective-permute-done.9
  32.8 0.0 collective-permute-done.8
  32.8 1.9 %fusion.24 = f32[256,512]{1,0:T(8,128)S(1)} fusion(bf16[5120,512]{1,0:T(8,128)(2,1)} %bitcast.12, s32[]{:T(128)S(6)} %select_n.21, bf16[256,1280]{1,0:T(8,128)(2,1)S(1)} %collective-permute-done.8, f32[1280]{0:T(1024)S(1)} %collective-permute-done.9, f32[256]{0:T(256)S(1)} %get-tuple-element.20, f32[256,512]{1,0:T(8,128)S(1)} %fusion.17, ...), kind=kOutput, calls=%fused_computation.33 | convolution fusion | flops 337117184 | bytes 3545092 | tf_op jit(solution)/shard_map/dot_general | solution.py:186
  34.7 12.2 %collective-permute-done.6 = bf16[256,1280]{1,0:T(8,128)(2,1)} collective-permute-done((bf16[256,1280]{1,0:T(8,128)(2,1)S(1)}, bf16[256,1280]{1,0:T(8,128)(2,1)}, u32[]{:S(2)}, u32[]{:S(2)}) %collective-permute-start.6) | collective-permute-done | bytes 655392 | tf_op jit(solution)/shard_map/ppermute | solution.py:23
  46.9 0.0 collective-permute-start.10
  46.9 0.1 copy.8.qdoc_ref
  47.1 0.1 broadcast_select_fusion
  47.2 2.1 %fusion.15 = f32[256,512]{1,0:T(8,128)S(1)} fusion(bf16[5120,512]{1,0:T(8,128)(2,1)} %bitcast.13, s32[]{:T(128)S(6)} %select_n.20, bf16[256,1280]{1,0:T(8,128)(2,1)} %collective-permute-done.6, f32[256]{0:T(256)S(1)} %get-tuple-element.19, f32[1280]{0:T(1024)S(1)} %collective-permute-done.7), kind=kOutput, calls=%fused_computation.23 | convolution fusion | flops 336855040 | bytes 2496516 | tf_op jit(solution)/shard_map/dot_general | solution.py:186
  49.3 0.0 collective-permute-done.10
  49.3 1.9 %fusion.27 = f32[256,512]{1,0:T(8,128)S(1)} fusion(bf16[5120,512]{1,0:T(8,128)(2,1)} %bitcast.14, s32[]{:T(128)S(6)} %select_n.21, bf16[256,1280]{1,0:T(8,128)(2,1)S(1)} %collective-permute-done.10, f32[256]{0:T(256)S(1)} %get-tuple-element.19, f32[1280]{0:T(1024)S(1)} %collective-permute-done.9, f32[256,512]{1,0:T(8,128)S(1)} %fusion.15, ...), kind=kOutput, calls=%fused_computation.34 | convolution fusion | flops 337117184 | bytes 3545092 | tf_op jit(solution)/shard_map/dot_general | solution.py:186
  51.1 0.0 copy-start
  51.2 0.1 fusion.19.kv_ref
  51.3 1.2 copy-done
  52.5 67.9 %shard_map.64 = bf16[512,1280]{1,0:T(8,128)(2,1)S(1)} custom-call(bf16[512,1280]{1,0:T(8,128)(2,1)S(1)} %copy-done, bf16[512,512]{1,0:T(8,128)(2,1)S(1)} %fusion.19.kv_ref, s32[512,1]{1,0:T(8,128)S(1)} %copy.8.qdoc_ref, s32[8,512]{1,0:T(8,128)S(1)} %concatenate.7.kdoc_ref), custom_call_target="tpu_custom_call" | custom-call | tf_op jit(solution)/shard_map/pallas_call | solution.py:146
  120.4 1.1 copy.12
  (12 shorter events, 0.1 us)
Async XLA Ops:
  0.0 2.7 %copy-start.1 = (bf16[512,1280]{1,0:T(8,128)(2,1)S(1)}, bf16[512,1280]{1,0:T(8,128)(2,1)}, u32[]{:S(2)}) copy-start(bf16[512,1280]{1,0:T(8,128)(2,1)} %param.6) | copy-start | bytes 3932164
  1.8 3.7 %collective-permute-start = (f32[512]{0:T(512)S(1)}, f32[512]{0:T(512)S(1)}, u32[]{:S(2)}, u32[]{:S(2)}) collective-permute-start(f32[512]{0:T(512)S(1)} %fusion), channel_id=1, source_target_pairs={{0,2},{1,3},{2,0},{3,1},{4,6},{5,7},{6,4},{7,5},{8,10},{9,11},{10,... | collective-permute-start | bytes 6152 | tf_op jit(solution)/shard_map/ppermute | solution.py:23
  2.7 8.9 %collective-permute-start.2 = (f32[512]{0:T(512)S(1)}, f32[512]{0:T(512)S(1)}, u32[]{:S(2)}, u32[]{:S(2)}) collective-permute-start(f32[512]{0:T(512)S(1)} %fusion), channel_id=1, source_target_pairs={{0,1},{1,0},{2,3},{3,2},{4,5},{5,4},{6,7},{7,6},{8,9},{9,8},{10,11... | collective-permute-start | bytes 6152 | tf_op jit(solution)/shard_map/ppermute | solution.py:23
  2.7 12.0 %collective-permute-start.4 = (bf16[512,1280]{1,0:T(8,128)(2,1)S(1)}, bf16[512,1280]{1,0:T(8,128)(2,1)}, u32[]{:S(2)}, u32[]{:S(2)}) collective-permute-start(bf16[512,1280]{1,0:T(8,128)(2,1)S(1)} %copy-done.1), channel_id=1, source_target_pairs={{0,1},{1,0},{2,3},{3,2},{4,5},{5,4},{6,7},{7,6},{8,9},{9,8},{10,11... | collective-permute-start | bytes 3932168 | tf_op jit(solution)/shard_map/ppermute | solution.py:23
  3.2 11.5 %collective-permute-start.5 = (f32[1280]{0:T(1024)}, f32[1280]{0:T(1024)S(1)}, u32[]{:S(2)}, u32[]{:S(2)}) collective-permute-start(f32[1280]{0:T(1024)} %param.9), channel_id=1, source_target_pairs={{0,1},{1,0},{2,3},{3,2},{4,5},{5,4},{6,7},{7,6},{8,9},{9,8},{10,11... | collective-permute-start | bytes 15368 | tf_op jit(solution)/shard_map/ppermute | solution.py:23
  3.2 27.3 %collective-permute-start.7 = (f32[1280]{0:T(1024)}, f32[1280]{0:T(1024)S(1)}, u32[]{:S(2)}, u32[]{:S(2)}) collective-permute-start(f32[1280]{0:T(1024)} %param.9), channel_id=1, source_target_pairs={{0,2},{1,3},{2,0},{3,1},{4,6},{5,7},{6,4},{7,5},{8,10},{9,11},{10,... | collective-permute-start | bytes 15368 | tf_op jit(solution)/shard_map/ppermute | solution.py:23
  4.4 0.7 copy-start.3
  5.5 6.9 %collective-permute-start.3 = (f32[512]{0:T(512)S(1)}, f32[512]{0:T(512)S(1)}, u32[]{:S(2)}, u32[]{:S(2)}) collective-permute-start(f32[512]{0:T(512)S(1)} %collective-permute-done), channel_id=1, source_target_pairs={{0,1},{1,0},{2,3},{3,2},{4,5},{5,4},{6,7},{7,6},{8,9},{9,8},{10,11... | collective-permute-start | bytes 6152 | tf_op jit(solution)/shard_map/ppermute | solution.py:23
  5.9 6.5 %copy-start.4 = (f32[1280]{0:T(1024)S(1)}, f32[1280]{0:T(1024)}, u32[]{:S(2)}) copy-start(f32[1280]{0:T(1024)} %param.9) | copy-start | bytes 15364
  11.6 17.0 %collective-permute-start.1 = (bf16[256,1280]{1,0:T(8,128)(2,1)S(1)}, bf16[256,1280]{1,0:T(8,128)(2,1)}, u32[]{:S(2)}, u32[]{:S(2)}) collective-permute-start(bf16[256,1280]{1,0:T(8,128)(2,1)S(1)} %get-tuple-element.11), channel_id=1, source_target_pairs={{0,2},{1,3},{2,0},{3,1},{4,6},{5,7},{6,4},{7,5},{8,10},{9,11},{10,... | collective-permute-start | bytes 1966088 | tf_op jit(solution)/shard_map/ppermute | solution.py:23
  28.6 4.2 %collective-permute-start.8 = (bf16[256,1280]{1,0:T(8,128)(2,1)}, bf16[256,1280]{1,0:T(8,128)(2,1)S(1)}, u32[]{:S(2)}, u32[]{:S(2)}) collective-permute-start(bf16[256,1280]{1,0:T(8,128)(2,1)} %collective-permute-done.1), channel_id=1, source_target_pairs={{0,1},{1,0},{2,3},{3,2},{4,5},{5,4},{6,7},{7,6},{8,9},{9,8},{10,11... | collective-permute-start | bytes 1966088 | tf_op jit(solution)/shard_map/ppermute | solution.py:23
  29.6 17.3 %collective-permute-start.6 = (bf16[256,1280]{1,0:T(8,128)(2,1)S(1)}, bf16[256,1280]{1,0:T(8,128)(2,1)}, u32[]{:S(2)}, u32[]{:S(2)}) collective-permute-start(bf16[256,1280]{1,0:T(8,128)(2,1)S(1)} %get-tuple-element.13), channel_id=1, source_target_pairs={{0,2},{1,3},{2,0},{3,1},{4,6},{5,7},{6,4},{7,5},{8,10},{9,11},{10,... | collective-permute-start | bytes 1966088 | tf_op jit(solution)/shard_map/ppermute | solution.py:23
  30.5 2.3 %collective-permute-start.9 = (f32[1280]{0:T(1024)S(1)}, f32[1280]{0:T(1024)S(1)}, u32[]{:S(2)}, u32[]{:S(2)}) collective-permute-start(f32[1280]{0:T(1024)S(1)} %collective-permute-done.7), channel_id=1, source_target_pairs={{0,1},{1,0},{2,3},{3,2},{4,5},{5,4},{6,7},{7,6},{8,9},{9,8},{10,11... | collective-permute-start | bytes 15368 | tf_op jit(solution)/shard_map/ppermute | solution.py:23
  32.8 14.1 %copy-start.2 = (f32[2,256]{1,0:T(2,128)S(1)}, f32[2,256]{1,0:T(2,128)}, u32[]{:S(2)}) copy-start(f32[2,256]{1,0:T(2,128)} %param.11) | copy-start | bytes 6148
  46.9 2.4 %collective-permute-start.10 = (bf16[256,1280]{1,0:T(8,128)(2,1)}, bf16[256,1280]{1,0:T(8,128)(2,1)S(1)}, u32[]{:S(2)}, u32[]{:S(2)}) collective-permute-start(bf16[256,1280]{1,0:T(8,128)(2,1)} %collective-permute-done.6), channel_id=1, source_target_pairs={{0,1},{1,0},{2,3},{3,2},{4,5},{5,4},{6,7},{7,6},{8,9},{9,8},{10,11... | collective-permute-start | bytes 1966088 | tf_op jit(solution)/shard_map/ppermute | solution.py:23
  51.1 1.3 %copy-start = (bf16[512,1280]{1,0:T(8,128)(2,1)S(1)}, bf16[512,1280]{1,0:T(8,128)(2,1)}, u32[]{:S(2)}) copy-start(bf16[512,1280]{1,0:T(8,128)(2,1)} %q_ref.1) | copy-start | bytes 3932164

commit v8 on v6

--- a/solution.py
+++ b/solution.py
@@ -45,11 +45,17 @@
     peers = (c > 0).astype(jnp.int32) + (c < n - 1).astype(jnp.int32)
     pl.semaphore_wait(barrier, peers)
 
-    def copy_of(step):
+    def copy_of(step, part=None):
         src = kv_ref if step == 0 else recv.at[step - 1]
+        dst = recv.at[step]
+        sem = step
+        if part is not None:
+            src = src.at[pl.ds(part * half, half)]
+            dst = dst.at[pl.ds(part * half, half)]
+            sem = step + part
         return pltpu.make_async_remote_copy(
-            src_ref=src, dst_ref=recv.at[step], send_sem=send_sem.at[step],
-            recv_sem=recv_sem.at[step], device_id=(c + 1, t),
+            src_ref=src, dst_ref=dst, send_sem=send_sem.at[sem],
+            recv_sem=recv_sem.at[sem], device_id=(c + 1, t),
             device_id_type=pl.DeviceIdType.MESH)
 
     def sends_at(step):
@@ -108,25 +114,37 @@
     def _():
         copy_of(0).start()
 
+    def parts_of(step):
+        return (0, 1) if step == nback - 1 else (None,)
+
     compute(0, kv_ref, lower)
     for s in range(1, nback + 1):
-        @pl.when(c >= s)
-        def _():
-            copy_of(s - 1).wait_recv()
-
         if s < nback:
+            @pl.when(c >= s)
+            def _():
+                copy_of(s - 1).wait_recv()
+
             @pl.when(sends_at(s))
             def _():
-                copy_of(s).start()
-
-        @pl.when(c >= s)
-        def _():
-            compute(s, recv.at[s - 1], upper if s == nback else full, finish=s == nback)
+                for part in parts_of(s):
+                    copy_of(s, part).start()
+
+            @pl.when(c >= s)
+            def _():
+                compute(s, recv.at[s - 1], full)
+        else:
+            @pl.when(c >= s)
+            def _():
+                copy_of(s - 1, 0).wait_recv()
+                compute(s, recv.at[s - 1], [(0, half, 0, half)])
+                copy_of(s - 1, 1).wait_recv()
+                compute(s, recv.at[s - 1], [(0, half, half, half), (half, half, half, half)], finish=True)
 
     for s in range(nback):
         @pl.when(sends_at(s))
         def _():
-            copy_of(s).wait_send()
+            for part in parts_of(s):
+                copy_of(s, part).wait_send()
 
     def finish(h, carry):
         col = pl.multiple_of(h * HD, HD)
@@ -150,8 +168,8 @@
         out_specs=pl.BlockSpec(memory_space=vmem),
         scratch_shapes=[
             vmem((CYCLE, tok, kv_local.shape[1]), kv_local.dtype),
-            pltpu.SemaphoreType.DMA((CYCLE,)),
-            pltpu.SemaphoreType.DMA((CYCLE,)),
+            pltpu.SemaphoreType.DMA((CYCLE + 1,)),
+            pltpu.SemaphoreType.DMA((CYCLE + 1,)),
             vmem((heads, tok, HD), jnp.float32),
             vmem((heads, tok, HD), jnp.float32),
             vmem((heads, tok, HD), jnp.float32),

time: 110 us -> 112 us (1.018)
  Pallas kernels: 66.3 us -> 68 us
    pallas_call x1, Pallas kernels: 66.3 us -> 68 us  [ring_attention(): pl.pallas_call(functools.partial(ring_kernel, group, tok, HD ** (-0.5)),...]
where the time goes in v8:
time: 112 us
  Pallas kernels  68 us (61%)
  waiting for transfers between devices  17.6 us (16%)
  matrix products  10.7 us (10%)
  local copies, waits for them, and re-layouts  7.21 us (6%)
  starting transfers between devices  4.13 us (4%)
  other arithmetic  3.78 us (3%)
    pallas_call x1, Pallas kernels, ring_attention(): pl.pallas_call(functools.partial(ring_kernel, group, tok, HD ** (-0.5)),...  68 us
    ppermute x9, waiting for transfers between devices, flipped(): lax.ppermute(value, axis, [(source, source ^ bit) for source in range(cou...  17.6 us
    dot_general x4, matrix products, project(): return jnp.dot(normed, rows, preferred_element_type=jnp.float32)  10.7 us
    unnamed x13, local copies, waits for them, and re-layouts  6.87 us
    ppermute x9, starting transfers between devices, flipped(): lax.ppermute(value, axis, [(source, source ^ bit) for source in range(cou...  4.13 us
  transfers between devices with their start and end apart: 9, of which 2 were waited for; matrix products, arithmetic and copies ran while one was open for 16% of the time, Pallas kernels for 0%

profile of v8, /device:TPU:6, one launch (start us, length us, event | category | flops | bytes accessed | tf_op | source)
XLA Modules:
  0.0 111.6 jit_solution(1435128306584624223)
XLA Ops:
  0.0 0.0 collective-permute-start.4
  0.0 1.6 %fusion = f32[512]{0:T(512)S(1)} fusion(bf16[512,1280]{1,0:T(8,128)(2,1)} %param.6), kind=kLoop, calls=%fused_computation.2 | loop fusion | flops 1965568 | bytes 1312768 | tf_op jit(solution)/shard_map/reduce_sum | solution.py:186
  1.6 0.9 collective-permute-start
  2.6 2.8 %collective-permute-done = f32[512]{0:T(512)S(1)} collective-permute-done((f32[512]{0:T(512)S(1)}, f32[512]{0:T(512)S(1)}, u32[]{:S(2)}, u32[]{:S(2)}) %collective-permute-start) | collective-permute-done | bytes 2080 | tf_op jit(solution)/shard_map/ppermute | solution.py:23
  5.3 0.8 collective-permute-start.1
  6.2 0.0 collective-permute-start.2
  6.2 0.5 collective-permute-start.5
  6.7 1.0 reduce-window.9
  7.6 0.1 slice.10
  7.8 0.1 slice_reduce_fusion
  7.9 0.1 collective-permute-start.3
  8.0 0.0 copy-start.3
  8.0 0.0 copy-start.1
  8.0 5.8 %copy.9 = bf16[640,8,2,256]{3,1,2,0:T(8,128)(2,1)} copy(bf16[640,8,2,256]{3,2,1,0:T(2,128)(2,1)} %bitcast.9) | data formatting | bytes 10485760
  13.8 0.0 collective-permute-done.2
  13.8 0.0 copy-done.3
  13.8 1.2 %collective-permute-start.6 = (f32[1280]{0:T(1024)S(1)}, f32[1280]{0:T(1024)S(1)}, u32[]{:S(2)}, u32[]{:S(2)}) collective-permute-start(f32[1280]{0:T(1024)S(1)} %copy-done.3), channel_id=1, source_target_pairs={{0,2},{1,3},{2,0},{3,1},{4,6},{5,7},{6,4},{7,5},{8,10},{9,11},{10,... | collective-permute-start | bytes 15368 | tf_op jit(solution)/shard_map/ppermute | solution.py:23
  15.0 0.0 collective-permute-done.3
  15.0 0.0 copy-done.1
  15.0 2.2 %fusion.5 = f32[512,512]{1,0:T(8,128)S(1)} fusion(bf16[512,1280]{1,0:T(8,128)(2,1)S(1)} %copy-done.1, bf16[5120,512]{1,0:T(8,128)(2,1)} %bitcast.10, s32[]{:T(128)S(6)} %select_n.16, f32[1280]{0:T(1024)S(1)} %copy-done.3, f32[512]{0:T(512)S(1)} %add_rsqrt_fusion), kind=kOutput, calls=%fused_computation.12 | convolution fusion | flops 673710080 | bytes 3677188 | tf_op jit(solution)/shard_map/dot_general | solution.py:203
  17.2 0.0 copy-start.2
  17.2 0.0 collective-permute-done.5
  17.3 0.0 collective-permute-done.4
  17.3 3.6 %convolution_add_fusion = f32[512,512]{1,0:T(8,128)} fusion(f32[512,512]{1,0:T(8,128)S(1)} %fusion.5, bf16[512,1280]{1,0:T(8,128)(2,1)} %collective-permute-done.4, bf16[5120,512]{1,0:T(8,128)(2,1)} %bitcast.11, s32[]{:T(128)S(6)} %select_n.17, f32[1280]{0:T(1024)S(1)} %collective-permute-done.5, f32[512]{0:T(512)S(1)} %add_rsqrt_fusion), kind=kOutput, calls=%fused_computation.9 | convolution fusion | flops 673972224 | bytes 4725764 | tf_op jit(solution)/shard_map/dot_general | solution.py:203
  20.8 14.8 %collective-permute-done.1 = bf16[512,1280]{1,0:T(8,128)(2,1)S(1)} collective-permute-done((bf16[512,1280]{1,0:T(8,128)(2,1)}, bf16[512,1280]{1,0:T(8,128)(2,1)S(1)}, u32[]{:S(2)}, u32[]{:S(2)}) %collective-permute-start.1) | collective-permute-done | bytes 1310752 | tf_op jit(solution)/shard_map/ppermute | solution.py:23
  35.7 0.0 collective-permute-start.7
  35.7 0.1 add_bitcast_fusion
  35.7 0.1 iota_add_fusion
  35.8 0.9 convert_reduce_fusion
  36.7 0.1 broadcast_select_fusion
  36.8 0.0 copy-done.2
  36.8 0.1 copy.8.qdoc_ref
  37.0 0.0 copy-start.4
  37.0 0.0 collective-permute-done.6
  37.0 0.6 collective-permute-start.8
  37.6 2.2 %fusion.3 = f32[512,512]{1,0:T(8,128)S(1)} fusion(bf16[512,1280]{1,0:T(8,128)(2,1)S(1)} %collective-permute-done.1, bf16[5120,512]{1,0:T(8,128)(2,1)} %bitcast.12, s32[]{:T(128)S(6)} %select_n.18, f32[1280]{0:T(1024)S(1)} %collective-permute-done.6, f32[512]{0:T(512)S(1)} %add_rsqrt_fusion), kind=kOutput, calls=%fused_computation.10 | convolution fusion | flops 673710080 | bytes 3677188 | tf_op jit(solution)/shard_map/dot_general | solution.py:203
  39.8 0.0 collective-permute-done.8
  39.8 0.0 collective-permute-done.7
  39.8 0.0 copy-done.4
  39.8 0.0 copy-start
  39.8 2.7 %fusion.25.kv_ref = bf16[512,512]{1,0:T(8,128)(2,1)S(1)} fusion(bf16[5120,512]{1,0:T(8,128)(2,1)} %bitcast.13, s32[]{:T(128)S(6)} %select_n.19, bf16[512,1280]{1,0:T(8,128)(2,1)} %collective-permute-done.7, f32[1280]{0:T(1024)S(1)} %collective-permute-done.8, f32[512]{0:T(512)S(1)} %add_rsqrt_fusion, f32[512,512]{1,0:T(8,128)S(1)} %copy-done.4, ...), kind=kOutput, calls=%fused_computation.27 | convolution fusion | flops 674758656 | bytes 5252100 | tf_op jit(solution)/shard_map/dot_general | solution.py:203
  42.6 0.0 copy-done
  42.6 68.0 %shard_map.64 = bf16[512,1280]{1,0:T(8,128)(2,1)S(1)} custom-call(bf16[512,1280]{1,0:T(8,128)(2,1)S(1)} %copy-done, bf16[512,512]{1,0:T(8,128)(2,1)S(1)} %fusion.25.kv_ref, s32[512,1]{1,0:T(8,128)S(1)} %copy.8.qdoc_ref, s32[8,512]{1,0:T(8,128)S(1)} %concatenate.3.kdoc_ref), custom_call_target="tpu_custom_call" | custom-call | tf_op jit(solution)/shard_map/pallas_call | solution.py:164
  110.5 1.1 copy.12
  (7 shorter events, 0.1 us)
Async XLA Ops:
  0.0 17.3 %collective-permute-start.4 = (bf16[512,1280]{1,0:T(8,128)(2,1)}, bf16[512,1280]{1,0:T(8,128)(2,1)}, u32[]{:S(2)}, u32[]{:S(2)}) collective-permute-start(bf16[512,1280]{1,0:T(8,128)(2,1)} %param.6), channel_id=1, source_target_pairs={{0,1},{1,0},{2,3},{3,2},{4,5},{5,4},{6,7},{7,6},{8,9},{9,8},{10,11... | collective-permute-start | bytes 3932168 | tf_op jit(solution)/shard_map/ppermute | solution.py:23
  1.6 3.7 %collective-permute-start = (f32[512]{0:T(512)S(1)}, f32[512]{0:T(512)S(1)}, u32[]{:S(2)}, u32[]{:S(2)}) collective-permute-start(f32[512]{0:T(512)S(1)} %fusion), channel_id=1, source_target_pairs={{0,2},{1,3},{2,0},{3,1},{4,6},{5,7},{6,4},{7,5},{8,10},{9,11},{10,... | collective-permute-start | bytes 6152 | tf_op jit(solution)/shard_map/ppermute | solution.py:23
  5.3 30.3 %collective-permute-start.1 = (bf16[512,1280]{1,0:T(8,128)(2,1)}, bf16[512,1280]{1,0:T(8,128)(2,1)S(1)}, u32[]{:S(2)}, u32[]{:S(2)}) collective-permute-start(bf16[512,1280]{1,0:T(8,128)(2,1)} %param.6), channel_id=1, source_target_pairs={{0,2},{1,3},{2,0},{3,1},{4,6},{5,7},{6,4},{7,5},{8,10},{9,11},{10,... | collective-permute-start | bytes 3932168 | tf_op jit(solution)/shard_map/ppermute | solution.py:23
  6.2 7.6 %collective-permute-start.2 = (f32[512]{0:T(512)S(1)}, f32[512]{0:T(512)S(1)}, u32[]{:S(2)}, u32[]{:S(2)}) collective-permute-start(f32[512]{0:T(512)S(1)} %fusion), channel_id=1, source_target_pairs={{0,1},{1,0},{2,3},{3,2},{4,5},{5,4},{6,7},{7,6},{8,9},{9,8},{10,11... | collective-permute-start | bytes 6152 | tf_op jit(solution)/shard_map/ppermute | solution.py:23
  6.2 11.1 %collective-permute-start.5 = (f32[1280]{0:T(1024)}, f32[1280]{0:T(1024)S(1)}, u32[]{:S(2)}, u32[]{:S(2)}) collective-permute-start(f32[1280]{0:T(1024)} %param.9), channel_id=1, source_target_pairs={{0,1},{1,0},{2,3},{3,2},{4,5},{5,4},{6,7},{7,6},{8,9},{9,8},{10,11... | collective-permute-start | bytes 15368 | tf_op jit(solution)/shard_map/ppermute | solution.py:23
  7.9 7.1 %collective-permute-start.3 = (f32[512]{0:T(512)S(1)}, f32[512]{0:T(512)S(1)}, u32[]{:S(2)}, u32[]{:S(2)}) collective-permute-start(f32[512]{0:T(512)S(1)} %collective-permute-done), channel_id=1, source_target_pairs={{0,1},{1,0},{2,3},{3,2},{4,5},{5,4},{6,7},{7,6},{8,9},{9,8},{10,11... | collective-permute-start | bytes 6152 | tf_op jit(solution)/shard_map/ppermute | solution.py:23
  8.0 5.8 %copy-start.3 = (f32[1280]{0:T(1024)S(1)}, f32[1280]{0:T(1024)}, u32[]{:S(2)}) copy-start(f32[1280]{0:T(1024)} %param.9) | copy-start | bytes 15364
  8.0 7.0 %copy-start.1 = (bf16[512,1280]{1,0:T(8,128)(2,1)S(1)}, bf16[512,1280]{1,0:T(8,128)(2,1)}, u32[]{:S(2)}) copy-start(bf16[512,1280]{1,0:T(8,128)(2,1)} %param.6) | copy-start | bytes 3932164
  13.8 23.2 %collective-permute-start.6 = (f32[1280]{0:T(1024)S(1)}, f32[1280]{0:T(1024)S(1)}, u32[]{:S(2)}, u32[]{:S(2)}) collective-permute-start(f32[1280]{0:T(1024)S(1)} %copy-done.3), channel_id=1, source_target_pairs={{0,2},{1,3},{2,0},{3,1},{4,6},{5,7},{6,4},{7,5},{8,10},{9,11},{10,... | collective-permute-start | bytes 15368 | tf_op jit(solution)/shard_map/ppermute | solution.py:23
  17.2 19.5 %copy-start.2 = (f32[2,256]{1,0:T(2,128)S(1)}, f32[2,256]{1,0:T(2,128)}, u32[]{:S(2)}) copy-start(f32[2,256]{1,0:T(2,128)} %param.11) | copy-start | bytes 6148
  35.7 4.1 %collective-permute-start.7 = (bf16[512,1280]{1,0:T(8,128)(2,1)S(1)}, bf16[512,1280]{1,0:T(8,128)(2,1)}, u32[]{:S(2)}, u32[]{:S(2)}) collective-permute-start(bf16[512,1280]{1,0:T(8,128)(2,1)S(1)} %collective-permute-done.1), channel_id=1, source_target_pairs={{0,1},{1,0},{2,3},{3,2},{4,5},{5,4},{6,7},{7,6},{8,9},{9,8},{10,11... | collective-permute-start | bytes 3932168 | tf_op jit(solution)/shard_map/ppermute | solution.py:23
  37.0 2.9 %copy-start.4 = (f32[512,512]{1,0:T(8,128)S(1)}, f32[512,512]{1,0:T(8,128)}, u32[]{:S(2)}) copy-start(f32[512,512]{1,0:T(8,128)} %convolution_add_fusion) | copy-start | bytes 3145732
  37.0 2.8 %collective-permute-start.8 = (f32[1280]{0:T(1024)S(1)}, f32[1280]{0:T(1024)S(1)}, u32[]{:S(2)}, u32[]{:S(2)}) collective-permute-start(f32[1280]{0:T(1024)S(1)} %collective-permute-done.6), channel_id=1, source_target_pairs={{0,1},{1,0},{2,3},{3,2},{4,5},{5,4},{6,7},{7,6},{8,9},{9,8},{10,11... | collective-permute-start | bytes 15368 | tf_op jit(solution)/shard_map/ppermute | solution.py:23
  39.8 2.7 %copy-start = (bf16[512,1280]{1,0:T(8,128)(2,1)S(1)}, bf16[512,1280]{1,0:T(8,128)(2,1)}, u32[]{:S(2)}) copy-start(bf16[512,1280]{1,0:T(8,128)(2,1)} %q_ref.1) | copy-start | bytes 3932164

commit v9 on v6

--- a/solution.py
+++ b/solution.py
@@ -45,11 +45,13 @@
     peers = (c > 0).astype(jnp.int32) + (c < n - 1).astype(jnp.int32)
     pl.semaphore_wait(barrier, peers)
 
+    right = jnp.minimum(c + 1, n - 1)
+
     def copy_of(step):
         src = kv_ref if step == 0 else recv.at[step - 1]
         return pltpu.make_async_remote_copy(
             src_ref=src, dst_ref=recv.at[step], send_sem=send_sem.at[step],
-            recv_sem=recv_sem.at[step], device_id=(c + 1, t),
+            recv_sem=recv_sem.at[step], device_id=(right, t),
             device_id_type=pl.DeviceIdType.MESH)
 
     def sends_at(step):

time: 110 us -> 110 us (level)
  no operation moved by 1% of the time
where the time goes in v9:
time: 110 us
  Pallas kernels  66.3 us (60%)
  waiting for transfers between devices  17.6 us (16%)
  matrix products  10.7 us (10%)
  local copies, waits for them, and re-layouts  7.21 us (7%)
  starting transfers between devices  4.13 us (4%)
  other arithmetic  3.78 us (3%)
    pallas_call x1, Pallas kernels, ring_attention(): pl.pallas_call(functools.partial(ring_kernel, group, tok, HD ** (-0.5)),...  66.3 us
    ppermute x9, waiting for transfers between devices, flipped(): lax.ppermute(value, axis, [(source, source ^ bit) for source in range(cou...  17.6 us
    dot_general x4, matrix products, project(): return jnp.dot(normed, rows, preferred_element_type=jnp.float32)  10.7 us
    unnamed x13, local copies, waits for them, and re-layouts  6.87 us
    ppermute x9, starting transfers between devices, flipped(): lax.ppermute(value, axis, [(source, source ^ bit) for source in range(cou...  4.13 us
  transfers between devices with their start and end apart: 9, of which 2 were waited for; matrix products, arithmetic and copies ran while one was open for 16% of the time, Pallas kernels for 0%

profile of v9, /device:TPU:6, one launch (start us, length us, event | category | flops | bytes accessed | tf_op | source)
XLA Modules:
  0.0 109.9 jit_solution(11423620074681312140)
XLA Ops:
  0.0 0.0 collective-permute-start.4
  0.0 1.6 %fusion = f32[512]{0:T(512)S(1)} fusion(bf16[512,1280]{1,0:T(8,128)(2,1)} %param.6), kind=kLoop, calls=%fused_computation.2 | loop fusion | flops 1965568 | bytes 1312768 | tf_op jit(solution)/shard_map/reduce_sum | solution.py:170
  1.6 0.9 collective-permute-start
  2.6 2.8 %collective-permute-done = f32[512]{0:T(512)S(1)} collective-permute-done((f32[512]{0:T(512)S(1)}, f32[512]{0:T(512)S(1)}, u32[]{:S(2)}, u32[]{:S(2)}) %collective-permute-start) | collective-permute-done | bytes 2080 | tf_op jit(solution)/shard_map/ppermute | solution.py:23
  5.3 0.8 collective-permute-start.1
  6.2 0.0 collective-permute-start.2
  6.2 0.5 collective-permute-start.5
  6.7 1.0 reduce-window.9
  7.6 0.1 slice.10
  7.8 0.1 slice_reduce_fusion
  7.9 0.1 collective-permute-start.3
  8.0 0.0 copy-start.3
  8.0 0.0 copy-start.1
  8.0 5.8 %copy.9 = bf16[640,8,2,256]{3,1,2,0:T(8,128)(2,1)} copy(bf16[640,8,2,256]{3,2,1,0:T(2,128)(2,1)} %bitcast.9) | data formatting | bytes 10485760
  13.8 0.0 collective-permute-done.2
  13.8 0.0 copy-done.3
  13.8 1.2 %collective-permute-start.6 = (f32[1280]{0:T(1024)S(1)}, f32[1280]{0:T(1024)S(1)}, u32[]{:S(2)}, u32[]{:S(2)}) collective-permute-start(f32[1280]{0:T(1024)S(1)} %copy-done.3), channel_id=1, source_target_pairs={{0,2},{1,3},{2,0},{3,1},{4,6},{5,7},{6,4},{7,5},{8,10},{9,11},{10,... | collective-permute-start | bytes 15368 | tf_op jit(solution)/shard_map/ppermute | solution.py:23
  15.0 0.0 collective-permute-done.3
  15.0 0.0 copy-done.1
  15.0 2.2 %fusion.5 = f32[512,512]{1,0:T(8,128)S(1)} fusion(bf16[512,1280]{1,0:T(8,128)(2,1)S(1)} %copy-done.1, bf16[5120,512]{1,0:T(8,128)(2,1)} %bitcast.10, s32[]{:T(128)S(6)} %select_n.16, f32[1280]{0:T(1024)S(1)} %copy-done.3, f32[512]{0:T(512)S(1)} %add_rsqrt_fusion), kind=kOutput, calls=%fused_computation.12 | convolution fusion | flops 673710080 | bytes 3677188 | tf_op jit(solution)/shard_map/dot_general | solution.py:187
  17.2 0.0 copy-start.2
  17.2 0.0 collective-permute-done.5
  17.3 0.0 collective-permute-done.4
  17.3 3.6 %convolution_add_fusion = f32[512,512]{1,0:T(8,128)} fusion(f32[512,512]{1,0:T(8,128)S(1)} %fusion.5, bf16[512,1280]{1,0:T(8,128)(2,1)} %collective-permute-done.4, bf16[5120,512]{1,0:T(8,128)(2,1)} %bitcast.11, s32[]{:T(128)S(6)} %select_n.17, f32[1280]{0:T(1024)S(1)} %collective-permute-done.5, f32[512]{0:T(512)S(1)} %add_rsqrt_fusion), kind=kOutput, calls=%fused_computation.9 | convolution fusion | flops 673972224 | bytes 4725764 | tf_op jit(solution)/shard_map/dot_general | solution.py:187
  20.8 14.8 %collective-permute-done.1 = bf16[512,1280]{1,0:T(8,128)(2,1)S(1)} collective-permute-done((bf16[512,1280]{1,0:T(8,128)(2,1)}, bf16[512,1280]{1,0:T(8,128)(2,1)S(1)}, u32[]{:S(2)}, u32[]{:S(2)}) %collective-permute-start.1) | collective-permute-done | bytes 1310752 | tf_op jit(solution)/shard_map/ppermute | solution.py:23
  35.7 0.0 collective-permute-start.7
  35.7 0.1 add_bitcast_fusion
  35.7 0.1 iota_add_fusion
  35.8 0.9 convert_reduce_fusion
  36.7 0.1 broadcast_select_fusion
  36.8 0.0 copy-done.2
  36.8 0.1 copy.8.qdoc_ref
  37.0 0.0 copy-start.4
  37.0 0.0 collective-permute-done.6
  37.0 0.6 collective-permute-start.8
  37.6 2.2 %fusion.3 = f32[512,512]{1,0:T(8,128)S(1)} fusion(bf16[512,1280]{1,0:T(8,128)(2,1)S(1)} %collective-permute-done.1, bf16[5120,512]{1,0:T(8,128)(2,1)} %bitcast.12, s32[]{:T(128)S(6)} %select_n.18, f32[1280]{0:T(1024)S(1)} %collective-permute-done.6, f32[512]{0:T(512)S(1)} %add_rsqrt_fusion), kind=kOutput, calls=%fused_computation.10 | convolution fusion | flops 673710080 | bytes 3677188 | tf_op jit(solution)/shard_map/dot_general | solution.py:187
  39.8 0.0 collective-permute-done.8
  39.8 0.0 collective-permute-done.7
  39.8 0.0 copy-done.4
  39.8 0.0 copy-start
  39.8 2.7 %fusion.25.kv_ref = bf16[512,512]{1,0:T(8,128)(2,1)S(1)} fusion(bf16[5120,512]{1,0:T(8,128)(2,1)} %bitcast.13, s32[]{:T(128)S(6)} %select_n.19, bf16[512,1280]{1,0:T(8,128)(2,1)} %collective-permute-done.7, f32[1280]{0:T(1024)S(1)} %collective-permute-done.8, f32[512]{0:T(512)S(1)} %add_rsqrt_fusion, f32[512,512]{1,0:T(8,128)S(1)} %copy-done.4, ...), kind=kOutput, calls=%fused_computation.27 | convolution fusion | flops 674758656 | bytes 5252100 | tf_op jit(solution)/shard_map/dot_general | solution.py:187
  42.6 0.0 copy-done
  42.6 66.3 %shard_map.64 = bf16[512,1280]{1,0:T(8,128)(2,1)S(1)} custom-call(bf16[512,1280]{1,0:T(8,128)(2,1)S(1)} %copy-done, bf16[512,512]{1,0:T(8,128)(2,1)S(1)} %fusion.25.kv_ref, s32[512,1]{1,0:T(8,128)S(1)} %copy.8.qdoc_ref, s32[8,512]{1,0:T(8,128)S(1)} %concatenate.3.kdoc_ref), custom_call_target="tpu_custom_call" | custom-call | tf_op jit(solution)/shard_map/pallas_call | solution.py:148
  108.8 1.1 copy.12
  (7 shorter events, 0.1 us)
Async XLA Ops:
  0.0 17.3 %collective-permute-start.4 = (bf16[512,1280]{1,0:T(8,128)(2,1)}, bf16[512,1280]{1,0:T(8,128)(2,1)}, u32[]{:S(2)}, u32[]{:S(2)}) collective-permute-start(bf16[512,1280]{1,0:T(8,128)(2,1)} %param.6), channel_id=1, source_target_pairs={{0,1},{1,0},{2,3},{3,2},{4,5},{5,4},{6,7},{7,6},{8,9},{9,8},{10,11... | collective-permute-start | bytes 3932168 | tf_op jit(solution)/shard_map/ppermute | solution.py:23
  1.6 3.7 %collective-permute-start = (f32[512]{0:T(512)S(1)}, f32[512]{0:T(512)S(1)}, u32[]{:S(2)}, u32[]{:S(2)}) collective-permute-start(f32[512]{0:T(512)S(1)} %fusion), channel_id=1, source_target_pairs={{0,2},{1,3},{2,0},{3,1},{4,6},{5,7},{6,4},{7,5},{8,10},{9,11},{10,... | collective-permute-start | bytes 6152 | tf_op jit(solution)/shard_map/ppermute | solution.py:23
  5.3 30.3 %collective-permute-start.1 = (bf16[512,1280]{1,0:T(8,128)(2,1)}, bf16[512,1280]{1,0:T(8,128)(2,1)S(1)}, u32[]{:S(2)}, u32[]{:S(2)}) collective-permute-start(bf16[512,1280]{1,0:T(8,128)(2,1)} %param.6), channel_id=1, source_target_pairs={{0,2},{1,3},{2,0},{3,1},{4,6},{5,7},{6,4},{7,5},{8,10},{9,11},{10,... | collective-permute-start | bytes 3932168 | tf_op jit(solution)/shard_map/ppermute | solution.py:23
  6.2 7.6 %collective-permute-start.2 = (f32[512]{0:T(512)S(1)}, f32[512]{0:T(512)S(1)}, u32[]{:S(2)}, u32[]{:S(2)}) collective-permute-start(f32[512]{0:T(512)S(1)} %fusion), channel_id=1, source_target_pairs={{0,1},{1,0},{2,3},{3,2},{4,5},{5,4},{6,7},{7,6},{8,9},{9,8},{10,11... | collective-permute-start | bytes 6152 | tf_op jit(solution)/shard_map/ppermute | solution.py:23
  6.2 11.1 %collective-permute-start.5 = (f32[1280]{0:T(1024)}, f32[1280]{0:T(1024)S(1)}, u32[]{:S(2)}, u32[]{:S(2)}) collective-permute-start(f32[1280]{0:T(1024)} %param.9), channel_id=1, source_target_pairs={{0,1},{1,0},{2,3},{3,2},{4,5},{5,4},{6,7},{7,6},{8,9},{9,8},{10,11... | collective-permute-start | bytes 15368 | tf_op jit(solution)/shard_map/ppermute | solution.py:23
  7.9 7.1 %collective-permute-start.3 = (f32[512]{0:T(512)S(1)}, f32[512]{0:T(512)S(1)}, u32[]{:S(2)}, u32[]{:S(2)}) collective-permute-start(f32[512]{0:T(512)S(1)} %collective-permute-done), channel_id=1, source_target_pairs={{0,1},{1,0},{2,3},{3,2},{4,5},{5,4},{6,7},{7,6},{8,9},{9,8},{10,11... | collective-permute-start | bytes 6152 | tf_op jit(solution)/shard_map/ppermute | solution.py:23
  8.0 5.8 %copy-start.3 = (f32[1280]{0:T(1024)S(1)}, f32[1280]{0:T(1024)}, u32[]{:S(2)}) copy-start(f32[1280]{0:T(1024)} %param.9) | copy-start | bytes 15364
  8.0 7.0 %copy-start.1 = (bf16[512,1280]{1,0:T(8,128)(2,1)S(1)}, bf16[512,1280]{1,0:T(8,128)(2,1)}, u32[]{:S(2)}) copy-start(bf16[512,1280]{1,0:T(8,128)(2,1)} %param.6) | copy-start | bytes 3932164
  13.8 23.2 %collective-permute-start.6 = (f32[1280]{0:T(1024)S(1)}, f32[1280]{0:T(1024)S(1)}, u32[]{:S(2)}, u32[]{:S(2)}) collective-permute-start(f32[1280]{0:T(1024)S(1)} %copy-done.3), channel_id=1, source_target_pairs={{0,2},{1,3},{2,0},{3,1},{4,6},{5,7},{6,4},{7,5},{8,10},{9,11},{10,... | collective-permute-start | bytes 15368 | tf_op jit(solution)/shard_map/ppermute | solution.py:23
  17.2 19.5 %copy-start.2 = (f32[2,256]{1,0:T(2,128)S(1)}, f32[2,256]{1,0:T(2,128)}, u32[]{:S(2)}) copy-start(f32[2,256]{1,0:T(2,128)} %param.11) | copy-start | bytes 6148
  35.7 4.1 %collective-permute-start.7 = (bf16[512,1280]{1,0:T(8,128)(2,1)S(1)}, bf16[512,1280]{1,0:T(8,128)(2,1)}, u32[]{:S(2)}, u32[]{:S(2)}) collective-permute-start(bf16[512,1280]{1,0:T(8,128)(2,1)S(1)} %collective-permute-done.1), channel_id=1, source_target_pairs={{0,1},{1,0},{2,3},{3,2},{4,5},{5,4},{6,7},{7,6},{8,9},{9,8},{10,11... | collective-permute-start | bytes 3932168 | tf_op jit(solution)/shard_map/ppermute | solution.py:23
  37.0 2.9 %copy-start.4 = (f32[512,512]{1,0:T(8,128)S(1)}, f32[512,512]{1,0:T(8,128)}, u32[]{:S(2)}) copy-start(f32[512,512]{1,0:T(8,128)} %convolution_add_fusion) | copy-start | bytes 3145732
  37.0 2.8 %collective-permute-start.8 = (f32[1280]{0:T(1024)S(1)}, f32[1280]{0:T(1024)S(1)}, u32[]{:S(2)}, u32[]{:S(2)}) collective-permute-start(f32[1280]{0:T(1024)S(1)} %collective-permute-done.6), channel_id=1, source_target_pairs={{0,1},{1,0},{2,3},{3,2},{4,5},{5,4},{6,7},{7,6},{8,9},{9,8},{10,11... | collective-permute-start | bytes 15368 | tf_op jit(solution)/shard_map/ppermute | solution.py:23
  39.8 2.7 %copy-start = (bf16[512,1280]{1,0:T(8,128)(2,1)S(1)}, bf16[512,1280]{1,0:T(8,128)(2,1)}, u32[]{:S(2)}) copy-start(bf16[512,1280]{1,0:T(8,128)(2,1)} %q_ref.1) | copy-start | bytes 3932164

commit v10 on v9

--- a/solution.py
+++ b/solution.py
@@ -103,7 +103,8 @@
 
     full = [(0, tok, 0, tok)]
     lower = [(0, half, 0, half), (half, half, 0, tok)]
-    upper = [(0, half, 0, tok), (half, half, half, half)]
+    quarter = tok // 4
+    upper = [(i * quarter, quarter, i * quarter, tok - i * quarter) for i in range(4)]
     nback = recv.shape[0]
 
     @pl.when(c < n - 1)
@@ -186,14 +187,6 @@
         rows = lax.dynamic_slice_in_dim(flat_weight, owner * width, width, 0)
         return jnp.dot(normed, rows, preferred_element_type=jnp.float32)
 
-    summed = project(hidden, norm_gain, tpi) + project(beside, gain_beside, tpi ^ 1)
-    across, summed = lax.optimization_barrier((across, summed))
-    diagonal = flipped(across, "tp", 1)
-    summed = summed + project(across, gain_across, tpi ^ 2)
-    summed = summed + project(diagonal, gain_diagonal, tpi ^ 3)
-    kv_local = (summed + kv_bias.reshape(-1)[None, :]).astype(jnp.bfloat16)
-    kv_heads = kv_weight.shape[2] // HD
-
     device = lax.axis_index("ctx")
     ends = jnp.cumsum(lengths)
     backs = jnp.arange(CYCLE + 1, dtype=jnp.int32)
@@ -203,6 +196,15 @@
     kdoc = jnp.where((device - backs >= 0)[:, None], found, -1)
     qdoc = found[0]
     kdoc = jnp.concatenate([kdoc, jnp.full((8 - CYCLE - 1, tok), -1, jnp.int32)], axis=0)
+
+    summed = project(hidden, norm_gain, tpi) + project(beside, gain_beside, tpi ^ 1)
+    across, summed, qdoc, kdoc = lax.optimization_barrier((across, summed, qdoc, kdoc))
+    diagonal = flipped(across, "tp", 1)
+    summed = summed + project(across, gain_across, tpi ^ 2)
+    summed = summed + project(diagonal, gain_diagonal, tpi ^ 3)
+    kv_local = (summed + kv_bias.reshape(-1)[None, :]).astype(jnp.bfloat16)
+    kv_heads = kv_weight.shape[2] // HD
+
     return ring_attention(queries, kv_local, qdoc[:, None], kdoc, kv_heads)
 
 

time: 110 us -> 120 us (1.091)
  Pallas kernels: 66.3 us -> 72.3 us
  waiting for transfers between devices: 17.6 us -> 20.3 us
  matrix products: 10.7 us -> 12.3 us
    pallas_call x1, Pallas kernels: 66.3 us -> 72.3 us  [ring_attention(): pl.pallas_call(functools.partial(ring_kernel, group, tok, HD ** (-0.5)),...]
    ppermute x9, waiting for transfers between devices: 17.6 us -> 20.3 us  [flipped(): lax.ppermute(value, axis, [(source, source ^ bit) for source in range(cou...]
    dot_general x4, matrix products: 10.7 us -> 12.3 us  [project(): return jnp.dot(normed, rows, preferred_element_type=jnp.float32)]
  transfers between devices with their start and end apart: 9 -> 9, of which waited for: 2 -> 3; matrix products, arithmetic and copies ran while one was open for 16% -> 14% of each run, Pallas kernels for 0% -> 0%
where the time goes in v10:
time: 120 us
  Pallas kernels  72.3 us (60%)
  waiting for transfers between devices  20.3 us (17%)
  matrix products  12.3 us (10%)
  local copies, waits for them, and re-layouts  7.2 us (6%)
  other arithmetic  3.78 us (3%)
  starting transfers between devices  3.55 us (3%)
    pallas_call x1, Pallas kernels, ring_attention(): pl.pallas_call(functools.partial(ring_kernel, group, tok, HD ** (-0.5)),...  72.3 us
    ppermute x9, waiting for transfers between devices, flipped(): lax.ppermute(value, axis, [(source, source ^ bit) for source in range(cou...  20.3 us
    dot_general x4, matrix products, project(): return jnp.dot(normed, rows, preferred_element_type=jnp.float32)  12.3 us
    unnamed x13, local copies, waits for them, and re-layouts  6.85 us
    ppermute x9, starting transfers between devices, flipped(): lax.ppermute(value, axis, [(source, source ^ bit) for source in range(cou...  3.55 us
  transfers between devices with their start and end apart: 9, of which 3 were waited for; matrix products, arithmetic and copies ran while one was open for 14% of the time, Pallas kernels for 0%

profile of v10, /device:TPU:6, one launch (start us, length us, event | category | flops | bytes accessed | tf_op | source)
XLA Modules:
  0.0 119.6 jit_solution(2997109351754015497)
XLA Ops:
  0.0 1.6 %fusion = f32[512]{0:T(512)S(1)} fusion(bf16[512,1280]{1,0:T(8,128)(2,1)} %param.6), kind=kLoop, calls=%fused_computation.2 | loop fusion | flops 1965568 | bytes 1312768 | tf_op jit(solution)/shard_map/reduce_sum | solution.py:171
  1.6 0.9 collective-permute-start
  2.6 0.0 collective-permute-start.2
  2.6 0.5 collective-permute-start.4
  3.1 0.0 collective-permute-start.5
  3.1 0.1 iota_add_fusion
  3.2 1.0 reduce-window.9
  4.1 0.1 slice.10
  4.2 0.1 slice_reduce_fusion
  4.4 1.0 collective-permute-done
  5.3 0.8 collective-permute-start.1
  6.1 0.1 add_bitcast_fusion
  6.2 0.9 convert_reduce_fusion
  7.1 0.0 copy-start.2
  7.1 0.1 collective-permute-start.3
  7.2 0.1 broadcast_select_fusion
  7.3 0.0 copy-start.1
  7.3 0.0 copy-start.4
  7.3 5.8 %copy.9 = bf16[640,8,2,256]{3,1,2,0:T(8,128)(2,1)} copy(bf16[640,8,2,256]{3,2,1,0:T(2,128)(2,1)} %bitcast.9) | data formatting | bytes 10485760
  13.1 0.0 copy-done.2
  13.1 0.0 collective-permute-done.2
  13.1 0.0 collective-permute-done.3
  13.1 0.0 copy-done.1
  13.1 0.0 copy-done.4
  13.1 2.2 %fusion.5 = f32[512,512]{1,0:T(8,128)S(1)} fusion(bf16[512,1280]{1,0:T(8,128)(2,1)S(1)} %copy-done.1, bf16[5120,512]{1,0:T(8,128)(2,1)} %bitcast.10, s32[]{:T(128)S(6)} %select_n.16, f32[1280]{0:T(1024)S(1)} %copy-done.4, f32[512]{0:T(512)S(1)} %add_rsqrt_fusion), kind=kOutput, calls=%fused_computation.12 | convolution fusion | flops 673710080 | bytes 3677188 | tf_op jit(solution)/shard_map/dot_general | solution.py:188
  15.4 0.0 copy-start.3
  15.4 0.0 collective-permute-done.5
  15.4 0.0 collective-permute-done.4
  15.4 3.6 %convolution_add_fusion = f32[512,512]{1,0:T(8,128)} fusion(f32[512,512]{1,0:T(8,128)S(1)} %fusion.5, bf16[512,1280]{1,0:T(8,128)(2,1)} %collective-permute-done.4, bf16[5120,512]{1,0:T(8,128)(2,1)} %bitcast.11, s32[]{:T(128)S(6)} %select_n.17, f32[1280]{0:T(1024)S(1)} %collective-permute-done.5, f32[512]{0:T(512)S(1)} %add_rsqrt_fusion), kind=kOutput, calls=%fused_computation.9 | convolution fusion | flops 673972224 | bytes 4725764 | tf_op jit(solution)/shard_map/dot_general | solution.py:188
  19.0 16.9 %collective-permute-done.1 = bf16[512,1280]{1,0:T(8,128)(2,1)S(1)} collective-permute-done((bf16[512,1280]{1,0:T(8,128)(2,1)}, bf16[512,1280]{1,0:T(8,128)(2,1)S(1)}, u32[]{:S(2)}, u32[]{:S(2)}) %collective-permute-start.1) | collective-permute-done | bytes 1310752 | tf_op jit(solution)/shard_map/ppermute | solution.py:23
  35.9 0.0 collective-permute-start.7
  35.9 1.2 %collective-permute-start.6 = (f32[1280]{0:T(1024)S(1)}, f32[1280]{0:T(1024)S(1)}, u32[]{:S(2)}, u32[]{:S(2)}) collective-permute-start(f32[1280]{0:T(1024)S(1)} %copy-done.4), channel_id=1, source_target_pairs={{0,2},{1,3},{2,0},{3,1},{4,6},{5,7},{6,4},{7,5},{8,10},{9,11},{10,... | collective-permute-start | bytes 15368 | tf_op jit(solution)/shard_map/ppermute | solution.py:23
  37.1 0.0 copy-done.3
  37.1 0.0 slice-start
  37.1 2.4 %collective-permute-done.6 = f32[1280]{0:T(1024)S(1)} collective-permute-done((f32[1280]{0:T(1024)S(1)}, f32[1280]{0:T(1024)S(1)}, u32[]{:S(2)}, u32[]{:S(2)}) %collective-permute-start.6) | collective-permute-done | bytes 5152 | tf_op jit(solution)/shard_map/ppermute | solution.py:23
  39.5 0.0 collective-permute-start.8
  39.5 3.2 %fusion.3 = f32[512,512]{1,0:T(8,128)} fusion(bf16[512,1280]{1,0:T(8,128)(2,1)S(1)} %collective-permute-done.1, bf16[5120,512]{1,0:T(8,128)(2,1)} %bitcast.12, s32[]{:T(128)S(6)} %select_n.19, f32[1280]{0:T(1024)S(1)} %collective-permute-done.6, f32[512]{0:T(512)S(1)} %add_rsqrt_fusion), kind=kOutput, calls=%fused_computation.10 | convolution fusion | flops 673710080 | bytes 3677188 | tf_op jit(solution)/shard_map/dot_general | solution.py:188
  42.7 0.0 slice-done
  42.7 0.1 copy.8.qdoc_ref
  42.9 0.0 collective-permute-done.8
  42.9 0.0 collective-permute-done.7
  42.9 0.0 copy-start
  42.9 3.3 %fusion.25.kv_ref = bf16[512,512]{1,0:T(8,128)(2,1)S(1)} fusion(bf16[5120,512]{1,0:T(8,128)(2,1)} %bitcast.13, s32[]{:T(128)S(6)} %select_n.20, bf16[512,1280]{1,0:T(8,128)(2,1)} %collective-permute-done.7, f32[1280]{0:T(1024)S(1)} %collective-permute-done.8, f32[512]{0:T(512)S(1)} %add_rsqrt_fusion, f32[512,512]{1,0:T(8,128)} %convolution_add_fusion, ...), kind=kOutput, calls=%fused_computation.27 | convolution fusion | flops 674758656 | bytes 5252100 | tf_op jit(solution)/shard_map/dot_general | solution.py:188
  46.3 0.0 copy-done
  46.3 72.3 %shard_map.64 = bf16[512,1280]{1,0:T(8,128)(2,1)S(1)} custom-call(bf16[512,1280]{1,0:T(8,128)(2,1)S(1)} %copy-done, bf16[512,512]{1,0:T(8,128)(2,1)S(1)} %fusion.25.kv_ref, s32[512,1]{1,0:T(8,128)S(1)} %copy.8.qdoc_ref, s32[8,512]{1,0:T(8,128)S(1)} %concatenate.3.kdoc_ref), custom_call_target="tpu_custom_call" | custom-call | tf_op jit(solution)/shard_map/pallas_call | solution.py:149
  118.6 1.1 copy.12
  (6 shorter events, 0.1 us)
Async XLA Ops:
  1.6 3.7 %collective-permute-start = (f32[512]{0:T(512)S(1)}, f32[512]{0:T(512)S(1)}, u32[]{:S(2)}, u32[]{:S(2)}) collective-permute-start(f32[512]{0:T(512)S(1)} %fusion), channel_id=1, source_target_pairs={{0,2},{1,3},{2,0},{3,1},{4,6},{5,7},{6,4},{7,5},{8,10},{9,11},{10,... | collective-permute-start | bytes 6152 | tf_op jit(solution)/shard_map/ppermute | solution.py:23
  2.6 10.5 %collective-permute-start.2 = (f32[512]{0:T(512)S(1)}, f32[512]{0:T(512)S(1)}, u32[]{:S(2)}, u32[]{:S(2)}) collective-permute-start(f32[512]{0:T(512)S(1)} %fusion), channel_id=1, source_target_pairs={{0,1},{1,0},{2,3},{3,2},{4,5},{5,4},{6,7},{7,6},{8,9},{9,8},{10,11... | collective-permute-start | bytes 6152 | tf_op jit(solution)/shard_map/ppermute | solution.py:23
  2.6 12.8 %collective-permute-start.4 = (bf16[512,1280]{1,0:T(8,128)(2,1)}, bf16[512,1280]{1,0:T(8,128)(2,1)}, u32[]{:S(2)}, u32[]{:S(2)}) collective-permute-start(bf16[512,1280]{1,0:T(8,128)(2,1)} %param.6), channel_id=1, source_target_pairs={{0,1},{1,0},{2,3},{3,2},{4,5},{5,4},{6,7},{7,6},{8,9},{9,8},{10,11... | collective-permute-start | bytes 3932168 | tf_op jit(solution)/shard_map/ppermute | solution.py:23
  3.1 12.3 %collective-permute-start.5 = (f32[1280]{0:T(1024)}, f32[1280]{0:T(1024)S(1)}, u32[]{:S(2)}, u32[]{:S(2)}) collective-permute-start(f32[1280]{0:T(1024)} %param.9), channel_id=1, source_target_pairs={{0,1},{1,0},{2,3},{3,2},{4,5},{5,4},{6,7},{7,6},{8,9},{9,8},{10,11... | collective-permute-start | bytes 15368 | tf_op jit(solution)/shard_map/ppermute | solution.py:23
  5.3 30.5 %collective-permute-start.1 = (bf16[512,1280]{1,0:T(8,128)(2,1)}, bf16[512,1280]{1,0:T(8,128)(2,1)S(1)}, u32[]{:S(2)}, u32[]{:S(2)}) collective-permute-start(bf16[512,1280]{1,0:T(8,128)(2,1)} %param.6), channel_id=1, source_target_pairs={{0,2},{1,3},{2,0},{3,1},{4,6},{5,7},{6,4},{7,5},{8,10},{9,11},{10,... | collective-permute-start | bytes 3932168 | tf_op jit(solution)/shard_map/ppermute | solution.py:23
  7.1 6.0 %copy-start.2 = (s32[5,512]{1,0:T(8,128)}, s32[5,512]{1,0:T(8,128)S(1)}, u32[]{:S(2)}) copy-start(s32[5,512]{1,0:T(8,128)S(1)} %convert_reduce_fusion) | copy-start | bytes 30724
  7.1 6.0 %collective-permute-start.3 = (f32[512]{0:T(512)S(1)}, f32[512]{0:T(512)S(1)}, u32[]{:S(2)}, u32[]{:S(2)}) collective-permute-start(f32[512]{0:T(512)S(1)} %collective-permute-done), channel_id=1, source_target_pairs={{0,1},{1,0},{2,3},{3,2},{4,5},{5,4},{6,7},{7,6},{8,9},{9,8},{10,11... | collective-permute-start | bytes 6152 | tf_op jit(solution)/shard_map/ppermute | solution.py:23
  7.3 5.8 %copy-start.1 = (bf16[512,1280]{1,0:T(8,128)(2,1)S(1)}, bf16[512,1280]{1,0:T(8,128)(2,1)}, u32[]{:S(2)}) copy-start(bf16[512,1280]{1,0:T(8,128)(2,1)} %param.6) | copy-start | bytes 3932164
  7.3 5.8 %copy-start.4 = (f32[1280]{0:T(1024)S(1)}, f32[1280]{0:T(1024)}, u32[]{:S(2)}) copy-start(f32[1280]{0:T(1024)} %param.9) | copy-start | bytes 15364
  15.4 21.7 %copy-start.3 = (f32[2,256]{1,0:T(2,128)S(1)}, f32[2,256]{1,0:T(2,128)}, u32[]{:S(2)}) copy-start(f32[2,256]{1,0:T(2,128)} %param.11) | copy-start | bytes 6148
  35.9 7.0 %collective-permute-start.7 = (bf16[512,1280]{1,0:T(8,128)(2,1)S(1)}, bf16[512,1280]{1,0:T(8,128)(2,1)}, u32[]{:S(2)}, u32[]{:S(2)}) collective-permute-start(bf16[512,1280]{1,0:T(8,128)(2,1)S(1)} %collective-permute-done.1), channel_id=1, source_target_pairs={{0,1},{1,0},{2,3},{3,2},{4,5},{5,4},{6,7},{7,6},{8,9},{9,8},{10,11... | collective-permute-start | bytes 3932168 | tf_op jit(solution)/shard_map/ppermute | solution.py:23
  35.9 3.7 %collective-permute-start.6 = (f32[1280]{0:T(1024)S(1)}, f32[1280]{0:T(1024)S(1)}, u32[]{:S(2)}, u32[]{:S(2)}) collective-permute-start(f32[1280]{0:T(1024)S(1)} %copy-done.4), channel_id=1, source_target_pairs={{0,2},{1,3},{2,0},{3,1},{4,6},{5,7},{6,4},{7,5},{8,10},{9,11},{10,... | collective-permute-start | bytes 15368 | tf_op jit(solution)/shard_map/ppermute | solution.py:23
  37.1 5.7 %slice-start = ((s32[5,512]{1,0:T(8,128)}), s32[1,512]{1,0:T(1,128)S(1)}, s32[]{:S(2)}) async-start(s32[5,512]{1,0:T(8,128)} %copy-done.2), calls=%async_computation | async-start | bytes 4096 | tf_op jit(solution)/shard_map/slice | solution.py:197
  39.5 3.4 %collective-permute-start.8 = (f32[1280]{0:T(1024)S(1)}, f32[1280]{0:T(1024)S(1)}, u32[]{:S(2)}, u32[]{:S(2)}) collective-permute-start(f32[1280]{0:T(1024)S(1)} %collective-permute-done.6), channel_id=1, source_target_pairs={{0,1},{1,0},{2,3},{3,2},{4,5},{5,4},{6,7},{7,6},{8,9},{9,8},{10,11... | collective-permute-start | bytes 15368 | tf_op jit(solution)/shard_map/ppermute | solution.py:23
  42.9 3.4 %copy-start = (bf16[512,1280]{1,0:T(8,128)(2,1)S(1)}, bf16[512,1280]{1,0:T(8,128)(2,1)}, u32[]{:S(2)}) copy-start(bf16[512,1280]{1,0:T(8,128)(2,1)} %q_ref.1) | copy-start | bytes 3932164

commit v11 on v10

--- a/solution.py
+++ b/solution.py
@@ -103,8 +103,7 @@
 
     full = [(0, tok, 0, tok)]
     lower = [(0, half, 0, half), (half, half, 0, tok)]
-    quarter = tok // 4
-    upper = [(i * quarter, quarter, i * quarter, tok - i * quarter) for i in range(4)]
+    upper = [(0, half, 0, tok), (half, half, half, half)]
     nback = recv.shape[0]
 
     @pl.when(c < n - 1)
@@ -197,8 +196,9 @@
     qdoc = found[0]
     kdoc = jnp.concatenate([kdoc, jnp.full((8 - CYCLE - 1, tok), -1, jnp.int32)], axis=0)
 
+    beside, qdoc, kdoc = lax.optimization_barrier((beside, qdoc, kdoc))
     summed = project(hidden, norm_gain, tpi) + project(beside, gain_beside, tpi ^ 1)
-    across, summed, qdoc, kdoc = lax.optimization_barrier((across, summed, qdoc, kdoc))
+    across, summed = lax.optimization_barrier((across, summed))
     diagonal = flipped(across, "tp", 1)
     summed = summed + project(across, gain_across, tpi ^ 2)
     summed = summed + project(diagonal, gain_diagonal, tpi ^ 3)

time: 120 us -> 114 us (0.950)
  Pallas kernels: 72.3 us -> 67.8 us
  matrix products: 12.3 us -> 10.8 us
    pallas_call x1, Pallas kernels: 72.3 us -> 67.8 us  [ring_attention(): pl.pallas_call(functools.partial(ring_kernel, group, tok, HD ** (-0.5)),...]
    dot_general x4, matrix products: 12.3 us -> 10.8 us  [project(): return jnp.dot(normed, rows, preferred_element_type=jnp.float32)]
    unnamed x13 -> x15, local copies, waits for them, and re-layouts: 6.85 us -> 6.86 us
where the time goes in v11:
time: 114 us
  Pallas kernels  67.8 us (59%)
  waiting for transfers between devices  20.3 us (18%)
  matrix products  10.8 us (9%)
  local copies, waits for them, and re-layouts  7.2 us (6%)
  other arithmetic  3.78 us (3%)
  starting transfers between devices  3.55 us (3%)
    pallas_call x1, Pallas kernels, ring_attention(): pl.pallas_call(functools.partial(ring_kernel, group, tok, HD ** (-0.5)),...  67.8 us
    ppermute x9, waiting for transfers between devices, flipped(): lax.ppermute(value, axis, [(source, source ^ bit) for source in range(cou...  20.3 us
    dot_general x4, matrix products, project(): return jnp.dot(normed, rows, preferred_element_type=jnp.float32)  10.8 us
    unnamed x15, local copies, waits for them, and re-layouts  6.86 us
    ppermute x9, starting transfers between devices, flipped(): lax.ppermute(value, axis, [(source, source ^ bit) for source in range(cou...  3.55 us
  transfers between devices with their start and end apart: 9, of which 3 were waited for; matrix products, arithmetic and copies ran while one was open for 14% of the time, Pallas kernels for 0%

profile of v11, /device:TPU:6, one launch (start us, length us, event | category | flops | bytes accessed | tf_op | source)
XLA Modules:
  0.0 113.7 jit_solution(4929533045403314012)
XLA Ops:
  0.0 1.6 %fusion = f32[512]{0:T(512)S(1)} fusion(bf16[512,1280]{1,0:T(8,128)(2,1)} %param.6), kind=kLoop, calls=%fused_computation.2 | loop fusion | flops 1965568 | bytes 1312768 | tf_op jit(solution)/shard_map/reduce_sum | solution.py:170
  1.6 0.9 collective-permute-start
  2.6 0.0 collective-permute-start.2
  2.6 0.5 collective-permute-start.4
  3.1 0.0 collective-permute-start.5
  3.1 0.1 iota_add_fusion
  3.2 1.0 reduce-window.9
  4.1 0.1 slice.10
  4.2 0.1 slice_reduce_fusion
  4.4 1.0 collective-permute-done
  5.3 0.8 collective-permute-start.1
  6.1 0.1 add_bitcast_fusion
  6.2 0.9 convert_reduce_fusion
  7.1 0.0 copy-start.2
  7.1 0.1 collective-permute-start.3
  7.2 0.1 broadcast_select_fusion
  7.3 0.0 copy-start.1
  7.3 0.0 copy-start.4
  7.3 5.8 %copy.9 = bf16[640,8,2,256]{3,1,2,0:T(8,128)(2,1)} copy(bf16[640,8,2,256]{3,2,1,0:T(2,128)(2,1)} %bitcast.9) | data formatting | bytes 10485760
  13.1 0.0 copy-done.2
  13.1 0.0 collective-permute-done.2
  13.1 0.0 collective-permute-done.3
  13.1 0.0 copy-done.1
  13.1 0.0 copy-done.4
  13.1 2.2 %fusion.5 = f32[512,512]{1,0:T(8,128)S(1)} fusion(bf16[512,1280]{1,0:T(8,128)(2,1)S(1)} %copy-done.1, bf16[5120,512]{1,0:T(8,128)(2,1)} %bitcast.10, s32[]{:T(128)S(6)} %select_n.16, f32[1280]{0:T(1024)S(1)} %copy-done.4, f32[512]{0:T(512)S(1)} %add_rsqrt_fusion), kind=kOutput, calls=%fused_computation.12 | convolution fusion | flops 673710080 | bytes 3677188 | tf_op jit(solution)/shard_map/dot_general | solution.py:187
  15.3 0.0 collective-permute-done.4
  15.3 0.0 copy-start.3
  15.4 0.0 slice-start
  15.4 0.0 collective-permute-done.5
  15.4 3.6 %convolution_add_fusion = f32[512,512]{1,0:T(8,128)} fusion(f32[512,512]{1,0:T(8,128)S(1)} %fusion.5, bf16[512,1280]{1,0:T(8,128)(2,1)} %collective-permute-done.4, bf16[5120,512]{1,0:T(8,128)(2,1)} %bitcast.11, s32[]{:T(128)S(6)} %select_n.18, f32[1280]{0:T(1024)S(1)} %collective-permute-done.5, f32[512]{0:T(512)S(1)} %add_rsqrt_fusion), kind=kOutput, calls=%fused_computation.9 | convolution fusion | flops 673972224 | bytes 4725764 | tf_op jit(solution)/shard_map/dot_general | solution.py:187
  19.0 16.9 %collective-permute-done.1 = bf16[512,1280]{1,0:T(8,128)(2,1)S(1)} collective-permute-done((bf16[512,1280]{1,0:T(8,128)(2,1)}, bf16[512,1280]{1,0:T(8,128)(2,1)S(1)}, u32[]{:S(2)}, u32[]{:S(2)}) %collective-permute-start.1) | collective-permute-done | bytes 1310752 | tf_op jit(solution)/shard_map/ppermute | solution.py:23
  35.9 0.0 collective-permute-start.7
  35.9 1.2 %collective-permute-start.6 = (f32[1280]{0:T(1024)S(1)}, f32[1280]{0:T(1024)S(1)}, u32[]{:S(2)}, u32[]{:S(2)}) collective-permute-start(f32[1280]{0:T(1024)S(1)} %copy-done.4), channel_id=1, source_target_pairs={{0,2},{1,3},{2,0},{3,1},{4,6},{5,7},{6,4},{7,5},{8,10},{9,11},{10,... | collective-permute-start | bytes 15368 | tf_op jit(solution)/shard_map/ppermute | solution.py:23
  37.1 0.0 copy-done.3
  37.1 2.4 %collective-permute-done.6 = f32[1280]{0:T(1024)S(1)} collective-permute-done((f32[1280]{0:T(1024)S(1)}, f32[1280]{0:T(1024)S(1)}, u32[]{:S(2)}, u32[]{:S(2)}) %collective-permute-start.6) | collective-permute-done | bytes 5152 | tf_op jit(solution)/shard_map/ppermute | solution.py:23
  39.5 0.0 collective-permute-start.8
  39.5 0.0 slice-done
  39.5 0.1 copy.8.qdoc_ref
  39.7 0.0 copy-start.5
  39.7 2.3 %fusion.3 = f32[512,512]{1,0:T(8,128)S(1)} fusion(bf16[512,1280]{1,0:T(8,128)(2,1)S(1)} %collective-permute-done.1, bf16[5120,512]{1,0:T(8,128)(2,1)} %bitcast.12, s32[]{:T(128)S(6)} %select_n.19, f32[1280]{0:T(1024)S(1)} %collective-permute-done.6, f32[512]{0:T(512)S(1)} %add_rsqrt_fusion), kind=kOutput, calls=%fused_computation.10 | convolution fusion | flops 673710080 | bytes 3677188 | tf_op jit(solution)/shard_map/dot_general | solution.py:187
  42.0 0.0 collective-permute-done.8
  42.0 0.0 collective-permute-done.7
  42.0 0.0 copy-done.5
  42.0 0.0 copy-start
  42.0 2.7 %fusion.25.kv_ref = bf16[512,512]{1,0:T(8,128)(2,1)S(1)} fusion(bf16[5120,512]{1,0:T(8,128)(2,1)} %bitcast.13, s32[]{:T(128)S(6)} %select_n.20, bf16[512,1280]{1,0:T(8,128)(2,1)} %collective-permute-done.7, f32[1280]{0:T(1024)S(1)} %collective-permute-done.8, f32[512]{0:T(512)S(1)} %add_rsqrt_fusion, f32[512,512]{1,0:T(8,128)S(1)} %copy-done.5, ...), kind=kOutput, calls=%fused_computation.27 | convolution fusion | flops 674758656 | bytes 5252100 | tf_op jit(solution)/shard_map/dot_general | solution.py:187
  44.8 0.0 copy-done
  44.8 67.8 %shard_map.64 = bf16[512,1280]{1,0:T(8,128)(2,1)S(1)} custom-call(bf16[512,1280]{1,0:T(8,128)(2,1)S(1)} %copy-done, bf16[512,512]{1,0:T(8,128)(2,1)S(1)} %fusion.25.kv_ref, s32[512,1]{1,0:T(8,128)S(1)} %copy.8.qdoc_ref, s32[8,512]{1,0:T(8,128)S(1)} %concatenate.3.kdoc_ref), custom_call_target="tpu_custom_call" | custom-call | tf_op jit(solution)/shard_map/pallas_call | solution.py:148
  112.6 1.1 copy.12
  (6 shorter events, 0.1 us)
Async XLA Ops:
  1.6 3.7 %collective-permute-start = (f32[512]{0:T(512)S(1)}, f32[512]{0:T(512)S(1)}, u32[]{:S(2)}, u32[]{:S(2)}) collective-permute-start(f32[512]{0:T(512)S(1)} %fusion), channel_id=1, source_target_pairs={{0,2},{1,3},{2,0},{3,1},{4,6},{5,7},{6,4},{7,5},{8,10},{9,11},{10,... | collective-permute-start | bytes 6152 | tf_op jit(solution)/shard_map/ppermute | solution.py:23
  2.6 10.5 %collective-permute-start.2 = (f32[512]{0:T(512)S(1)}, f32[512]{0:T(512)S(1)}, u32[]{:S(2)}, u32[]{:S(2)}) collective-permute-start(f32[512]{0:T(512)S(1)} %fusion), channel_id=1, source_target_pairs={{0,1},{1,0},{2,3},{3,2},{4,5},{5,4},{6,7},{7,6},{8,9},{9,8},{10,11... | collective-permute-start | bytes 6152 | tf_op jit(solution)/shard_map/ppermute | solution.py:23
  2.6 12.8 %collective-permute-start.4 = (bf16[512,1280]{1,0:T(8,128)(2,1)}, bf16[512,1280]{1,0:T(8,128)(2,1)}, u32[]{:S(2)}, u32[]{:S(2)}) collective-permute-start(bf16[512,1280]{1,0:T(8,128)(2,1)} %param.6), channel_id=1, source_target_pairs={{0,1},{1,0},{2,3},{3,2},{4,5},{5,4},{6,7},{7,6},{8,9},{9,8},{10,11... | collective-permute-start | bytes 3932168 | tf_op jit(solution)/shard_map/ppermute | solution.py:23
  3.1 12.3 %collective-permute-start.5 = (f32[1280]{0:T(1024)}, f32[1280]{0:T(1024)S(1)}, u32[]{:S(2)}, u32[]{:S(2)}) collective-permute-start(f32[1280]{0:T(1024)} %param.9), channel_id=1, source_target_pairs={{0,1},{1,0},{2,3},{3,2},{4,5},{5,4},{6,7},{7,6},{8,9},{9,8},{10,11... | collective-permute-start | bytes 15368 | tf_op jit(solution)/shard_map/ppermute | solution.py:23
  5.3 30.5 %collective-permute-start.1 = (bf16[512,1280]{1,0:T(8,128)(2,1)}, bf16[512,1280]{1,0:T(8,128)(2,1)S(1)}, u32[]{:S(2)}, u32[]{:S(2)}) collective-permute-start(bf16[512,1280]{1,0:T(8,128)(2,1)} %param.6), channel_id=1, source_target_pairs={{0,2},{1,3},{2,0},{3,1},{4,6},{5,7},{6,4},{7,5},{8,10},{9,11},{10,... | collective-permute-start | bytes 3932168 | tf_op jit(solution)/shard_map/ppermute | solution.py:23
  7.1 6.0 %copy-start.2 = (s32[5,512]{1,0:T(8,128)}, s32[5,512]{1,0:T(8,128)S(1)}, u32[]{:S(2)}) copy-start(s32[5,512]{1,0:T(8,128)S(1)} %convert_reduce_fusion) | copy-start | bytes 30724
  7.1 6.0 %collective-permute-start.3 = (f32[512]{0:T(512)S(1)}, f32[512]{0:T(512)S(1)}, u32[]{:S(2)}, u32[]{:S(2)}) collective-permute-start(f32[512]{0:T(512)S(1)} %collective-permute-done), channel_id=1, source_target_pairs={{0,1},{1,0},{2,3},{3,2},{4,5},{5,4},{6,7},{7,6},{8,9},{9,8},{10,11... | collective-permute-start | bytes 6152 | tf_op jit(solution)/shard_map/ppermute | solution.py:23
  7.3 5.8 %copy-start.1 = (bf16[512,1280]{1,0:T(8,128)(2,1)S(1)}, bf16[512,1280]{1,0:T(8,128)(2,1)}, u32[]{:S(2)}) copy-start(bf16[512,1280]{1,0:T(8,128)(2,1)} %param.6) | copy-start | bytes 3932164
  7.3 5.8 %copy-start.4 = (f32[1280]{0:T(1024)S(1)}, f32[1280]{0:T(1024)}, u32[]{:S(2)}) copy-start(f32[1280]{0:T(1024)} %param.9) | copy-start | bytes 15364
  15.3 21.7 %copy-start.3 = (f32[2,256]{1,0:T(2,128)S(1)}, f32[2,256]{1,0:T(2,128)}, u32[]{:S(2)}) copy-start(f32[2,256]{1,0:T(2,128)} %param.11) | copy-start | bytes 6148
  15.4 24.2 %slice-start = ((s32[5,512]{1,0:T(8,128)}), s32[1,512]{1,0:T(1,128)S(1)}, s32[]{:S(2)}) async-start(s32[5,512]{1,0:T(8,128)} %copy-done.2), calls=%async_computation | async-start | bytes 4096 | tf_op jit(solution)/shard_map/slice | solution.py:196
  35.9 6.1 %collective-permute-start.7 = (bf16[512,1280]{1,0:T(8,128)(2,1)S(1)}, bf16[512,1280]{1,0:T(8,128)(2,1)}, u32[]{:S(2)}, u32[]{:S(2)}) collective-permute-start(bf16[512,1280]{1,0:T(8,128)(2,1)S(1)} %collective-permute-done.1), channel_id=1, source_target_pairs={{0,1},{1,0},{2,3},{3,2},{4,5},{5,4},{6,7},{7,6},{8,9},{9,8},{10,11... | collective-permute-start | bytes 3932168 | tf_op jit(solution)/shard_map/ppermute | solution.py:23
  35.9 3.7 %collective-permute-start.6 = (f32[1280]{0:T(1024)S(1)}, f32[1280]{0:T(1024)S(1)}, u32[]{:S(2)}, u32[]{:S(2)}) collective-permute-start(f32[1280]{0:T(1024)S(1)} %copy-done.4), channel_id=1, source_target_pairs={{0,2},{1,3},{2,0},{3,1},{4,6},{5,7},{6,4},{7,5},{8,10},{9,11},{10,... | collective-permute-start | bytes 15368 | tf_op jit(solution)/shard_map/ppermute | solution.py:23
  39.5 2.5 %collective-permute-start.8 = (f32[1280]{0:T(1024)S(1)}, f32[1280]{0:T(1024)S(1)}, u32[]{:S(2)}, u32[]{:S(2)}) collective-permute-start(f32[1280]{0:T(1024)S(1)} %collective-permute-done.6), channel_id=1, source_target_pairs={{0,1},{1,0},{2,3},{3,2},{4,5},{5,4},{6,7},{7,6},{8,9},{9,8},{10,11... | collective-permute-start | bytes 15368 | tf_op jit(solution)/shard_map/ppermute | solution.py:23
  39.7 2.3 %copy-start.5 = (f32[512,512]{1,0:T(8,128)S(1)}, f32[512,512]{1,0:T(8,128)}, u32[]{:S(2)}) copy-start(f32[512,512]{1,0:T(8,128)} %convolution_add_fusion) | copy-start | bytes 3145732
  42.0 2.7 %copy-start = (bf16[512,1280]{1,0:T(8,128)(2,1)S(1)}, bf16[512,1280]{1,0:T(8,128)(2,1)}, u32[]{:S(2)}) copy-start(bf16[512,1280]{1,0:T(8,128)(2,1)} %q_ref.1) | copy-start | bytes 3932164

commit v12 on v5

--- a/solution.py
+++ b/solution.py
@@ -166,9 +166,9 @@
     squares = own_squares + squares_beside + squares_across + squares_diagonal
     scale_rows = lax.rsqrt(squares / D + 1e-06)
     beside = flipped(hidden, "tp", 1)
-    gain_across = flipped(norm_gain, "tp", 2)
+    gain_diagonal = flipped(norm_gain, "tp", 3)
     gain_beside = flipped(norm_gain, "tp", 1)
-    gain_diagonal = flipped(gain_across, "tp", 1)
+    gain_across = flipped(gain_diagonal, "tp", 1)
     flat_weight = kv_weight.reshape(kv_weight.shape[0], -1)
 
     def project(part, gain, owner):

time: 114 us -> 111 us (0.974)
  Pallas kernels: 68.7 us -> 66.6 us
  matrix products: 12.3 us -> 10.8 us
    pallas_call x1, Pallas kernels: 68.7 us -> 66.6 us  [ring_attention(): pl.pallas_call(functools.partial(ring_kernel, group, tok, HD ** (-0.5)),...]
    dot_general x4, matrix products: 12.3 us -> 10.8 us  [project(): return jnp.dot(normed, rows, preferred_element_type=jnp.float32)]
    unnamed x13 -> x15, local copies, waits for them, and re-layouts: 6.85 us -> 6.86 us
where the time goes in v12:
time: 111 us
  Pallas kernels  66.6 us (60%)
  waiting for transfers between devices  17.3 us (16%)
  matrix products  10.8 us (10%)
  local copies, waits for them, and re-layouts  7.2 us (6%)
  starting transfers between devices  4.65 us (4%)
  other arithmetic  3.79 us (3%)
    pallas_call x1, Pallas kernels, ring_attention(): pl.pallas_call(functools.partial(ring_kernel, group, tok, HD ** (-0.5)),...  66.6 us
    ppermute x9, waiting for transfers between devices, flipped(): lax.ppermute(value, axis, [(source, source ^ bit) for source in range(cou...  17.3 us
    dot_general x4, matrix products, project(): return jnp.dot(normed, rows, preferred_element_type=jnp.float32)  10.8 us
    unnamed x15, local copies, waits for them, and re-layouts  6.86 us
    ppermute x9, starting transfers between devices, flipped(): lax.ppermute(value, axis, [(source, source ^ bit) for source in range(cou...  4.65 us
  transfers between devices with their start and end apart: 9, of which 2 were waited for; matrix products, arithmetic and copies ran while one was open for 15% of the time, Pallas kernels for 0%

profile of v12, /device:TPU:6, one launch (start us, length us, event | category | flops | bytes accessed | tf_op | source)
XLA Modules:
  0.0 110.5 jit_solution(13121081669646803867)
XLA Ops:
  0.0 1.6 %fusion = f32[512]{0:T(512)S(1)} fusion(bf16[512,1280]{1,0:T(8,128)(2,1)} %param.6), kind=kLoop, calls=%fused_computation.2 | loop fusion | flops 1965568 | bytes 1312768 | tf_op jit(solution)/shard_map/reduce_sum | solution.py:162
  1.6 0.4 collective-permute-start.2
  2.0 0.7 collective-permute-start.1
  2.7 0.0 collective-permute-start.4
  2.7 1.2 %collective-permute-start = (bf16[512,1280]{1,0:T(8,128)(2,1)}, bf16[512,1280]{1,0:T(8,128)(2,1)S(1)}, u32[]{:S(2)}, u32[]{:S(2)}) collective-permute-start(bf16[512,1280]{1,0:T(8,128)(2,1)} %param.6), channel_id=1, source_target_pairs={{0,2},{1,3},{2,0},{3,1},{4,6},{5,7},{6,4},{7,5},{8,10},{9,11},{10,... | collective-permute-start | bytes 3932168 | tf_op jit(solution)/shard_map/ppermute | solution.py:23
  3.9 0.2 collective-permute-start.5
  4.1 0.1 iota_add_fusion
  4.2 1.0 reduce-window.9
  5.2 0.1 slice.10
  5.3 0.1 slice_reduce_fusion
  5.4 0.1 add_bitcast_fusion
  5.5 0.9 convert_reduce_fusion
  6.4 0.0 copy-start.2
  6.4 0.0 collective-permute-done.2
  6.4 0.4 collective-permute-start.3
  6.8 0.1 broadcast_select_fusion
  6.8 0.0 copy-start.1
  6.8 0.0 copy-start.4
  6.8 5.8 %copy.9 = bf16[640,8,2,256]{3,1,2,0:T(8,128)(2,1)} copy(bf16[640,8,2,256]{3,2,1,0:T(2,128)(2,1)} %bitcast.9) | data formatting | bytes 10485760
  12.6 0.0 copy-done.2
  12.6 0.0 collective-permute-done.1
  12.6 0.0 collective-permute-done.3
  12.6 0.0 copy-done.1
  12.7 0.0 copy-done.4
  12.7 2.2 %fusion.5 = f32[512,512]{1,0:T(8,128)S(1)} fusion(bf16[512,1280]{1,0:T(8,128)(2,1)S(1)} %copy-done.1, bf16[5120,512]{1,0:T(8,128)(2,1)} %bitcast.10, s32[]{:T(128)S(6)} %select_n.16, f32[1280]{0:T(1024)S(1)} %copy-done.4, f32[512]{0:T(512)S(1)} %add_rsqrt_fusion), kind=kOutput, calls=%fused_computation.13 | convolution fusion | flops 673710080 | bytes 3677188 | tf_op jit(solution)/shard_map/dot_general | solution.py:177
  14.9 0.0 copy-start.3
  14.9 0.0 slice-start
  14.9 0.0 collective-permute-done.5
  14.9 0.0 collective-permute-done.4
  14.9 3.6 %convolution_add_fusion.1 = f32[512,512]{1,0:T(8,128)} fusion(f32[512,512]{1,0:T(8,128)S(1)} %fusion.5, bf16[512,1280]{1,0:T(8,128)(2,1)} %collective-permute-done.4, bf16[5120,512]{1,0:T(8,128)(2,1)} %bitcast.11, s32[]{:T(128)S(6)} %select_n.17, f32[1280]{0:T(1024)S(1)} %collective-permute-done.5, f32[512]{0:T(512)S(1)} %add_rsqrt_fusion), kind=kOutput, calls=%fused_computation.11 | convolution fusion | flops 673972224 | bytes 4725764 | tf_op jit(solution)/shard_map/dot_general | solution.py:177
  18.5 15.6 %collective-permute-done = bf16[512,1280]{1,0:T(8,128)(2,1)S(1)} collective-permute-done((bf16[512,1280]{1,0:T(8,128)(2,1)}, bf16[512,1280]{1,0:T(8,128)(2,1)S(1)}, u32[]{:S(2)}, u32[]{:S(2)}) %collective-permute-start) | collective-permute-done | bytes 1310752 | tf_op jit(solution)/shard_map/ppermute | solution.py:23
  34.1 0.0 collective-permute-start.8
  34.1 1.3 %collective-permute-start.6 = (f32[1280]{0:T(1024)S(1)}, f32[1280]{0:T(1024)S(1)}, u32[]{:S(2)}, u32[]{:S(2)}) collective-permute-start(f32[1280]{0:T(1024)S(1)} %copy-done.4), channel_id=1, source_target_pairs={{0,3},{1,2},{2,1},{3,0},{4,7},{5,6},{6,5},{7,4},{8,11},{9,10},{10,... | collective-permute-start | bytes 15368 | tf_op jit(solution)/shard_map/ppermute | solution.py:23
  35.4 0.0 copy-done.3
  35.4 1.8 %collective-permute-done.6 = f32[1280]{0:T(1024)S(1)} collective-permute-done((f32[1280]{0:T(1024)S(1)}, f32[1280]{0:T(1024)S(1)}, u32[]{:S(2)}, u32[]{:S(2)}) %collective-permute-start.6) | collective-permute-done | bytes 5152 | tf_op jit(solution)/shard_map/ppermute | solution.py:23
  37.2 0.5 collective-permute-start.7
  37.7 0.0 slice-done
  37.7 0.1 copy.8.qdoc_ref
  37.8 0.0 copy-start.5
  37.8 0.0 collective-permute-done.8
  37.8 2.7 %fusion.4 = f32[512,512]{1,0:T(8,128)S(1)} fusion(bf16[512,1280]{1,0:T(8,128)(2,1)} %collective-permute-done.8, bf16[5120,512]{1,0:T(8,128)(2,1)} %bitcast.12, s32[]{:T(128)S(6)} %select_n.20, f32[1280]{0:T(1024)S(1)} %collective-permute-done.6, f32[512]{0:T(512)S(1)} %add_rsqrt_fusion), kind=kOutput, calls=%fused_computation.12 | convolution fusion | flops 673710080 | bytes 3677188 | tf_op jit(solution)/shard_map/dot_general | solution.py:177
  40.5 0.0 collective-permute-done.7
  40.6 0.0 copy-done.5
  40.6 0.0 copy-start
  40.6 2.3 %fusion.22.kv_ref = bf16[512,512]{1,0:T(8,128)(2,1)S(1)} fusion(f32[512,512]{1,0:T(8,128)S(1)} %fusion.4, f32[512,512]{1,0:T(8,128)S(1)} %copy-done.5, bf16[5120,512]{1,0:T(8,128)(2,1)} %bitcast.13, s32[]{:T(128)S(6)} %select_n.19, bf16[512,1280]{1,0:T(8,128)(2,1)S(1)} %collective-permute-done, f32[1280]{0:T(1024)S(1)} %collective-permute-done.7, ...), kind=kOutput, calls=%fused_computation.27 | convolution fusion | flops 674758656 | bytes 5252100 | tf_op jit(solution)/shard_map/dot_general | solution.py:177
  42.9 0.0 copy-done
  42.9 66.6 %shard_map.64 = bf16[512,1280]{1,0:T(8,128)(2,1)S(1)} custom-call(bf16[512,1280]{1,0:T(8,128)(2,1)S(1)} %copy-done, bf16[512,512]{1,0:T(8,128)(2,1)S(1)} %fusion.22.kv_ref, s32[512,1]{1,0:T(8,128)S(1)} %copy.8.qdoc_ref, s32[8,512]{1,0:T(8,128)S(1)} %concatenate.3.kdoc_ref), custom_call_target="tpu_custom_call" | custom-call | tf_op jit(solution)/shard_map/pallas_call | solution.py:139
  109.5 1.1 copy.12
  (6 shorter events, 0.1 us)
Async XLA Ops:
  1.6 4.7 %collective-permute-start.2 = (f32[512]{0:T(512)S(1)}, f32[512]{0:T(512)S(1)}, u32[]{:S(2)}, u32[]{:S(2)}) collective-permute-start(f32[512]{0:T(512)S(1)} %fusion), channel_id=1, source_target_pairs={{0,3},{1,2},{2,1},{3,0},{4,7},{5,6},{6,5},{7,4},{8,11},{9,10},{10,... | collective-permute-start | bytes 6152 | tf_op jit(solution)/shard_map/ppermute | solution.py:23
  2.0 10.6 %collective-permute-start.1 = (f32[512]{0:T(512)S(1)}, f32[512]{0:T(512)S(1)}, u32[]{:S(2)}, u32[]{:S(2)}) collective-permute-start(f32[512]{0:T(512)S(1)} %fusion), channel_id=1, source_target_pairs={{0,1},{1,0},{2,3},{3,2},{4,5},{5,4},{6,7},{7,6},{8,9},{9,8},{10,11... | collective-permute-start | bytes 6152 | tf_op jit(solution)/shard_map/ppermute | solution.py:23
  2.7 12.2 %collective-permute-start.4 = (bf16[512,1280]{1,0:T(8,128)(2,1)}, bf16[512,1280]{1,0:T(8,128)(2,1)}, u32[]{:S(2)}, u32[]{:S(2)}) collective-permute-start(bf16[512,1280]{1,0:T(8,128)(2,1)} %param.6), channel_id=1, source_target_pairs={{0,1},{1,0},{2,3},{3,2},{4,5},{5,4},{6,7},{7,6},{8,9},{9,8},{10,11... | collective-permute-start | bytes 3932168 | tf_op jit(solution)/shard_map/ppermute | solution.py:23
  2.7 31.4 %collective-permute-start = (bf16[512,1280]{1,0:T(8,128)(2,1)}, bf16[512,1280]{1,0:T(8,128)(2,1)S(1)}, u32[]{:S(2)}, u32[]{:S(2)}) collective-permute-start(bf16[512,1280]{1,0:T(8,128)(2,1)} %param.6), channel_id=1, source_target_pairs={{0,2},{1,3},{2,0},{3,1},{4,6},{5,7},{6,4},{7,5},{8,10},{9,11},{10,... | collective-permute-start | bytes 3932168 | tf_op jit(solution)/shard_map/ppermute | solution.py:23
  3.9 11.0 %collective-permute-start.5 = (f32[1280]{0:T(1024)}, f32[1280]{0:T(1024)S(1)}, u32[]{:S(2)}, u32[]{:S(2)}) collective-permute-start(f32[1280]{0:T(1024)} %param.9), channel_id=1, source_target_pairs={{0,1},{1,0},{2,3},{3,2},{4,5},{5,4},{6,7},{7,6},{8,9},{9,8},{10,11... | collective-permute-start | bytes 15368 | tf_op jit(solution)/shard_map/ppermute | solution.py:23
  6.4 6.2 %copy-start.2 = (s32[5,512]{1,0:T(8,128)}, s32[5,512]{1,0:T(8,128)S(1)}, u32[]{:S(2)}) copy-start(s32[5,512]{1,0:T(8,128)S(1)} %convert_reduce_fusion) | copy-start | bytes 30724
  6.4 6.2 %collective-permute-start.3 = (f32[512]{0:T(512)S(1)}, f32[512]{0:T(512)S(1)}, u32[]{:S(2)}, u32[]{:S(2)}) collective-permute-start(f32[512]{0:T(512)S(1)} %collective-permute-done.2), channel_id=1, source_target_pairs={{0,1},{1,0},{2,3},{3,2},{4,5},{5,4},{6,7},{7,6},{8,9},{9,8},{10,11... | collective-permute-start | bytes 6152 | tf_op jit(solution)/shard_map/ppermute | solution.py:23
  6.8 5.8 %copy-start.1 = (bf16[512,1280]{1,0:T(8,128)(2,1)S(1)}, bf16[512,1280]{1,0:T(8,128)(2,1)}, u32[]{:S(2)}) copy-start(bf16[512,1280]{1,0:T(8,128)(2,1)} %param.6) | copy-start | bytes 3932164
  6.8 5.8 %copy-start.4 = (f32[1280]{0:T(1024)S(1)}, f32[1280]{0:T(1024)}, u32[]{:S(2)}) copy-start(f32[1280]{0:T(1024)} %param.9) | copy-start | bytes 15364
  14.9 20.5 %copy-start.3 = (f32[2,256]{1,0:T(2,128)S(1)}, f32[2,256]{1,0:T(2,128)}, u32[]{:S(2)}) copy-start(f32[2,256]{1,0:T(2,128)} %param.11) | copy-start | bytes 6148
  14.9 22.8 %slice-start = ((s32[5,512]{1,0:T(8,128)}), s32[1,512]{1,0:T(1,128)S(1)}, s32[]{:S(2)}) async-start(s32[5,512]{1,0:T(8,128)} %copy-done.2), calls=%async_computation | async-start | bytes 4096 | tf_op jit(solution)/shard_map/slice | solution.py:186
  34.1 3.8 %collective-permute-start.8 = (bf16[512,1280]{1,0:T(8,128)(2,1)S(1)}, bf16[512,1280]{1,0:T(8,128)(2,1)}, u32[]{:S(2)}, u32[]{:S(2)}) collective-permute-start(bf16[512,1280]{1,0:T(8,128)(2,1)S(1)} %collective-permute-done), channel_id=1, source_target_pairs={{0,1},{1,0},{2,3},{3,2},{4,5},{5,4},{6,7},{7,6},{8,9},{9,8},{10,11... | collective-permute-start | bytes 3932168 | tf_op jit(solution)/shard_map/ppermute | solution.py:23
  34.1 3.1 %collective-permute-start.6 = (f32[1280]{0:T(1024)S(1)}, f32[1280]{0:T(1024)S(1)}, u32[]{:S(2)}, u32[]{:S(2)}) collective-permute-start(f32[1280]{0:T(1024)S(1)} %copy-done.4), channel_id=1, source_target_pairs={{0,3},{1,2},{2,1},{3,0},{4,7},{5,6},{6,5},{7,4},{8,11},{9,10},{10,... | collective-permute-start | bytes 15368 | tf_op jit(solution)/shard_map/ppermute | solution.py:23
  37.2 3.4 %collective-permute-start.7 = (f32[1280]{0:T(1024)S(1)}, f32[1280]{0:T(1024)S(1)}, u32[]{:S(2)}, u32[]{:S(2)}) collective-permute-start(f32[1280]{0:T(1024)S(1)} %collective-permute-done.6), channel_id=1, source_target_pairs={{0,1},{1,0},{2,3},{3,2},{4,5},{5,4},{6,7},{7,6},{8,9},{9,8},{10,11... | collective-permute-start | bytes 15368 | tf_op jit(solution)/shard_map/ppermute | solution.py:23
  37.8 2.7 %copy-start.5 = (f32[512,512]{1,0:T(8,128)S(1)}, f32[512,512]{1,0:T(8,128)}, u32[]{:S(2)}) copy-start(f32[512,512]{1,0:T(8,128)} %convolution_add_fusion.1) | copy-start | bytes 3145732
  40.6 2.3 %copy-start = (bf16[512,1280]{1,0:T(8,128)(2,1)S(1)}, bf16[512,1280]{1,0:T(8,128)(2,1)}, u32[]{:S(2)}) copy-start(bf16[512,1280]{1,0:T(8,128)(2,1)} %q_ref.1) | copy-start | bytes 3932164
